TPU v7x, 32 devices: a whole 2x2x4 slice. The times are simulated.
32 devices in a mesh: seq: 4 (over y, core), dp: 8 (over z, x).
Axes of the slice: x: 2, y: 2, z: 4, core: 2. Of those that a mesh axis runs over, the one named last changes fastest.
Arguments:
- mlp_hidden: bfloat16 [8, 256, 8192], P('dp', None, 'seq'), may hold values from -6 to 6
- encoder_stream: bfloat16 [8, 256, 4096], P('dp', 'seq'), may hold values from -18 to 18
- down_proj: bfloat16 [8192, 4096], P('seq', 'dp'), may hold values from -0.0625 to 0.0625
- final_gain: bfloat16 [4096], replicated, may hold values from 0.25 to 1.75
- kv_proj: bfloat16 [4096, 2, 2048], P('dp', None, 'seq'), may hold values from -0.09375 to 0.09375
- queries: bfloat16 [8, 128, 2048], P('dp', None, 'seq'), may hold values from -640 to 640
- out_proj: bfloat16 [2048, 4096], P('seq'), may hold values from -0.39648438 to 0.39648438
- enc_len: int32 [8], P('dp'), may hold values from 128 to 256, as said below
- dec_pad: int32 [8], P('dp'), may hold values from 0 to 64, as said below
Outputs:
- cross_out: bfloat16 [8, 128, 4096], P('dp', 'seq')
Inputs may be any that keep to these rules, and one draw needn't show every extreme that they name: `enc_len`: at least one filing uses all 256 positions and one uses 256 // 2. `dec_pad`: some filing has no padding and some has 64 padded rows.
All inputs are finite; a program needn't handle non-finite values.
Results may differ from a plain program's by a relative error of at most 0.015.
The roundings to bfloat16 on the way count: a program that leaves them out, or rounds other values in their place, can miss the bound.
Values may be sent and summed in bfloat16 or wider, within the bound.
No kernel may reach another device: no remote copies, remote signals or barrier semaphores. Data moves between devices by JAX's collectives and lax.ppermute only.
A program may use at most 128 MiB of HBM per device.

v0:
```python
import math

import jax
import jax.numpy as jnp
from jax import lax
from jax.sharding import PartitionSpec as P

HD = 256


def normalize(resid, gain_row):
    spread = jnp.mean(resid * resid, axis=-1, keepdims=True)
    return (resid * lax.rsqrt(spread + 1e-06) * gain_row).astype(jnp.bfloat16)


def on_device(
    mlp_hidden, encoder_stream, down_proj, final_gain, kv_proj, queries, out_proj, enc_len, dec_pad
):
    hidden = mlp_hidden[0]
    enc_total = hidden.shape[0]
    gain_row = final_gain.astype(jnp.float32)
    full_down = lax.all_gather(down_proj, "dp", axis=1, tiled=True)
    row_block = hidden
    mlp_out = lax.psum_scatter(
        jnp.dot(row_block, full_down, preferred_element_type=jnp.float32),
        "seq",
        scatter_dimension=0,
        tiled=True,
    )
    normed = normalize(encoder_stream[0].astype(jnp.float32) + mlp_out, gain_row)
    encoded = lax.all_gather(normed, "seq", axis=0, tiled=True)
    heads_here = queries.shape[2] // HD
    kv_width = 2 * heads_here * HD
    weight_piece = lax.all_gather(kv_proj, "dp", axis=0, tiled=True)
    key_value = jnp.dot(
        encoded,
        weight_piece.reshape(weight_piece.shape[0], kv_width),
        preferred_element_type=jnp.float32,
    ).astype(jnp.bfloat16)
    key_value = key_value.reshape(enc_total, 2, heads_here, HD)
    key_rows = key_value[:, 0]
    value_rows = key_value[:, 1]
    dec_rows = queries.shape[1]
    query_rows = queries[0].reshape(dec_rows, heads_here, HD)
    scores = jnp.einsum(
        "qhd,khd->hqk", query_rows, key_rows, preferred_element_type=jnp.float32
    ) / math.sqrt(HD)
    visible = jnp.arange(enc_total, dtype=jnp.int32) < enc_len[0]
    scores = jnp.where(visible[None, None, :], scores, -jnp.inf)
    highest = jnp.max(scores, axis=-1, keepdims=True)
    expo = jnp.exp(scores - highest)
    attention = (expo / jnp.sum(expo, axis=-1, keepdims=True)).astype(jnp.bfloat16)
    attended = jnp.einsum(
        "hqk,khd->qhd", attention, value_rows, preferred_element_type=jnp.float32
    ).astype(jnp.bfloat16)
    row_live = jnp.arange(dec_rows, dtype=jnp.int32) < dec_rows - dec_pad[0]
    attended = jnp.where(row_live[:, None, None], attended, jnp.zeros_like(attended)).reshape(
        dec_rows, heads_here * HD
    )
    row_block = attended
    result = lax.psum_scatter(
        jnp.dot(row_block, out_proj, preferred_element_type=jnp.float32),
        "seq",
        scatter_dimension=0,
        tiled=True,
    )
    return result.astype(jnp.bfloat16)[None]


def solution(mesh):
    placed = (
        P("dp", None, "seq"),
        P("dp", "seq", None),
        P("seq", "dp"),
        P(),
        P("dp", None, "seq"),
        P("dp", None, "seq"),
        P("seq", None),
        P("dp"),
        P("dp"),
    )
    return jax.shard_map(
        on_device, mesh=mesh, in_specs=placed, out_specs=P("dp", "seq", None), check_vma=False
    )
```

profile of v0, /device:TPU:0, one launch (start us, length us, event | category | flops | bytes accessed | tf_op | source)
XLA Modules:
  0.0 494.5 jit_solution(16718448679306863005)
XLA Ops:
  6.5 0.0 copy-start
  6.5 0.0 all-gather.4.cloned.1.call-start
  6.5 0.7 all-gather.4.cloned.1.call-update
  7.3 0.0 reduce-scatter.3.cloned.1.call-start
  7.3 232.6 %all-gather.4.cloned.1.call-done = bf16[2048,4096]{1,0:T(8,128)(2,1)} async-done(((bf16[2048,512]{1,0:T(8,128)(2,1)}), bf16[2048,4096]{1,0:T(8,128)(2,1)}) %all-gather.4.cloned.1.call-update) | async-done | bytes 16777232 | tf_op jit(solution)/shard_map/all_gather | solution.py:22
  239.9 0.0 copy-done
  239.9 10.1 %fusion.6 = f32[256,4096]{1,0:T(8,128)} fusion(bf16[2048,4096]{1,0:T(8,128)(2,1)} %all-gather.4.cloned.1.call-done, bf16[1,256,2048]{2,1,0:T(8,128)(2,1)S(1)} %copy-done), kind=kOutput, calls=%fused_computation.10 | convolution fusion | flops 4294967296 | bytes 22020096 | tf_op jit(solution)/shard_map/dot_general | solution.py:25
  250.0 0.0 copy-start.3
  250.0 0.0 copy-start.1
  250.0 0.0 copy-start.2
  250.0 0.0 reduce-scatter.3.cloned.1.call-update
  250.0 0.0 all-gather.8.cloned.1.call-start
  250.0 0.7 all-gather.8.cloned.1.call-update
  250.7 0.0 all-gather.6.cloned.1.call-start
  250.8 0.0 copy-done.3
  250.8 42.0 %reduce-scatter.3.cloned.1.call-done = f32[64,4096]{1,0:T(8,128)} async-done(((f32[256,4096]{1,0:T(8,128)}), f32[64,4096]{1,0:T(8,128)}) %reduce-scatter.3.cloned.1.call-update) | async-done | bytes 1048592 | tf_op jit(solution)/shard_map/reduce_scatter | solution.py:24
  292.8 0.0 copy-done.1
  292.8 1.5 multiply_reduce_fusion
  294.3 2.2 multiply_convert_fusion
  296.5 0.0 all-gather.6.cloned.1.call-update
  296.5 0.0 reduce-scatter.5.cloned.1.call-start
  296.6 0.0 copy-done.2
  297.9 122.2 %all-gather.8.cloned.1.call-done = bf16[4096,2,512]{2,1,0:T(2,128)(2,1)} async-done(((bf16[512,2,512]{2,1,0:T(2,128)(2,1)}), bf16[4096,2,512]{2,1,0:T(2,128)(2,1)}) %all-gather.8.cloned.1.call-update) | async-done | bytes 8388624 | tf_op jit(solution)/shard_map/all_gather | solution.py:34
  420.1 9.3 %copy.21 = bf16[512,8,2,512]{3,1,2,0:T(8,128)(2,1)} copy(bf16[512,8,2,512]{3,2,1,0:T(2,128)(2,1)} %bitcast.32) | data formatting | bytes 16777216
  429.4 13.0 %all-gather.6.cloned.1.call-done = bf16[256,4096]{1,0:T(8,128)(2,1)} async-done(((bf16[64,4096]{1,0:T(8,128)(2,1)}), bf16[256,4096]{1,0:T(8,128)(2,1)}) %all-gather.6.cloned.1.call-update) | async-done | bytes 2097168 | tf_op jit(solution)/shard_map/all_gather | solution.py:31
  442.4 6.3 %convolution_convert_fusion = bf16[256,1024]{1,0:T(8,128)(2,1)S(1)} fusion(bf16[256,4096]{1,0:T(8,128)(2,1)} %all-gather.6.cloned.1.call-done, bf16[4096,1024]{1,0:T(8,128)(2,1)} %bitcast.33), kind=kOutput, calls=%fused_computation.1 | convolution fusion | flops 2147745792 | bytes 11010048 | tf_op jit(solution)/shard_map/dot_general | solution.py:35
  448.8 0.4 reshape.33
  449.2 0.4 fusion.12
  449.5 0.2 fusion.3
  449.8 0.1 fusion.13
  449.9 0.2 copy.19
  450.1 0.3 fusion.5
  450.3 4.3 fusion.14
  454.6 0.0 reduce-scatter.5.cloned.1.call-update
  454.6 31.6 %reduce-scatter.5.cloned.1.call-done = f32[32,4096]{1,0:T(8,128)} async-done(((f32[128,4096]{1,0:T(8,128)}), f32[32,4096]{1,0:T(8,128)}) %reduce-scatter.5.cloned.1.call-update) | async-done | bytes 524304 | tf_op jit(solution)/shard_map/reduce_scatter | solution.py:61
  486.2 1.8 convert_bitcast_fusion
  (5 shorter events, 0.1 us)
Async XLA Ops:
  6.5 233.4 %copy-start = (bf16[1,256,2048]{2,1,0:T(8,128)(2,1)S(1)}, bf16[1,256,2048]{2,1,0:T(8,128)(2,1)}, u32[]{:S(2)}) copy-start(bf16[1,256,2048]{2,1,0:T(8,128)(2,1)} %param.9) | copy-start | bytes 3145732
  6.5 233.3 %all-gather.4.cloned.1.call-start = ((), (), s32[]{:S(2)}) async-start(), calls=%async_computation.2 | async-start | bytes 18874368 | tf_op jit(solution)/shard_map/all_gather | solution.py:22
  7.3 285.6 %reduce-scatter.3.cloned.1.call-start = ((), (), s32[]{:S(2)}) async-start(), calls=%async_computation.3 | async-start | bytes 5242880 | tf_op jit(solution)/shard_map/reduce_scatter | solution.py:24
  250.0 0.8 copy-start.3
  250.0 42.9 %copy-start.1 = (bf16[1,64,4096]{2,1,0:T(8,128)(2,1)S(1)}, bf16[1,64,4096]{2,1,0:T(8,128)(2,1)}, u32[]{:S(2)}) copy-start(bf16[1,64,4096]{2,1,0:T(8,128)(2,1)} %param.10) | copy-start | bytes 1572868
  250.0 46.6 %copy-start.2 = (bf16[1,128,512]{2,1,0:T(8,128)(2,1)S(1)}, bf16[1,128,512]{2,1,0:T(8,128)(2,1)}, u32[]{:S(2)}) copy-start(bf16[1,128,512]{2,1,0:T(8,128)(2,1)} %param.14) | copy-start | bytes 393220
  250.0 170.1 %all-gather.8.cloned.1.call-start = ((), (), s32[]{:S(2)}) async-start(), calls=%async_computation.5 | async-start | bytes 9437184 | tf_op jit(solution)/shard_map/all_gather | solution.py:34
  250.7 191.7 %all-gather.6.cloned.1.call-start = ((), (), s32[]{:S(2)}) async-start(), calls=%async_computation.4 | async-start | bytes 2621440 | tf_op jit(solution)/shard_map/all_gather | solution.py:31
  296.5 189.7 %reduce-scatter.5.cloned.1.call-start = ((), (), s32[]{:S(2)}) async-start(), calls=%async_computation.6 | async-start | bytes 2621440 | tf_op jit(solution)/shard_map/reduce_scatter | solution.py:61
Sparse Core Ops, SparseCore 0:
  9.4 230.4 all-gather.3
  250.1 42.6 reduce-scatter.2
  295.2 124.9 all-gather.7
  421.6 20.7 all-gather.5
  454.8 31.3 reduce-scatter.4
where the time goes:
time: 495 us
  waiting for transfers between devices  443 us (89%)
  matrix products  21.2 us (4%)
  between operations  14.5 us (3%)
  local copies, waits for them, and re-layouts  10.3 us (2%)
  other arithmetic  5.56 us (1%)
    all_gather x1, waiting for transfers between devices, on_device(): full_down = lax.all_gather(down_proj, 'dp', axis=1, tiled=True)  233 us
    all_gather x1, waiting for transfers between devices, on_device(): weight_piece = lax.all_gather(kv_proj, 'dp', axis=0, tiled=True)  122 us
    reduce_scatter x1, waiting for transfers between devices, on_device(): lax.psum_scatter(jnp.dot(row_block, full_down, preferred_element_type=jnp...  42 us
    reduce_scatter x1, waiting for transfers between devices, on_device(): lax.psum_scatter(jnp.dot(row_block, out_proj, preferred_element_type=jnp....  31.6 us
    all_gather x1, waiting for transfers between devices, on_device(): encoded = lax.all_gather(normed, 'seq', axis=0, tiled=True)  13 us
    dot_general x1, matrix products, on_device(): jnp.dot(row_block, full_down, preferred_element_type=jnp.float32)  10.1 us
  transfers between devices with their start and end apart: 5, of which 5 were waited for; matrix products, arithmetic and copies ran while one was open for 3% of the time, Pallas kernels for 0%

commit v1 on v0

v1 whole, which is shorter than its diff:
```python
import math

import jax
import jax.numpy as jnp
from jax import lax
from jax.sharding import PartitionSpec as P

HD = 256


class Line:
    def __init__(self, name, total, size, stride):
        self.name, self.total, self.size, self.stride = name, total, size, stride
        self.at = (lax.axis_index(name) // stride) % size

    def place(self, index):
        return (index // self.stride) % self.size

    def shift(self, value, step):
        pairs = [
            (i, i + step * self.stride)
            for i in range(self.total)
            if 0 <= self.place(i) + step < self.size
        ]
        return lax.ppermute(value, self.name, pairs)

    def swap(self, value, mask):
        pairs = [
            (i, i + ((self.place(i) ^ mask) - self.place(i)) * self.stride)
            for i in range(self.total)
        ]
        return lax.ppermute(value, self.name, pairs)

    def gather(self, pieces):
        n = self.size
        if n == 1:
            return [pieces]
        if n == 2:
            return [pieces, [self.swap(p, 1) for p in pieces]]
        hops = {}
        up = down = pieces
        for step in range(1, n):
            up = [self.shift(p, 1) for p in up]
            down = [self.shift(p, -1) for p in down]
            hops[step], hops[-step] = up, down
        slots = [pieces]
        for m in range(1, n):
            moves = sorted({i - (i ^ m) for i in range(n)})
            slot = []
            for p in range(len(pieces)):
                value = hops[moves[0]][p]
                for move in moves[1:]:
                    value = jnp.where(self.at - (self.at ^ m) == move, hops[move][p], value)
                slot.append(value)
            slots.append(slot)
        return slots


def after(values, earlier):
    out = lax.optimization_barrier((tuple(values), tuple(earlier)))
    return list(out[0])


def on_device(
    mlp_hidden, encoder_stream, down_proj, final_gain, kv_proj, queries, out_proj, enc_len, dec_pad
):
    seq, dp = lax.axis_size("seq"), lax.axis_size("dp")
    nx = 1 << ((dp.bit_length() - 1) // 2)
    nz = dp // nx
    nc = 2
    ny = seq // nc
    z = Line("dp", dp, nz, nx)
    x = Line("dp", dp, nx, 1)
    y = Line("seq", seq, ny, nc)
    c = Line("seq", seq, nc, 1)

    hidden = mlp_hidden[0]
    enc_total, depth = hidden.shape
    rows = enc_total // seq
    block = down_proj.shape[1]
    width = block * dp
    dot = lambda a, b: jnp.dot(a, b, preferred_element_type=jnp.float32)

    halves = [hidden[: enc_total // 2], hidden[enc_total // 2 :]]
    hidden_slots = z.gather(halves)
    down_slots = [s[0] for s in x.gather([down_proj])]

    keys_local, values_local = kv_proj[:, 0], kv_proj[:, 1]
    kv_own = after([keys_local, values_local], hidden_slots[-1])
    kv_z = z.gather(kv_own)
    kv_slots = [x.gather(slot) for slot in kv_z]

    summed = []
    for m in range(nz):
        a = jnp.concatenate(hidden_slots[m], axis=0).reshape(ny, nc, rows, depth)
        pick = lambda i: lax.dynamic_index_in_dim(a, i, 1, keepdims=False).reshape(ny * rows, depth)
        product = lambda i: jnp.concatenate([dot(pick(i), w) for w in down_slots], axis=1)
        part = product(c.at) + c.swap(product(1 - c.at), 1)
        part = part.reshape(ny, rows, nx * block)
        total = lax.dynamic_index_in_dim(part, y.at, 0, keepdims=False)
        for k in range(1, ny):
            other = lax.dynamic_index_in_dim(part, y.at ^ k, 0, keepdims=False)
            total = total + y.swap(other, k)
        summed.append(total if m == 0 else z.swap(total, m))

    stream = encoder_stream[0]
    gain = final_gain.astype(jnp.float32)
    resid, gains = [], []
    for m in range(nz):
        for k in range(nx):
            start = ((z.at ^ m) * nx + (x.at ^ k)) * block
            piece = lax.dynamic_slice_in_dim(stream, start, block, 1).astype(jnp.float32)
            resid.append(piece + summed[m][:, k * block : (k + 1) * block])
            gains.append(lax.dynamic_slice_in_dim(gain, start, block, 0))
    resid = jnp.concatenate(resid, axis=1)
    gains = jnp.concatenate(gains, axis=0)
    spread = jnp.sum(resid * resid, axis=-1, keepdims=True) / width
    normed = (resid * lax.rsqrt(spread + 1e-06) * gains).astype(jnp.bfloat16)
    encoded, places = [], []
    for k, (far,) in enumerate(y.gather([normed])):
        encoded += [far, c.swap(far, 1)]
        for j in range(nc):
            start = ((y.at ^ k) * nc + (c.at ^ j)) * rows
            places.append(start + jnp.arange(rows, dtype=jnp.int32))
    encoded = jnp.concatenate(encoded, axis=0)
    visible = jnp.concatenate(places) < enc_len[0]

    keys = values = None
    for m in range(nz):
        for k in range(nx):
            at = (m * nx + k) * block
            piece = encoded[:, at : at + block]
            wk, wv = kv_slots[m][k]
            dk, dv = dot(piece, wk), dot(piece, wv)
            keys = dk if keys is None else keys + dk
            values = dv if values is None else values + dv
    keys = keys.astype(jnp.bfloat16)
    values = values.astype(jnp.bfloat16)

    heads_here = queries.shape[2] // HD
    dec_rows = queries.shape[1]
    attended = []
    for h in range(heads_here):
        cols = slice(h * HD, (h + 1) * HD)
        scores = lax.dot_general(
            queries[0][:, cols], keys[:, cols], (((1,), (1,)), ((), ())),
            preferred_element_type=jnp.float32,
        ) / math.sqrt(HD)
        scores = jnp.where(visible[None, :], scores, -jnp.inf)
        expo = jnp.exp(scores - jnp.max(scores, axis=-1, keepdims=True))
        attention = (expo / jnp.sum(expo, axis=-1, keepdims=True)).astype(jnp.bfloat16)
        attended.append(dot(attention, values[:, cols]).astype(jnp.bfloat16))
    attended = jnp.concatenate(attended, axis=1)
    row_live = jnp.arange(dec_rows, dtype=jnp.int32) < dec_rows - dec_pad[0]
    attended = jnp.where(row_live[:, None], attended, jnp.zeros_like(attended))

    out_rows = dec_rows // seq
    att = attended.reshape(ny, nc, out_rows, heads_here * HD)
    pick = lambda i: lax.dynamic_index_in_dim(att, i, 1, keepdims=False).reshape(
        ny * out_rows, heads_here * HD
    )
    part = dot(pick(c.at), out_proj) + c.swap(dot(pick(1 - c.at), out_proj), 1)
    part = part.reshape(ny, out_rows, width)
    total = lax.dynamic_index_in_dim(part, y.at, 0, keepdims=False)
    for k in range(1, ny):
        total = total + y.swap(lax.dynamic_index_in_dim(part, y.at ^ k, 0, keepdims=False), k)
    return total.astype(jnp.bfloat16)[None]


def solution(mesh):
    placed = (
        P("dp", None, "seq"),
        P("dp", "seq", None),
        P("seq", "dp"),
        P(),
        P("dp", None, "seq"),
        P("dp", None, "seq"),
        P("seq", None),
        P("dp"),
        P("dp"),
    )
    return jax.shard_map(
        on_device, mesh=mesh, in_specs=placed, out_specs=P("dp", "seq", None), check_vma=False
    )
```

time: 495 us -> 322 us (0.65)
  waiting for transfers between devices: 443 us -> 182 us
  starting transfers between devices: 0.16 us -> 87.8 us
  between operations: 14.5 us -> 2.37 us
  matrix products: 21.2 us -> 27.3 us
    all_gather x3 -> x0, waiting for transfers between devices: 368 us -> none  [the longest x1 233 us: on_device(): full_down = lax.all_gather(down_proj, 'dp', axis=1, tiled=True)]
    ppermute x0 -> x49, waiting for transfers between devices: none -> 182 us  [the longest x25 137 us: swap(): return lax.ppermute(value, self.name, pairs)]
    ppermute x0 -> x49, starting transfers between devices: none -> 87.8 us  [the longest x24 66 us: shift(): return lax.ppermute(value, self.name, pairs)]
    reduce_scatter x2 -> x0, waiting for transfers between devices: 73.6 us -> none  [the longest x1 42 us: on_device(): lax.psum_scatter(jnp.dot(row_block, full_down, preferred_element_type=jnp...]
    unnamed x10 -> x21, local copies, waits for them, and re-layouts: 9.51 us -> 1.52 us
    slice x1 -> x2, local copies, waits for them, and re-layouts: 0.36 us -> 6.85 us  [the longest x1 4.42 us: on_device(): keys_local, values_local = (kv_proj[:, 0], kv_proj[:, 1])]
    dot_general x5 -> x38, matrix products: 21.2 us -> 27.3 us  [the longest x36 26.9 us: on_device(): dot = lambda a, b: jnp.dot(a, b, preferred_element_type=jnp.float32)]
    select_n x0 -> x9, other arithmetic: none -> 5.39 us  [the longest x8 5.3 us: gather(): value = jnp.where(self.at - (self.at ^ m) == move, hops[move][p], value)]
  transfers between devices with their start and end apart: 5 -> 49, of which waited for: 5 -> 23; matrix products, arithmetic and copies ran while one was open for 3% -> 13% of each run, Pallas kernels for 0% -> 0%
where the time goes in v1:
time: 322 us; the launch traced here: 320 us
  waiting for transfers between devices  182 us (57%)
  starting transfers between devices  87.8 us (27%)
  matrix products  27.3 us (8%)
  local copies, waits for them, and re-layouts  11.8 us (4%)
  other arithmetic  9.2 us (3%)
    ppermute x25, waiting for transfers between devices, swap(): return lax.ppermute(value, self.name, pairs)  137 us
    ppermute x24, starting transfers between devices, shift(): return lax.ppermute(value, self.name, pairs)  66 us
    ppermute x24, waiting for transfers between devices, shift(): return lax.ppermute(value, self.name, pairs)  44.9 us
    dot_general x36, matrix products, on_device(): dot = lambda a, b: jnp.dot(a, b, preferred_element_type=jnp.float32)  26.9 us
    ppermute x25, starting transfers between devices, swap(): return lax.ppermute(value, self.name, pairs)  21.8 us
  transfers between devices with their start and end apart: 49, of which 23 were waited for; matrix products, arithmetic and copies ran while one was open for 13% of the time, Pallas kernels for 0%

profile of v1, /device:TPU:0, one launch (start us, length us, event | category | flops | bytes accessed | tf_op | source)
XLA Modules:
  0.0 320.3 jit_solution(15384981352660912122)
XLA Ops:
  0.0 2.4 slice_bitcast_fusion
  2.4 5.7 %collective-permute-start.5 = (bf16[128,2048]{1,0:T(8,128)(2,1)}, bf16[128,2048]{1,0:T(8,128)(2,1)}, u32[]{:S(2)}, u32[]{:S(2)}) collective-permute-start(bf16[128,2048]{1,0:T(8,128)(2,1)} %get-tuple-element.25), channel_id=1, source_target_pairs={{0,2},{1,3},{2,4},{3,5},{4,6},{5,7},{8,10},{9,11},{10,12},{11,13},... | collective-permute-start | bytes 1572872 | tf_op jit(solution)/shard_map/ppermute | solution.py:25
  9.5 5.4 %collective-permute-start.3 = (bf16[128,2048]{1,0:T(8,128)(2,1)}, bf16[128,2048]{1,0:T(8,128)(2,1)}, u32[]{:S(2)}, u32[]{:S(2)}) collective-permute-start(bf16[128,2048]{1,0:T(8,128)(2,1)} %get-tuple-element.26), channel_id=1, source_target_pairs={{0,2},{1,3},{2,4},{3,5},{4,6},{5,7},{8,10},{9,11},{10,12},{11,13},... | collective-permute-start | bytes 1572872 | tf_op jit(solution)/shard_map/ppermute | solution.py:25
  20.3 4.4 %fusion.60 = (bf16[512,1,512]{2,1,0:T(2,128)(2,1)}, bf16[512,1,512]{2,1,0:T(2,128)(2,1)}) fusion(bf16[512,2,512]{2,1,0:T(2,128)(2,1)} %param.13), kind=kLoop, calls=%fused_computation.150 | loop fusion | bytes 2097152 | tf_op jit(solution)/shard_map/slice | solution.py:88
  24.7 5.4 %collective-permute-start.12 = (bf16[128,2048]{1,0:T(8,128)(2,1)}, bf16[128,2048]{1,0:T(8,128)(2,1)}, u32[]{:S(2)}, u32[]{:S(2)}) collective-permute-start(bf16[128,2048]{1,0:T(8,128)(2,1)} %collective-permute-done.5), channel_id=1, source_target_pairs={{0,2},{1,3},{2,4},{3,5},{4,6},{5,7},{8,10},{9,11},{10,12},{11,13},... | collective-permute-start | bytes 1572872 | tf_op jit(solution)/shard_map/ppermute | solution.py:25
  32.2 2.9 copy_bitcast_fusion
  35.0 5.3 %collective-permute-start.10 = (bf16[128,2048]{1,0:T(8,128)(2,1)}, bf16[128,2048]{1,0:T(8,128)(2,1)}, u32[]{:S(2)}, u32[]{:S(2)}) collective-permute-start(bf16[128,2048]{1,0:T(8,128)(2,1)} %collective-permute-done.3), channel_id=1, source_target_pairs={{0,2},{1,3},{2,4},{3,5},{4,6},{5,7},{8,10},{9,11},{10,12},{11,13},... | collective-permute-start | bytes 1572872 | tf_op jit(solution)/shard_map/ppermute | solution.py:25
  42.5 5.2 %collective-permute-done.13 = bf16[128,2048]{1,0:T(8,128)(2,1)} collective-permute-done((bf16[128,2048]{1,0:T(8,128)(2,1)}, bf16[128,2048]{1,0:T(8,128)(2,1)}, u32[]{:S(2)}, u32[]{:S(2)}) %collective-permute-start.13) | collective-permute-done | bytes 524320 | tf_op jit(solution)/shard_map/ppermute | solution.py:25
  48.8 3.8 %collective-permute-done.10 = bf16[128,2048]{1,0:T(8,128)(2,1)} collective-permute-done((bf16[128,2048]{1,0:T(8,128)(2,1)}, bf16[128,2048]{1,0:T(8,128)(2,1)}, u32[]{:S(2)}, u32[]{:S(2)}) %collective-permute-start.10) | collective-permute-done | bytes 524320 | tf_op jit(solution)/shard_map/ppermute | solution.py:25
  52.5 4.9 %collective-permute-done.11 = bf16[128,2048]{1,0:T(8,128)(2,1)} collective-permute-done((bf16[128,2048]{1,0:T(8,128)(2,1)}, bf16[128,2048]{1,0:T(8,128)(2,1)}, u32[]{:S(2)}, u32[]{:S(2)}) %collective-permute-start.11) | collective-permute-done | bytes 524320 | tf_op jit(solution)/shard_map/ppermute | solution.py:25
  59.8 2.7 collective-permute-start.19
  63.8 4.6 %collective-permute-start.17 = (bf16[128,2048]{1,0:T(8,128)(2,1)}, bf16[128,2048]{1,0:T(8,128)(2,1)S(1)}, u32[]{:S(2)}, u32[]{:S(2)}) collective-permute-start(bf16[128,2048]{1,0:T(8,128)(2,1)} %collective-permute-done.10), channel_id=1, source_target_pairs={{0,2},{1,3},{2,4},{3,5},{4,6},{5,7},{8,10},{9,11},{10,12},{11,13},... | collective-permute-start | bytes 1572872 | tf_op jit(solution)/shard_map/ppermute | solution.py:25
  70.6 4.5 %collective-permute-done.19 = bf16[128,2048]{1,0:T(8,128)(2,1)S(1)} collective-permute-done((bf16[128,2048]{1,0:T(8,128)(2,1)}, bf16[128,2048]{1,0:T(8,128)(2,1)S(1)}, u32[]{:S(2)}, u32[]{:S(2)}) %collective-permute-start.19) | collective-permute-done | bytes 524320 | tf_op jit(solution)/shard_map/ppermute | solution.py:25
  75.1 4.3 %collective-permute-done.20 = bf16[128,2048]{1,0:T(8,128)(2,1)S(1)} collective-permute-done((bf16[128,2048]{1,0:T(8,128)(2,1)}, bf16[128,2048]{1,0:T(8,128)(2,1)S(1)}, u32[]{:S(2)}, u32[]{:S(2)}) %collective-permute-start.20) | collective-permute-done | bytes 524320 | tf_op jit(solution)/shard_map/ppermute | solution.py:25
  80.8 3.2 collective-permute-done.17
  84.0 4.0 %collective-permute-done.18 = bf16[128,2048]{1,0:T(8,128)(2,1)S(1)} collective-permute-done((bf16[128,2048]{1,0:T(8,128)(2,1)}, bf16[128,2048]{1,0:T(8,128)(2,1)S(1)}, u32[]{:S(2)}, u32[]{:S(2)}) %collective-permute-start.18) | collective-permute-done | bytes 524320 | tf_op jit(solution)/shard_map/ppermute | solution.py:25
  89.4 3.5 %collective-permute-start.28 = (bf16[512,512]{1,0:T(8,128)(2,1)S(1)}, bf16[512,512]{1,0:T(8,128)(2,1)S(1)}, u32[]{:S(2)}, u32[]{:S(2)}) collective-permute-start(bf16[512,512]{1,0:T(8,128)(2,1)S(1)} %copy-done.3), channel_id=1, source_target_pairs={{0,2},{1,3},{2,4},{3,5},{4,6},{5,7},{8,10},{9,11},{10,12},{11,13},... | collective-permute-start | bytes 1572872 | tf_op jit(solution)/shard_map/ppermute | solution.py:25
  96.4 2.0 fusion.78
  98.6 2.0 fusion.74
  101.2 2.0 fusion.70
  103.4 2.0 fusion.76
  105.4 2.0 fusion.72
  107.5 2.0 fusion.68
  109.5 2.0 fusion.66
  111.6 2.1 fusion.64
  113.8 4.6 %collective-permute-start.38 = (bf16[512,512]{1,0:T(8,128)(2,1)S(1)}, bf16[512,512]{1,0:T(8,128)(2,1)S(1)}, u32[]{:S(2)}, u32[]{:S(2)}) collective-permute-start(bf16[512,512]{1,0:T(8,128)(2,1)S(1)} %copy-done.2), channel_id=1, source_target_pairs={{0,2},{1,3},{2,4},{3,5},{4,6},{5,7},{8,10},{9,11},{10,12},{11,13},... | collective-permute-start | bytes 1572872 | tf_op jit(solution)/shard_map/ppermute | solution.py:25
  122.7 6.9 %collective-permute-done.22 = f32[64,1024]{1,0:T(8,128)S(1)} collective-permute-done((f32[64,1024]{1,0:T(8,128)S(1)}, f32[64,1024]{1,0:T(8,128)S(1)}, u32[]{:S(2)}, u32[]{:S(2)}) %collective-permute-start.22) | collective-permute-done | bytes 262176 | tf_op jit(solution)/shard_map/ppermute | solution.py:32
  131.1 4.5 %collective-permute-start.31 = (bf16[512,512]{1,0:T(8,128)(2,1)S(1)}, bf16[512,512]{1,0:T(8,128)(2,1)S(1)}, u32[]{:S(2)}, u32[]{:S(2)}) collective-permute-start(bf16[512,512]{1,0:T(8,128)(2,1)S(1)} %collective-permute-done.28), channel_id=1, source_target_pairs={{0,2},{1,3},{2,4},{3,5},{4,6},{5,7},{8,10},{9,11},{10,12},{11,13},... | collective-permute-start | bytes 1572872 | tf_op jit(solution)/shard_map/ppermute | solution.py:25
  136.9 4.6 %collective-permute-start.41 = (bf16[512,512]{1,0:T(8,128)(2,1)S(1)}, bf16[512,512]{1,0:T(8,128)(2,1)S(1)}, u32[]{:S(2)}, u32[]{:S(2)}) collective-permute-start(bf16[512,512]{1,0:T(8,128)(2,1)S(1)} %collective-permute-done.38), channel_id=1, source_target_pairs={{0,2},{1,3},{2,4},{3,5},{4,6},{5,7},{8,10},{9,11},{10,12},{11,13},... | collective-permute-start | bytes 1572872 | tf_op jit(solution)/shard_map/ppermute | solution.py:25
  143.5 4.4 %collective-permute-done.31 = bf16[512,512]{1,0:T(8,128)(2,1)S(1)} collective-permute-done((bf16[512,512]{1,0:T(8,128)(2,1)S(1)}, bf16[512,512]{1,0:T(8,128)(2,1)S(1)}, u32[]{:S(2)}, u32[]{:S(2)}) %collective-permute-start.31) | collective-permute-done | bytes 524320 | tf_op jit(solution)/shard_map/ppermute | solution.py:25
  147.9 2.5 collective-permute-start.9
  150.4 1.9 collective-permute-done.32
  152.4 2.2 collective-permute-start.34
  154.5 4.6 %collective-permute-done.41 = bf16[512,512]{1,0:T(8,128)(2,1)S(1)} collective-permute-done((bf16[512,512]{1,0:T(8,128)(2,1)S(1)}, bf16[512,512]{1,0:T(8,128)(2,1)S(1)}, u32[]{:S(2)}, u32[]{:S(2)}) %collective-permute-start.41) | collective-permute-done | bytes 524320 | tf_op jit(solution)/shard_map/ppermute | solution.py:25
  160.4 3.1 collective-permute-done.42
  163.6 1.9 collective-permute-start.44
  167.0 2.2 collective-permute-done.9
  169.2 2.0 collective-permute-start.16
  171.2 25.4 %collective-permute-done.16 = f32[64,1024]{1,0:T(8,128)S(1)} collective-permute-done((f32[64,1024]{1,0:T(8,128)S(1)}, f32[64,1024]{1,0:T(8,128)S(1)}, u32[]{:S(2)}, u32[]{:S(2)}) %collective-permute-start.16) | collective-permute-done | bytes 262176 | tf_op jit(solution)/shard_map/ppermute | solution.py:32
  196.7 8.2 %collective-permute-done.23 = f32[64,1024]{1,0:T(8,128)S(1)} collective-permute-done((f32[64,1024]{1,0:T(8,128)S(1)}, f32[64,1024]{1,0:T(8,128)S(1)}, u32[]{:S(2)}, u32[]{:S(2)}) %collective-permute-start.23) | collective-permute-done | bytes 262176 | tf_op jit(solution)/shard_map/ppermute | solution.py:32
  207.5 7.0 %collective-permute-done.25 = bf16[64,4096]{1,0:T(8,128)(2,1)S(1)} collective-permute-done((bf16[64,4096]{1,0:T(8,128)(2,1)S(1)}, bf16[64,4096]{1,0:T(8,128)(2,1)S(1)}, u32[]{:S(2)}, u32[]{:S(2)}) %collective-permute-start.25) | collective-permute-done | bytes 524320 | tf_op jit(solution)/shard_map/ppermute | solution.py:32
  214.7 1.6 collective-permute-start.37
  216.9 1.6 collective-permute-start.43
  219.8 42.9 %collective-permute-done.30 = bf16[512,512]{1,0:T(8,128)(2,1)S(1)} collective-permute-done((bf16[512,512]{1,0:T(8,128)(2,1)S(1)}, bf16[512,512]{1,0:T(8,128)(2,1)S(1)}, u32[]{:S(2)}, u32[]{:S(2)}) %collective-permute-start.30) | collective-permute-done | bytes 524320 | tf_op jit(solution)/shard_map/ppermute | solution.py:32
  267.7 21.1 %collective-permute-done.36 = bf16[512,512]{1,0:T(8,128)(2,1)S(1)} collective-permute-done((bf16[512,512]{1,0:T(8,128)(2,1)S(1)}, bf16[512,512]{1,0:T(8,128)(2,1)S(1)}, u32[]{:S(2)}, u32[]{:S(2)}) %collective-permute-start.36) | collective-permute-done | bytes 524320 | tf_op jit(solution)/shard_map/ppermute | solution.py:32
  291.9 6.9 %collective-permute-done.46 = bf16[512,512]{1,0:T(8,128)(2,1)S(1)} collective-permute-done((bf16[512,512]{1,0:T(8,128)(2,1)S(1)}, bf16[512,512]{1,0:T(8,128)(2,1)S(1)}, u32[]{:S(2)}, u32[]{:S(2)}) %collective-permute-start.46) | collective-permute-done | bytes 524320 | tf_op jit(solution)/shard_map/ppermute | solution.py:32
  301.9 2.6 collective-permute-done.47
  306.1 13.5 %collective-permute-done.48 = f32[32,4096]{1,0:T(8,128)S(1)} collective-permute-done((f32[32,4096]{1,0:T(8,128)S(1)}, f32[32,4096]{1,0:T(8,128)S(1)}, u32[]{:S(2)}, u32[]{:S(2)}) %collective-permute-start.48) | collective-permute-done | bytes 524320 | tf_op jit(solution)/shard_map/ppermute | solution.py:32
  (167 shorter events, 53.1 us)
Async XLA Ops:
  2.4 22.3 %collective-permute-start.5 = (bf16[128,2048]{1,0:T(8,128)(2,1)}, bf16[128,2048]{1,0:T(8,128)(2,1)}, u32[]{:S(2)}, u32[]{:S(2)}) collective-permute-start(bf16[128,2048]{1,0:T(8,128)(2,1)} %get-tuple-element.25), channel_id=1, source_target_pairs={{0,2},{1,3},{2,4},{3,5},{4,6},{5,7},{8,10},{9,11},{10,12},{11,13},... | collective-permute-start | bytes 1572872 | tf_op jit(solution)/shard_map/ppermute | solution.py:25
  8.2 21.9 %collective-permute-start.6 = (bf16[128,2048]{1,0:T(8,128)(2,1)}, bf16[128,2048]{1,0:T(8,128)(2,1)}, u32[]{:S(2)}, u32[]{:S(2)}) collective-permute-start(bf16[128,2048]{1,0:T(8,128)(2,1)} %get-tuple-element.25), channel_id=1, source_target_pairs={{2,0},{3,1},{4,2},{5,3},{6,4},{7,5},{10,8},{11,9},{12,10},{13,11},... | collective-permute-start | bytes 1572872 | tf_op jit(solution)/shard_map/ppermute | solution.py:25
  9.5 25.6 %collective-permute-start.3 = (bf16[128,2048]{1,0:T(8,128)(2,1)}, bf16[128,2048]{1,0:T(8,128)(2,1)}, u32[]{:S(2)}, u32[]{:S(2)}) collective-permute-start(bf16[128,2048]{1,0:T(8,128)(2,1)} %get-tuple-element.26), channel_id=1, source_target_pairs={{0,2},{1,3},{2,4},{3,5},{4,6},{5,7},{8,10},{9,11},{10,12},{11,13},... | collective-permute-start | bytes 1572872 | tf_op jit(solution)/shard_map/ppermute | solution.py:25
  14.8 25.5 %collective-permute-start.4 = (bf16[128,2048]{1,0:T(8,128)(2,1)}, bf16[128,2048]{1,0:T(8,128)(2,1)}, u32[]{:S(2)}, u32[]{:S(2)}) collective-permute-start(bf16[128,2048]{1,0:T(8,128)(2,1)} %get-tuple-element.26), channel_id=1, source_target_pairs={{2,0},{3,1},{4,2},{5,3},{6,4},{7,5},{10,8},{11,9},{12,10},{13,11},... | collective-permute-start | bytes 1572872 | tf_op jit(solution)/shard_map/ppermute | solution.py:25
  16.1 80.3 %collective-permute-start = (bf16[2048,512]{1,0:T(8,128)(2,1)S(1)}, bf16[2048,512]{1,0:T(8,128)(2,1)}, u32[]{:S(2)}, u32[]{:S(2)}) collective-permute-start(bf16[2048,512]{1,0:T(8,128)(2,1)S(1)} %copy-done), channel_id=1, source_target_pairs={{0,1},{1,0},{2,3},{3,2},{4,5},{5,4},{6,7},{7,6},{8,9},{9,8},{10,11... | collective-permute-start | bytes 6291464 | tf_op jit(solution)/shard_map/ppermute | solution.py:32
  24.7 17.8 %collective-permute-start.12 = (bf16[128,2048]{1,0:T(8,128)(2,1)}, bf16[128,2048]{1,0:T(8,128)(2,1)}, u32[]{:S(2)}, u32[]{:S(2)}) collective-permute-start(bf16[128,2048]{1,0:T(8,128)(2,1)} %collective-permute-done.5), channel_id=1, source_target_pairs={{0,2},{1,3},{2,4},{3,5},{4,6},{5,7},{8,10},{9,11},{10,12},{11,13},... | collective-permute-start | bytes 1572872 | tf_op jit(solution)/shard_map/ppermute | solution.py:25
  30.1 17.6 %collective-permute-start.13 = (bf16[128,2048]{1,0:T(8,128)(2,1)}, bf16[128,2048]{1,0:T(8,128)(2,1)}, u32[]{:S(2)}, u32[]{:S(2)}) collective-permute-start(bf16[128,2048]{1,0:T(8,128)(2,1)} %collective-permute-done.6), channel_id=1, source_target_pairs={{2,0},{3,1},{4,2},{5,3},{6,4},{7,5},{10,8},{11,9},{12,10},{13,11},... | collective-permute-start | bytes 1572872 | tf_op jit(solution)/shard_map/ppermute | solution.py:25
  35.0 17.5 %collective-permute-start.10 = (bf16[128,2048]{1,0:T(8,128)(2,1)}, bf16[128,2048]{1,0:T(8,128)(2,1)}, u32[]{:S(2)}, u32[]{:S(2)}) collective-permute-start(bf16[128,2048]{1,0:T(8,128)(2,1)} %collective-permute-done.3), channel_id=1, source_target_pairs={{0,2},{1,3},{2,4},{3,5},{4,6},{5,7},{8,10},{9,11},{10,12},{11,13},... | collective-permute-start | bytes 1572872 | tf_op jit(solution)/shard_map/ppermute | solution.py:25
  40.4 17.1 %collective-permute-start.11 = (bf16[128,2048]{1,0:T(8,128)(2,1)}, bf16[128,2048]{1,0:T(8,128)(2,1)}, u32[]{:S(2)}, u32[]{:S(2)}) collective-permute-start(bf16[128,2048]{1,0:T(8,128)(2,1)} %collective-permute-done.4), channel_id=1, source_target_pairs={{2,0},{3,1},{4,2},{5,3},{6,4},{7,5},{10,8},{11,9},{12,10},{13,11},... | collective-permute-start | bytes 1572872 | tf_op jit(solution)/shard_map/ppermute | solution.py:25
  59.8 15.4 %collective-permute-start.19 = (bf16[128,2048]{1,0:T(8,128)(2,1)}, bf16[128,2048]{1,0:T(8,128)(2,1)S(1)}, u32[]{:S(2)}, u32[]{:S(2)}) collective-permute-start(bf16[128,2048]{1,0:T(8,128)(2,1)} %collective-permute-done.12), channel_id=1, source_target_pairs={{0,2},{1,3},{2,4},{3,5},{4,6},{5,7},{8,10},{9,11},{10,12},{11,13},... | collective-permute-start | bytes 1572872 | tf_op jit(solution)/shard_map/ppermute | solution.py:25
  62.5 17.0 %collective-permute-start.20 = (bf16[128,2048]{1,0:T(8,128)(2,1)}, bf16[128,2048]{1,0:T(8,128)(2,1)S(1)}, u32[]{:S(2)}, u32[]{:S(2)}) collective-permute-start(bf16[128,2048]{1,0:T(8,128)(2,1)} %collective-permute-done.13), channel_id=1, source_target_pairs={{2,0},{3,1},{4,2},{5,3},{6,4},{7,5},{10,8},{11,9},{12,10},{13,11},... | collective-permute-start | bytes 1572872 | tf_op jit(solution)/shard_map/ppermute | solution.py:25
  63.8 20.2 %collective-permute-start.17 = (bf16[128,2048]{1,0:T(8,128)(2,1)}, bf16[128,2048]{1,0:T(8,128)(2,1)S(1)}, u32[]{:S(2)}, u32[]{:S(2)}) collective-permute-start(bf16[128,2048]{1,0:T(8,128)(2,1)} %collective-permute-done.10), channel_id=1, source_target_pairs={{0,2},{1,3},{2,4},{3,5},{4,6},{5,7},{8,10},{9,11},{10,12},{11,13},... | collective-permute-start | bytes 1572872 | tf_op jit(solution)/shard_map/ppermute | solution.py:25
  68.4 19.6 %collective-permute-start.18 = (bf16[128,2048]{1,0:T(8,128)(2,1)}, bf16[128,2048]{1,0:T(8,128)(2,1)S(1)}, u32[]{:S(2)}, u32[]{:S(2)}) collective-permute-start(bf16[128,2048]{1,0:T(8,128)(2,1)} %collective-permute-done.11), channel_id=1, source_target_pairs={{2,0},{3,1},{4,2},{5,3},{6,4},{7,5},{10,8},{11,9},{12,10},{13,11},... | collective-permute-start | bytes 1572872 | tf_op jit(solution)/shard_map/ppermute | solution.py:25
  89.4 32.7 %collective-permute-start.28 = (bf16[512,512]{1,0:T(8,128)(2,1)S(1)}, bf16[512,512]{1,0:T(8,128)(2,1)S(1)}, u32[]{:S(2)}, u32[]{:S(2)}) collective-permute-start(bf16[512,512]{1,0:T(8,128)(2,1)S(1)} %copy-done.3), channel_id=1, source_target_pairs={{0,2},{1,3},{2,4},{3,5},{4,6},{5,7},{8,10},{9,11},{10,12},{11,13},... | collective-permute-start | bytes 1572872 | tf_op jit(solution)/shard_map/ppermute | solution.py:25
  92.9 38.2 %collective-permute-start.29 = (bf16[512,512]{1,0:T(8,128)(2,1)S(1)}, bf16[512,512]{1,0:T(8,128)(2,1)S(1)}, u32[]{:S(2)}, u32[]{:S(2)}) collective-permute-start(bf16[512,512]{1,0:T(8,128)(2,1)S(1)} %copy-done.3), channel_id=1, source_target_pairs={{2,0},{3,1},{4,2},{5,3},{6,4},{7,5},{10,8},{11,9},{12,10},{13,11},... | collective-permute-start | bytes 1572872 | tf_op jit(solution)/shard_map/ppermute | solution.py:25
  98.5 15.2 %collective-permute-start.21 = (f32[128,1024]{1,0:T(8,128)S(1)}, f32[128,1024]{1,0:T(8,128)S(1)}, u32[]{:S(2)}, u32[]{:S(2)}) collective-permute-start(f32[128,1024]{1,0:T(8,128)S(1)} %pad_maximum_fusion.8), channel_id=1, source_target_pairs={{0,8},{8,0},{16,24},{24,16},{1,9},{9,1},{17,25},{25,17},{2,10},{10... | collective-permute-start | bytes 1572872 | tf_op jit(solution)/shard_map/ppermute | solution.py:32
  100.7 17.7 %collective-permute-start.14 = (f32[128,1024]{1,0:T(8,128)S(1)}, f32[128,1024]{1,0:T(8,128)S(1)}, u32[]{:S(2)}, u32[]{:S(2)}) collective-permute-start(f32[128,1024]{1,0:T(8,128)S(1)} %pad_maximum_fusion.7), channel_id=1, source_target_pairs={{0,8},{8,0},{16,24},{24,16},{1,9},{9,1},{17,25},{25,17},{2,10},{10... | collective-permute-start | bytes 1572872 | tf_op jit(solution)/shard_map/ppermute | solution.py:32
  103.3 15.4 %collective-permute-start.7 = (f32[128,1024]{1,0:T(8,128)S(1)}, f32[128,1024]{1,0:T(8,128)S(1)}, u32[]{:S(2)}, u32[]{:S(2)}) collective-permute-start(f32[128,1024]{1,0:T(8,128)S(1)} %pad_maximum_fusion.6), channel_id=1, source_target_pairs={{0,8},{8,0},{16,24},{24,16},{1,9},{9,1},{17,25},{25,17},{2,10},{10... | collective-permute-start | bytes 1572872 | tf_op jit(solution)/shard_map/ppermute | solution.py:32
  113.8 21.8 %collective-permute-start.38 = (bf16[512,512]{1,0:T(8,128)(2,1)S(1)}, bf16[512,512]{1,0:T(8,128)(2,1)S(1)}, u32[]{:S(2)}, u32[]{:S(2)}) collective-permute-start(bf16[512,512]{1,0:T(8,128)(2,1)S(1)} %copy-done.2), channel_id=1, source_target_pairs={{0,2},{1,3},{2,4},{3,5},{4,6},{5,7},{8,10},{9,11},{10,12},{11,13},... | collective-permute-start | bytes 1572872 | tf_op jit(solution)/shard_map/ppermute | solution.py:25
  118.8 18.1 %collective-permute-start.39 = (bf16[512,512]{1,0:T(8,128)(2,1)S(1)}, bf16[512,512]{1,0:T(8,128)(2,1)S(1)}, u32[]{:S(2)}, u32[]{:S(2)}) collective-permute-start(bf16[512,512]{1,0:T(8,128)(2,1)S(1)} %copy-done.2), channel_id=1, source_target_pairs={{2,0},{3,1},{4,2},{5,3},{6,4},{7,5},{10,8},{11,9},{12,10},{13,11},... | collective-permute-start | bytes 1572872 | tf_op jit(solution)/shard_map/ppermute | solution.py:25
  120.4 9.1 %collective-permute-start.22 = (f32[64,1024]{1,0:T(8,128)S(1)}, f32[64,1024]{1,0:T(8,128)S(1)}, u32[]{:S(2)}, u32[]{:S(2)}) collective-permute-start(f32[64,1024]{1,0:T(8,128)S(1)} %dynamic-slice_bitcast_fusion.1), channel_id=1, source_target_pairs={{0,16},{8,24},{16,0},{24,8},{1,17},{9,25},{17,1},{25,9},{2,18},{10... | collective-permute-start | bytes 786440 | tf_op jit(solution)/shard_map/ppermute | solution.py:32
  122.1 19.4 %collective-permute-start.8 = (f32[64,1024]{1,0:T(8,128)S(1)}, f32[64,1024]{1,0:T(8,128)S(1)}, u32[]{:S(2)}, u32[]{:S(2)}) collective-permute-start(f32[64,1024]{1,0:T(8,128)S(1)} %dynamic-slice_bitcast_fusion.3), channel_id=1, source_target_pairs={{0,16},{8,24},{16,0},{24,8},{1,17},{9,25},{17,1},{25,9},{2,18},{10... | collective-permute-start | bytes 786440 | tf_op jit(solution)/shard_map/ppermute | solution.py:32
  129.5 13.3 %collective-permute-start.2 = (f32[64,1024]{1,0:T(8,128)S(1)}, f32[64,1024]{1,0:T(8,128)S(1)}, u32[]{:S(2)}, u32[]{:S(2)}) collective-permute-start(f32[64,1024]{1,0:T(8,128)S(1)} %dynamic-slice_bitcast_fusion.4), channel_id=1, source_target_pairs={{0,16},{8,24},{16,0},{24,8},{1,17},{9,25},{17,1},{25,9},{2,18},{10... | collective-permute-start | bytes 786440 | tf_op jit(solution)/shard_map/ppermute | solution.py:32
  131.1 16.8 %collective-permute-start.31 = (bf16[512,512]{1,0:T(8,128)(2,1)S(1)}, bf16[512,512]{1,0:T(8,128)(2,1)S(1)}, u32[]{:S(2)}, u32[]{:S(2)}) collective-permute-start(bf16[512,512]{1,0:T(8,128)(2,1)S(1)} %collective-permute-done.28), channel_id=1, source_target_pairs={{0,2},{1,3},{2,4},{3,5},{4,6},{5,7},{8,10},{9,11},{10,12},{11,13},... | collective-permute-start | bytes 1572872 | tf_op jit(solution)/shard_map/ppermute | solution.py:25
  135.6 16.8 %collective-permute-start.32 = (bf16[512,512]{1,0:T(8,128)(2,1)S(1)}, bf16[512,512]{1,0:T(8,128)(2,1)S(1)}, u32[]{:S(2)}, u32[]{:S(2)}) collective-permute-start(bf16[512,512]{1,0:T(8,128)(2,1)S(1)} %collective-permute-done.29), channel_id=1, source_target_pairs={{2,0},{3,1},{4,2},{5,3},{6,4},{7,5},{10,8},{11,9},{12,10},{13,11},... | collective-permute-start | bytes 1572872 | tf_op jit(solution)/shard_map/ppermute | solution.py:25
  136.9 22.2 %collective-permute-start.41 = (bf16[512,512]{1,0:T(8,128)(2,1)S(1)}, bf16[512,512]{1,0:T(8,128)(2,1)S(1)}, u32[]{:S(2)}, u32[]{:S(2)}) collective-permute-start(bf16[512,512]{1,0:T(8,128)(2,1)S(1)} %collective-permute-done.38), channel_id=1, source_target_pairs={{0,2},{1,3},{2,4},{3,5},{4,6},{5,7},{8,10},{9,11},{10,12},{11,13},... | collective-permute-start | bytes 1572872 | tf_op jit(solution)/shard_map/ppermute | solution.py:25
  141.5 22.1 %collective-permute-start.42 = (bf16[512,512]{1,0:T(8,128)(2,1)S(1)}, bf16[512,512]{1,0:T(8,128)(2,1)S(1)}, u32[]{:S(2)}, u32[]{:S(2)}) collective-permute-start(bf16[512,512]{1,0:T(8,128)(2,1)S(1)} %collective-permute-done.39), channel_id=1, source_target_pairs={{2,0},{3,1},{4,2},{5,3},{6,4},{7,5},{10,8},{11,9},{12,10},{13,11},... | collective-permute-start | bytes 1572872 | tf_op jit(solution)/shard_map/ppermute | solution.py:25
  142.9 22.6 %collective-permute-start.15 = (f32[64,1024]{1,0:T(8,128)S(1)}, f32[64,1024]{1,0:T(8,128)S(1)}, u32[]{:S(2)}, u32[]{:S(2)}) collective-permute-start(f32[64,1024]{1,0:T(8,128)S(1)} %dynamic-slice_bitcast_fusion.2), channel_id=1, source_target_pairs={{0,16},{8,24},{16,0},{24,8},{1,17},{9,25},{17,1},{25,9},{2,18},{10... | collective-permute-start | bytes 786440 | tf_op jit(solution)/shard_map/ppermute | solution.py:32
  147.9 21.3 %collective-permute-start.9 = (f32[64,1024]{1,0:T(8,128)S(1)}, f32[64,1024]{1,0:T(8,128)S(1)}, u32[]{:S(2)}, u32[]{:S(2)}) collective-permute-start(f32[64,1024]{1,0:T(8,128)S(1)} %bitcast_add_fusion.3), channel_id=1, source_target_pairs={{0,2},{1,3},{2,0},{3,1},{4,6},{5,7},{6,4},{7,5},{8,10},{9,11},{10,... | collective-permute-start | bytes 786440 | tf_op jit(solution)/shard_map/ppermute | solution.py:32
  152.4 53.6 %collective-permute-start.34 = (bf16[512,512]{1,0:T(8,128)(2,1)S(1)}, bf16[512,512]{1,0:T(8,128)(2,1)S(1)}, u32[]{:S(2)}, u32[]{:S(2)}) collective-permute-start(bf16[512,512]{1,0:T(8,128)(2,1)S(1)} %collective-permute-done.31), channel_id=1, source_target_pairs={{0,2},{1,3},{2,4},{3,5},{4,6},{5,7},{8,10},{9,11},{10,12},{11,13},... | collective-permute-start | bytes 1572872 | tf_op jit(solution)/shard_map/ppermute | solution.py:25
  159.2 48.4 %collective-permute-start.35 = (bf16[512,512]{1,0:T(8,128)(2,1)S(1)}, bf16[512,512]{1,0:T(8,128)(2,1)S(1)}, u32[]{:S(2)}, u32[]{:S(2)}) collective-permute-start(bf16[512,512]{1,0:T(8,128)(2,1)S(1)} %collective-permute-done.32), channel_id=1, source_target_pairs={{2,0},{3,1},{4,2},{5,3},{6,4},{7,5},{10,8},{11,9},{12,10},{13,11},... | collective-permute-start | bytes 1572872 | tf_op jit(solution)/shard_map/ppermute | solution.py:25
  163.6 51.1 %collective-permute-start.44 = (bf16[512,512]{1,0:T(8,128)(2,1)S(1)}, bf16[512,512]{1,0:T(8,128)(2,1)S(1)}, u32[]{:S(2)}, u32[]{:S(2)}) collective-permute-start(bf16[512,512]{1,0:T(8,128)(2,1)S(1)} %collective-permute-done.41), channel_id=1, source_target_pairs={{0,2},{1,3},{2,4},{3,5},{4,6},{5,7},{8,10},{9,11},{10,12},{11,13},... | collective-permute-start | bytes 1572872 | tf_op jit(solution)/shard_map/ppermute | solution.py:25
  165.5 50.7 %collective-permute-start.45 = (bf16[512,512]{1,0:T(8,128)(2,1)S(1)}, bf16[512,512]{1,0:T(8,128)(2,1)S(1)}, u32[]{:S(2)}, u32[]{:S(2)}) collective-permute-start(bf16[512,512]{1,0:T(8,128)(2,1)S(1)} %collective-permute-done.42), channel_id=1, source_target_pairs={{2,0},{3,1},{4,2},{5,3},{6,4},{7,5},{10,8},{11,9},{12,10},{13,11},... | collective-permute-start | bytes 1572872 | tf_op jit(solution)/shard_map/ppermute | solution.py:25
  169.2 27.4 %collective-permute-start.16 = (f32[64,1024]{1,0:T(8,128)S(1)}, f32[64,1024]{1,0:T(8,128)S(1)}, u32[]{:S(2)}, u32[]{:S(2)}) collective-permute-start(f32[64,1024]{1,0:T(8,128)S(1)} %bitcast_add_fusion.2), channel_id=1, source_target_pairs={{0,4},{1,5},{2,6},{3,7},{4,0},{5,1},{6,2},{7,3},{8,12},{9,13},{10,... | collective-permute-start | bytes 786440 | tf_op jit(solution)/shard_map/ppermute | solution.py:32
  196.6 8.2 %collective-permute-start.23 = (f32[64,1024]{1,0:T(8,128)S(1)}, f32[64,1024]{1,0:T(8,128)S(1)}, u32[]{:S(2)}, u32[]{:S(2)}) collective-permute-start(f32[64,1024]{1,0:T(8,128)S(1)} %bitcast_add_fusion.1), channel_id=1, source_target_pairs={{0,6},{1,7},{2,4},{3,5},{4,2},{5,3},{6,0},{7,1},{8,14},{9,15},{10,... | collective-permute-start | bytes 786440 | tf_op jit(solution)/shard_map/ppermute | solution.py:32
  205.3 9.2 %collective-permute-start.25 = (bf16[64,4096]{1,0:T(8,128)(2,1)S(1)}, bf16[64,4096]{1,0:T(8,128)(2,1)S(1)}, u32[]{:S(2)}, u32[]{:S(2)}) collective-permute-start(bf16[64,4096]{1,0:T(8,128)(2,1)S(1)} %multiply_convert_fusion), channel_id=1, source_target_pairs={{0,16},{8,24},{16,0},{24,8},{1,17},{9,25},{17,1},{25,9},{2,18},{10... | collective-permute-start | bytes 1572872 | tf_op jit(solution)/shard_map/ppermute | solution.py:32
  206.0 58.6 %collective-permute-start.27 = (bf16[512,512]{1,0:T(8,128)(2,1)S(1)}, bf16[512,512]{1,0:T(8,128)(2,1)S(1)}, u32[]{:S(2)}, u32[]{:S(2)}) collective-permute-start(bf16[512,512]{1,0:T(8,128)(2,1)S(1)} %copy-done.3), channel_id=1, source_target_pairs={{0,1},{1,0},{2,3},{3,2},{4,5},{5,4},{6,7},{7,6},{8,9},{9,8},{10,11... | collective-permute-start | bytes 1572872 | tf_op jit(solution)/shard_map/ppermute | solution.py:32
  207.5 9.4 %collective-permute-start.24 = (bf16[64,4096]{1,0:T(8,128)(2,1)S(1)}, bf16[64,4096]{1,0:T(8,128)(2,1)S(1)}, u32[]{:S(2)}, u32[]{:S(2)}) collective-permute-start(bf16[64,4096]{1,0:T(8,128)(2,1)S(1)} %multiply_convert_fusion), channel_id=1, source_target_pairs={{0,8},{8,0},{16,24},{24,16},{1,9},{9,1},{17,25},{25,17},{2,10},{10... | collective-permute-start | bytes 1572872 | tf_op jit(solution)/shard_map/ppermute | solution.py:32
  214.5 4.0 %collective-permute-start.26 = (bf16[64,4096]{1,0:T(8,128)(2,1)S(1)}, bf16[64,4096]{1,0:T(8,128)(2,1)S(1)}, u32[]{:S(2)}, u32[]{:S(2)}) collective-permute-start(bf16[64,4096]{1,0:T(8,128)(2,1)S(1)} %collective-permute-done.25), channel_id=1, source_target_pairs={{0,8},{8,0},{16,24},{24,16},{1,9},{9,1},{17,25},{25,17},{2,10},{10... | collective-permute-start | bytes 1572872 | tf_op jit(solution)/shard_map/ppermute | solution.py:32
  214.7 74.8 %collective-permute-start.37 = (bf16[512,512]{1,0:T(8,128)(2,1)S(1)}, bf16[512,512]{1,0:T(8,128)(2,1)S(1)}, u32[]{:S(2)}, u32[]{:S(2)}) collective-permute-start(bf16[512,512]{1,0:T(8,128)(2,1)S(1)} %copy-done.2), channel_id=1, source_target_pairs={{0,1},{1,0},{2,3},{3,2},{4,5},{5,4},{6,7},{7,6},{8,9},{9,8},{10,11... | collective-permute-start | bytes 1572872 | tf_op jit(solution)/shard_map/ppermute | solution.py:32
  216.3 49.2 %collective-permute-start.33 = (bf16[512,512]{1,0:T(8,128)(2,1)S(1)}, bf16[512,512]{1,0:T(8,128)(2,1)S(1)}, u32[]{:S(2)}, u32[]{:S(2)}) collective-permute-start(bf16[512,512]{1,0:T(8,128)(2,1)S(1)} %broadcast_select_fusion.1), channel_id=1, source_target_pairs={{0,1},{1,0},{2,3},{3,2},{4,5},{5,4},{6,7},{7,6},{8,9},{9,8},{10,11... | collective-permute-start | bytes 1572872 | tf_op jit(solution)/shard_map/ppermute | solution.py:32
  216.9 74.0 %collective-permute-start.43 = (bf16[512,512]{1,0:T(8,128)(2,1)S(1)}, bf16[512,512]{1,0:T(8,128)(2,1)S(1)}, u32[]{:S(2)}, u32[]{:S(2)}) collective-permute-start(bf16[512,512]{1,0:T(8,128)(2,1)S(1)} %broadcast_select_fusion), channel_id=1, source_target_pairs={{0,1},{1,0},{2,3},{3,2},{4,5},{5,4},{6,7},{7,6},{8,9},{9,8},{10,11... | collective-permute-start | bytes 1572872 | tf_op jit(solution)/shard_map/ppermute | solution.py:32
  218.5 44.2 %collective-permute-start.30 = (bf16[512,512]{1,0:T(8,128)(2,1)S(1)}, bf16[512,512]{1,0:T(8,128)(2,1)S(1)}, u32[]{:S(2)}, u32[]{:S(2)}) collective-permute-start(bf16[512,512]{1,0:T(8,128)(2,1)S(1)} %get-tuple-element.9), channel_id=1, source_target_pairs={{0,1},{1,0},{2,3},{3,2},{4,5},{5,4},{6,7},{7,6},{8,9},{9,8},{10,11... | collective-permute-start | bytes 1572872 | tf_op jit(solution)/shard_map/ppermute | solution.py:32
  262.8 27.3 %collective-permute-start.40 = (bf16[512,512]{1,0:T(8,128)(2,1)S(1)}, bf16[512,512]{1,0:T(8,128)(2,1)S(1)}, u32[]{:S(2)}, u32[]{:S(2)}) collective-permute-start(bf16[512,512]{1,0:T(8,128)(2,1)S(1)} %get-tuple-element.11), channel_id=1, source_target_pairs={{0,1},{1,0},{2,3},{3,2},{4,5},{5,4},{6,7},{7,6},{8,9},{9,8},{10,11... | collective-permute-start | bytes 1572872 | tf_op jit(solution)/shard_map/ppermute | solution.py:32
  264.6 24.2 %collective-permute-start.36 = (bf16[512,512]{1,0:T(8,128)(2,1)S(1)}, bf16[512,512]{1,0:T(8,128)(2,1)S(1)}, u32[]{:S(2)}, u32[]{:S(2)}) collective-permute-start(bf16[512,512]{1,0:T(8,128)(2,1)S(1)} %get-tuple-element.10), channel_id=1, source_target_pairs={{0,1},{1,0},{2,3},{3,2},{4,5},{5,4},{6,7},{7,6},{8,9},{9,8},{10,11... | collective-permute-start | bytes 1572872 | tf_op jit(solution)/shard_map/ppermute | solution.py:32
  265.5 33.3 %collective-permute-start.46 = (bf16[512,512]{1,0:T(8,128)(2,1)S(1)}, bf16[512,512]{1,0:T(8,128)(2,1)S(1)}, u32[]{:S(2)}, u32[]{:S(2)}) collective-permute-start(bf16[512,512]{1,0:T(8,128)(2,1)S(1)} %get-tuple-element.12), channel_id=1, source_target_pairs={{0,1},{1,0},{2,3},{3,2},{4,5},{5,4},{6,7},{7,6},{8,9},{9,8},{10,11... | collective-permute-start | bytes 1572872 | tf_op jit(solution)/shard_map/ppermute | solution.py:32
  301.9 2.7 collective-permute-start.47
  305.5 14.0 %collective-permute-start.48 = (f32[32,4096]{1,0:T(8,128)S(1)}, f32[32,4096]{1,0:T(8,128)S(1)}, u32[]{:S(2)}, u32[]{:S(2)}) collective-permute-start(f32[32,4096]{1,0:T(8,128)S(1)} %dynamic-slice_bitcast_fusion), channel_id=1, source_target_pairs={{0,16},{8,24},{16,0},{24,8},{1,17},{9,25},{17,1},{25,9},{2,18},{10... | collective-permute-start | bytes 1572872 | tf_op jit(solution)/shard_map/ppermute | solution.py:32
  (8 other events, 72.4 us)

commit v2 on v1

--- a/solution.py
+++ b/solution.py
@@ -31,34 +31,117 @@
         ]
         return lax.ppermute(value, self.name, pairs)
 
-    def gather(self, pieces):
+    def cross(self, value):
+        turned = {1: 2, 2: 1}
+        pairs = [
+            (i, i + (turned.get(self.place(i), self.place(i)) - self.place(i)) * self.stride)
+            for i in range(self.total)
+        ]
+        return lax.ppermute(value, self.name, pairs)
+
+    def gather(self, pieces, gates=((), ())):
         n = self.size
-        if n == 1:
-            return [pieces]
-        if n == 2:
-            return [pieces, [self.swap(p, 1) for p in pieces]]
-        hops = {}
-        up = down = pieces
-        for step in range(1, n):
-            up = [self.shift(p, 1) for p in up]
-            down = [self.shift(p, -1) for p in down]
-            hops[step], hops[-step] = up, down
-        slots = [pieces]
-        for m in range(1, n):
-            moves = sorted({i - (i ^ m) for i in range(n)})
-            slot = []
-            for p in range(len(pieces)):
-                value = hops[moves[0]][p]
-                for move in moves[1:]:
-                    value = jnp.where(self.at - (self.at ^ m) == move, hops[move][p], value)
-                slot.append(value)
-            slots.append(slot)
+        if n != 4:
+            return [pieces] + [[self.swap(p, m) for p in pieces] for m in range(1, n)]
+        inner = (self.at == 1) | (self.at == 2)
+        first = after(pieces, gates[0])
+        middle = after(pieces, gates[1])
+        slots = [pieces, [], [], []]
+        for p, q in zip(first, middle):
+            near = self.swap(p, 1)
+            far = self.cross(q)
+            far2 = self.cross(near)
+            out2 = self.swap(far, 1)
+            out3 = self.swap(far2, 1)
+            slots[1].append(near)
+            slots[2].append(jnp.where(inner, far2, out2))
+            slots[3].append(jnp.where(inner, far, out3))
         return slots
 
 
 def after(values, earlier):
+    if not earlier:
+        return list(values)
     out = lax.optimization_barrier((tuple(values), tuple(earlier)))
     return list(out[0])
+
+
+def tick(*groups):
+    sizes = [len(g) for g in groups]
+    flat = lax.optimization_barrier(tuple(v for g in groups for v in g))
+    out, at = [], 0
+    for size in sizes:
+        out.append(list(flat[at : at + size]))
+        at += size
+    return out
+
+
+def woven(z, x, halves, downs, kv, dot, seq_core, seq_y):
+    E, O, X = (lambda v: z.swap(v, 1)), z.cross, (lambda v: x.swap(v, 1))
+    inner = (z.at == 1) | (z.at == 2)
+    choose = lambda a, b: jnp.where(inner, a, b)
+    (ha, hb), (da, db), (k, v) = halves, downs, kv
+
+    e1a, o1a, xda = E(ha), O(ha), X(da)
+    e1b, o1b, xdb = E(hb), O(hb), X(db)
+    e2a, o2a = E(o1a), O(e1a)
+    e2b, o2b = E(o1b), O(e1b)
+    (e2a, o2a, xda), (k, v) = tick((e2a, o2a, xda), (k, v))
+    e3a = E(o2a)
+    o1k = O(k)
+    wa = jnp.concatenate([da, xda], axis=1)
+    c0, c1 = dot(ha, wa), dot(e1a, wa)
+    s2a, s2b = choose(o2a, e2a), None
+    (e2b, o2b, xdb), (k, v), (c0, c1) = tick((e2b, o2b, xdb), (k, v), (c0, c1))
+    e3b = E(o2b)
+    o1v = O(v)
+    xk0 = X(k)
+    s2b = choose(o2b, e2b)
+    wb = jnp.concatenate([db, xdb], axis=1)
+    c0 = c0 + dot(hb, wb)
+    c1 = c1 + dot(e1b, wb)
+    r1 = seq_core(c1)
+    r0 = seq_core(c0)
+    (e3a,), (k, v), r1 = tick((e3a,), (k, v), r1)
+    e1k = E(k)
+    xv0 = X(v)
+    c2 = dot(s2a, wa) + dot(s2b, wb)
+    r2 = seq_core(c2)
+    t1 = seq_y(*r1)
+    (e3b, o1k, o1v), (v,), r2, t1 = tick((e3b, o1k, o1v), (v,), r2, t1)
+    e1v = E(v)
+    c3 = dot(choose(o1a, e3a), wa) + dot(choose(o1b, e3b), wb)
+    r3 = seq_core(c3)
+    q1 = z.swap(sum(t1), 1)
+    t2 = seq_y(*r2)
+    (e1k, xk0), r3, t2 = tick((e1k, xk0), r3, t2)
+    e2k, o2k = E(o1k), O(e1k)
+    xk1 = X(e1k)
+    t3 = seq_y(*r3)
+    q2 = z.swap(sum(t2), 2)
+    (e1v, xv0, q1), t3, r0 = tick((e1v, xv0, q1), t3, r0)
+    q3 = z.swap(sum(t3), 3)
+    e2v, o2v = E(o1v), O(e1v)
+    xv1 = X(e1v)
+    t0 = seq_y(*r0)
+    (e2k, o2k, xk1, q2), t0 = tick((e2k, o2k, xk1, q2), t0)
+    e3k = E(o2k)
+    k2 = choose(o2k, e2k)
+    xk2 = X(k2)
+    (e2v, o2v, xv1, q3), = tick((e2v, o2v, xv1, q3))
+    e3v = E(o2v)
+    v2 = choose(o2v, e2v)
+    xv2 = X(v2)
+    k3 = choose(o1k, e3k)
+    v3 = choose(o1v, e3v)
+    xk3, xv3 = X(k3), X(v3)
+    kv_slots = [
+        [[k, v], [xk0, xv0]],
+        [[e1k, e1v], [xk1, xv1]],
+        [[k2, v2], [xk2, xv2]],
+        [[k3, v3], [xk3, xv3]],
+    ]
+    return kv_slots, [sum(t0), q1, q2, q3]
 
 
 def on_device(
@@ -81,27 +164,40 @@
     width = block * dp
     dot = lambda a, b: jnp.dot(a, b, preferred_element_type=jnp.float32)
 
-    halves = [hidden[: enc_total // 2], hidden[enc_total // 2 :]]
-    hidden_slots = z.gather(halves)
-    down_slots = [s[0] for s in x.gather([down_proj])]
-
-    keys_local, values_local = kv_proj[:, 0], kv_proj[:, 1]
-    kv_own = after([keys_local, values_local], hidden_slots[-1])
-    kv_z = z.gather(kv_own)
-    kv_slots = [x.gather(slot) for slot in kv_z]
-
-    summed = []
-    for m in range(nz):
-        a = jnp.concatenate(hidden_slots[m], axis=0).reshape(ny, nc, rows, depth)
-        pick = lambda i: lax.dynamic_index_in_dim(a, i, 1, keepdims=False).reshape(ny * rows, depth)
-        product = lambda i: jnp.concatenate([dot(pick(i), w) for w in down_slots], axis=1)
-        part = product(c.at) + c.swap(product(1 - c.at), 1)
-        part = part.reshape(ny, rows, nx * block)
+    half = depth // 2
+    halves = [hidden[:, :half], hidden[:, half:]]
+    downs = [down_proj[:half], down_proj[half:]]
+    kv_local = [kv_proj[:, 0], kv_proj[:, 1]]
+
+    def seq_core(part):
+        part = part.reshape(ny, nc, rows, nx * block)
+        pick = lambda i: lax.dynamic_index_in_dim(part, i, 1, keepdims=False)
+        return pick(c.at), c.swap(pick(1 - c.at), 1)
+
+    def seq_y(mine, theirs):
+        part = mine + theirs
         total = lax.dynamic_index_in_dim(part, y.at, 0, keepdims=False)
-        for k in range(1, ny):
-            other = lax.dynamic_index_in_dim(part, y.at ^ k, 0, keepdims=False)
-            total = total + y.swap(other, k)
-        summed.append(total if m == 0 else z.swap(total, m))
+        others = [
+            y.swap(lax.dynamic_index_in_dim(part, y.at ^ k, 0, keepdims=False), k)
+            for k in range(1, ny)
+        ]
+        return [total] + others
+
+    def seq_sum(part):
+        return sum(seq_y(*seq_core(part))[0:])
+
+    if (nz, nx) == (4, 2):
+        kv_slots, summed = woven(z, x, halves, downs, kv_local, dot, seq_core, seq_y)
+    else:
+        hidden_slots = z.gather(halves)
+        down_slots = x.gather(downs)
+        kv_slots = [x.gather(slot) for slot in z.gather(kv_local)]
+        weights = [jnp.concatenate([s[p] for s in down_slots], axis=1) for p in range(2)]
+        summed = []
+        for m in range(nz):
+            part = dot(hidden_slots[m][0], weights[0]) + dot(hidden_slots[m][1], weights[1])
+            total = seq_sum(part)
+            summed.append(total if m == 0 else z.swap(total, m))
 
     stream = encoder_stream[0]
     gain = final_gain.astype(jnp.float32)

time: 322 us -> 239 us (0.74); the launches traced: 320 us -> 234 us
  waiting for transfers between devices: 182 us -> 106 us
  starting transfers between devices: 87.8 us -> 70.6 us
    ppermute x24 -> x8, starting transfers between devices: 66 us -> 19.5 us  [cross(): return lax.ppermute(value, self.name, pairs)]
    ppermute x24 -> x8, waiting for transfers between devices: 44.9 us -> 0.02 us  [cross(): return lax.ppermute(value, self.name, pairs)]
    ppermute x25 -> x38, waiting for transfers between devices: 137 us -> 106 us  [swap(): return lax.ppermute(value, self.name, pairs)]
    ppermute x25 -> x38, starting transfers between devices: 21.8 us -> 51.1 us  [swap(): return lax.ppermute(value, self.name, pairs)]
    add x8 -> x10, other arithmetic: 0.39 us -> 6.94 us  [the longest x1 1.76 us: woven(): q2 = z.swap(sum(t2), 2)]
    select_n x8 -> x4, other arithmetic: 5.3 us -> 1.27 us  [woven(): choose = lambda a, b: jnp.where(inner, a, b)]
    slice x2 -> x3, local copies, waits for them, and re-layouts: 6.85 us -> 4.02 us  [the longest x1 1.48 us: on_device(): kv_local = [kv_proj[:, 0], kv_proj[:, 1]]]
    dot_general x36 -> x28, matrix products: 26.9 us -> 28.4 us  [on_device(): dot = lambda a, b: jnp.dot(a, b, preferred_element_type=jnp.float32)]
  transfers between devices with their start and end apart: 49 -> 46, of which waited for: 23 -> 16; matrix products, arithmetic and copies ran while one was open for 13% -> 20% of each run, Pallas kernels for 0% -> 0%
where the time goes in v2:
time: 239 us; the launch traced here: 234 us
  waiting for transfers between devices  106 us (44%)
  starting transfers between devices  70.6 us (30%)
  matrix products  28.9 us (12%)
  local copies, waits for them, and re-layouts  14.6 us (6%)
  other arithmetic  11.9 us (5%)
    ppermute x38, waiting for transfers between devices, swap(): return lax.ppermute(value, self.name, pairs)  106 us
    ppermute x38, starting transfers between devices, swap(): return lax.ppermute(value, self.name, pairs)  51.1 us
    dot_general x28, matrix products, on_device(): dot = lambda a, b: jnp.dot(a, b, preferred_element_type=jnp.float32)  28.4 us
    ppermute x8, starting transfers between devices, cross(): return lax.ppermute(value, self.name, pairs)  19.5 us
  transfers between devices with their start and end apart: 46, of which 16 were waited for; matrix products, arithmetic and copies ran while one was open for 20% of the time, Pallas kernels for 0%

profile of v2, /device:TPU:0, one launch (start us, length us, event | category | flops | bytes accessed | tf_op | source)
XLA Modules:
  0.0 234.1 jit_solution(1415071907803032314)
XLA Ops:
  1.4 1.5 collective-permute-start.5
  2.9 5.1 %collective-permute-start.7 = (bf16[256,1024]{1,0:T(8,128)(2,1)S(1)}, bf16[256,1024]{1,0:T(8,128)(2,1)}, u32[]{:S(2)}, u32[]{:S(2)}) collective-permute-start(bf16[256,1024]{1,0:T(8,128)(2,1)S(1)} %get-tuple-element.113), channel_id=1, source_target_pairs={{0,2},{1,3},{2,0},{3,1},{4,6},{5,7},{6,4},{7,5},{8,10},{9,11},{10,... | collective-permute-start | bytes 1572872 | tf_op jit(solution)/shard_map/ppermute | solution.py:32
  8.0 1.6 collective-permute-start
  10.7 1.5 collective-permute-start.9
  12.2 1.5 collective-permute-start.2
  14.4 6.5 %collective-permute-done.7 = bf16[256,1024]{1,0:T(8,128)(2,1)} collective-permute-done((bf16[256,1024]{1,0:T(8,128)(2,1)S(1)}, bf16[256,1024]{1,0:T(8,128)(2,1)}, u32[]{:S(2)}, u32[]{:S(2)}) %collective-permute-start.7) | collective-permute-done | bytes 524320 | tf_op jit(solution)/shard_map/ppermute | solution.py:32
  20.9 2.1 collective-permute-start.6
  23.0 1.7 collective-permute-start.8
  26.5 5.7 %collective-permute-done.2 = bf16[256,1024]{1,0:T(8,128)(2,1)} collective-permute-done((bf16[256,1024]{1,0:T(8,128)(2,1)S(1)}, bf16[256,1024]{1,0:T(8,128)(2,1)}, u32[]{:S(2)}, u32[]{:S(2)}) %collective-permute-start.2) | collective-permute-done | bytes 524320 | tf_op jit(solution)/shard_map/ppermute | solution.py:32
  32.1 4.6 %collective-permute-start.1 = (bf16[256,1024]{1,0:T(8,128)(2,1)}, bf16[256,1024]{1,0:T(8,128)(2,1)S(1)}, u32[]{:S(2)}, u32[]{:S(2)}) collective-permute-start(bf16[256,1024]{1,0:T(8,128)(2,1)} %collective-permute-done), channel_id=1, source_target_pairs={{0,2},{1,3},{2,0},{3,1},{4,6},{5,7},{6,4},{7,5},{8,10},{9,11},{10,... | collective-permute-start | bytes 1572872 | tf_op jit(solution)/shard_map/ppermute | solution.py:32
  36.9 5.4 %collective-permute-start.3 = (bf16[256,1024]{1,0:T(8,128)(2,1)}, bf16[256,1024]{1,0:T(8,128)(2,1)}, u32[]{:S(2)}, u32[]{:S(2)}) collective-permute-start(bf16[256,1024]{1,0:T(8,128)(2,1)} %collective-permute-done.2), channel_id=1, source_target_pairs={{0,0},{1,1},{2,4},{3,5},{4,2},{5,3},{6,6},{7,7},{8,8},{9,9},{10,12... | collective-permute-start | bytes 1572872 | tf_op jit(solution)/shard_map/ppermute | solution.py:40
  43.3 1.6 collective-permute-start.11
  44.9 2.1 convolution_bitcast_fusion.2
  47.0 3.0 %convolution_bitcast_fusion.3 = f32[256,1024]{0,1:T(8,128)} fusion(bf16[256,2048]{1,0:T(8,128)(2,1)S(1)} %bitcast.119, bf16[1024,512]{1,0:T(8,128)(2,1)} %collective-permute-done.9, bf16[1024,512]{1,0:T(8,128)(2,1)S(1)} %copy-done.9), kind=kOutput, calls=%fused_computation.7 | convolution fusion | flops 541065216 | bytes 3670016 | tf_op jit(solution)/shard_map/dot_general | solution.py:165
  50.0 7.5 %collective-permute-done.4 = bf16[1024,512]{1,0:T(8,128)(2,1)S(1)} collective-permute-done((bf16[1024,512]{1,0:T(8,128)(2,1)}, bf16[1024,512]{1,0:T(8,128)(2,1)S(1)}, u32[]{:S(2)}, u32[]{:S(2)}) %collective-permute-start.4) | collective-permute-done | bytes 1048608 | tf_op jit(solution)/shard_map/ppermute | solution.py:32
  58.5 2.1 convolution_bitcast_fusion.1
  62.1 1.5 collective-permute-start.13
  64.1 2.0 fusion.20
  66.1 2.0 convolution_add_fusion.2
  69.1 7.9 %collective-permute-done.13 = bf16[256,1024]{1,0:T(8,128)(2,1)S(1)} collective-permute-done((bf16[256,1024]{1,0:T(8,128)(2,1)S(1)}, bf16[256,1024]{1,0:T(8,128)(2,1)S(1)}, u32[]{:S(2)}, u32[]{:S(2)}) %collective-permute-start.13) | collective-permute-done | bytes 524320 | tf_op jit(solution)/shard_map/ppermute | solution.py:32
  77.8 1.5 collective-permute-start.16
  80.3 1.5 collective-permute-start.19
  81.8 5.2 %collective-permute-done.10 = bf16[256,1024]{1,0:T(8,128)(2,1)} collective-permute-done((bf16[256,1024]{1,0:T(8,128)(2,1)}, bf16[256,1024]{1,0:T(8,128)(2,1)}, u32[]{:S(2)}, u32[]{:S(2)}) %collective-permute-start.10) | collective-permute-done | bytes 524320 | tf_op jit(solution)/shard_map/ppermute | solution.py:32
  87.0 1.5 collective-permute-start.18
  89.5 1.5 collective-permute-start.21
  91.0 2.1 fusion.17
  93.2 2.0 convolution_add_fusion.1
  96.7 2.0 convolution_bitcast_fusion
  100.2 1.5 collective-permute-start.26
  102.5 1.7 add.299
  109.3 12.9 %collective-permute-done.27 = f32[64,1024]{1,0:T(8,128)S(1)} collective-permute-done((f32[64,1024]{1,0:T(8,128)}, f32[64,1024]{1,0:T(8,128)S(1)}, u32[]{:S(2)}, u32[]{:S(2)}) %collective-permute-start.27) | collective-permute-done | bytes 262176 | tf_op jit(solution)/shard_map/ppermute | solution.py:32
  122.2 5.4 %collective-permute-start.22 = (bf16[512,512]{1,0:T(8,128)(2,1)}, bf16[512,512]{1,0:T(8,128)(2,1)}, u32[]{:S(2)}, u32[]{:S(2)}) collective-permute-start(bf16[512,512]{1,0:T(8,128)(2,1)} %collective-permute-done.18), channel_id=1, source_target_pairs={{0,0},{1,1},{2,4},{3,5},{4,2},{5,3},{6,6},{7,7},{8,8},{9,9},{10,12... | collective-permute-start | bytes 1572872 | tf_op jit(solution)/shard_map/ppermute | solution.py:40
  128.4 1.8 add.298
  132.8 2.1 collective-permute-start.31
  134.9 13.3 %collective-permute-done.24 = f32[64,1024]{1,0:T(8,128)} collective-permute-done((f32[64,1024]{1,0:T(8,128)}, f32[64,1024]{1,0:T(8,128)}, u32[]{:S(2)}, u32[]{:S(2)}) %collective-permute-start.24) | collective-permute-done | bytes 262176 | tf_op jit(solution)/shard_map/ppermute | solution.py:32
  148.2 1.7 collective-permute-start.32
  150.4 1.9 collective-permute-start.34
  155.4 6.1 %collective-permute-done.34 = f32[64,1024]{1,0:T(8,128)S(1)} collective-permute-done((f32[64,1024]{1,0:T(8,128)S(1)}, f32[64,1024]{1,0:T(8,128)S(1)}, u32[]{:S(2)}, u32[]{:S(2)}) %collective-permute-start.34) | collective-permute-done | bytes 262176 | tf_op jit(solution)/shard_map/ppermute | solution.py:32
  163.6 1.6 collective-permute-start.38
  165.1 9.6 %collective-permute-start.42 = (bf16[512,512]{1,0:T(8,128)(2,1)S(1)}, bf16[512,512]{1,0:T(8,128)(2,1)S(1)}, u32[]{:S(2)}, u32[]{:S(2)}) collective-permute-start(bf16[512,512]{1,0:T(8,128)(2,1)S(1)} %collective-permute-done.32), channel_id=1, source_target_pairs={{0,2},{1,3},{2,0},{3,1},{4,6},{5,7},{6,4},{7,5},{8,10},{9,11},{10,... | collective-permute-start | bytes 1572872 | tf_op jit(solution)/shard_map/ppermute | solution.py:32
  174.8 1.6 collective-permute-start.41
  176.4 10.9 %collective-permute-done.42 = bf16[512,512]{1,0:T(8,128)(2,1)S(1)} collective-permute-done((bf16[512,512]{1,0:T(8,128)(2,1)S(1)}, bf16[512,512]{1,0:T(8,128)(2,1)S(1)}, u32[]{:S(2)}, u32[]{:S(2)}) %collective-permute-start.42) | collective-permute-done | bytes 524320 | tf_op jit(solution)/shard_map/ppermute | solution.py:32
  187.3 1.5 collective-permute-start.40
  196.9 5.2 %collective-permute-done.40 = bf16[512,512]{1,0:T(8,128)(2,1)S(1)} collective-permute-done((bf16[512,512]{1,0:T(8,128)(2,1)S(1)}, bf16[512,512]{1,0:T(8,128)(2,1)S(1)}, u32[]{:S(2)}, u32[]{:S(2)}) %collective-permute-start.40) | collective-permute-done | bytes 524320 | tf_op jit(solution)/shard_map/ppermute | solution.py:32
  204.4 7.9 %collective-permute-done.43 = bf16[512,512]{1,0:T(8,128)(2,1)S(1)} collective-permute-done((bf16[512,512]{1,0:T(8,128)(2,1)S(1)}, bf16[512,512]{1,0:T(8,128)(2,1)S(1)}, u32[]{:S(2)}, u32[]{:S(2)}) %collective-permute-start.43) | collective-permute-done | bytes 524320 | tf_op jit(solution)/shard_map/ppermute | solution.py:32
  215.7 2.6 %collective-permute-done.44 = f32[64,4096]{1,0:T(8,128)S(1)} collective-permute-done((f32[64,4096]{1,0:T(8,128)S(1)}, f32[64,4096]{1,0:T(8,128)S(1)}, u32[]{:S(2)}, u32[]{:S(2)}) %collective-permute-start.44) | collective-permute-done | bytes 1048608 | tf_op jit(solution)/shard_map/ppermute | solution.py:32
  219.2 1.6 collective-permute-start.45
  220.8 12.4 %collective-permute-done.45 = f32[32,4096]{1,0:T(8,128)S(1)} collective-permute-done((f32[32,4096]{1,0:T(8,128)S(1)}, f32[32,4096]{1,0:T(8,128)S(1)}, u32[]{:S(2)}, u32[]{:S(2)}) %collective-permute-start.45) | collective-permute-done | bytes 524320 | tf_op jit(solution)/shard_map/ppermute | solution.py:32
  (198 shorter events, 44.7 us)
Async XLA Ops:
  1.4 12.3 %collective-permute-start.5 = (bf16[256,1024]{1,0:T(8,128)(2,1)S(1)}, bf16[256,1024]{1,0:T(8,128)(2,1)}, u32[]{:S(2)}, u32[]{:S(2)}) collective-permute-start(bf16[256,1024]{1,0:T(8,128)(2,1)S(1)} %get-tuple-element.113), channel_id=1, source_target_pairs={{0,0},{1,1},{2,4},{3,5},{4,2},{5,3},{6,6},{7,7},{8,8},{9,9},{10,12... | collective-permute-start | bytes 1572872 | tf_op jit(solution)/shard_map/ppermute | solution.py:40
  2.9 18.0 %collective-permute-start.7 = (bf16[256,1024]{1,0:T(8,128)(2,1)S(1)}, bf16[256,1024]{1,0:T(8,128)(2,1)}, u32[]{:S(2)}, u32[]{:S(2)}) collective-permute-start(bf16[256,1024]{1,0:T(8,128)(2,1)S(1)} %get-tuple-element.113), channel_id=1, source_target_pairs={{0,2},{1,3},{2,0},{3,1},{4,6},{5,7},{6,4},{7,5},{8,10},{9,11},{10,... | collective-permute-start | bytes 1572872 | tf_op jit(solution)/shard_map/ppermute | solution.py:32
  8.0 15.0 %collective-permute-start = (bf16[256,1024]{1,0:T(8,128)(2,1)S(1)}, bf16[256,1024]{1,0:T(8,128)(2,1)}, u32[]{:S(2)}, u32[]{:S(2)}) collective-permute-start(bf16[256,1024]{1,0:T(8,128)(2,1)S(1)} %get-tuple-element.114), channel_id=1, source_target_pairs={{0,0},{1,1},{2,4},{3,5},{4,2},{5,3},{6,6},{7,7},{8,8},{9,9},{10,12... | collective-permute-start | bytes 1572872 | tf_op jit(solution)/shard_map/ppermute | solution.py:40
  10.7 26.2 %collective-permute-start.9 = (bf16[1024,512]{1,0:T(8,128)(2,1)S(1)}, bf16[1024,512]{1,0:T(8,128)(2,1)}, u32[]{:S(2)}, u32[]{:S(2)}) collective-permute-start(bf16[1024,512]{1,0:T(8,128)(2,1)S(1)} %get-tuple-element.101), channel_id=1, source_target_pairs={{0,1},{1,0},{2,3},{3,2},{4,5},{5,4},{6,7},{7,6},{8,9},{9,8},{10,11... | collective-permute-start | bytes 3145736 | tf_op jit(solution)/shard_map/ppermute | solution.py:32
  12.2 19.9 %collective-permute-start.2 = (bf16[256,1024]{1,0:T(8,128)(2,1)S(1)}, bf16[256,1024]{1,0:T(8,128)(2,1)}, u32[]{:S(2)}, u32[]{:S(2)}) collective-permute-start(bf16[256,1024]{1,0:T(8,128)(2,1)S(1)} %get-tuple-element.114), channel_id=1, source_target_pairs={{0,2},{1,3},{2,0},{3,1},{4,6},{5,7},{6,4},{7,5},{8,10},{9,11},{10,... | collective-permute-start | bytes 1572872 | tf_op jit(solution)/shard_map/ppermute | solution.py:32
  13.8 43.8 %collective-permute-start.4 = (bf16[1024,512]{1,0:T(8,128)(2,1)}, bf16[1024,512]{1,0:T(8,128)(2,1)S(1)}, u32[]{:S(2)}, u32[]{:S(2)}) collective-permute-start(bf16[1024,512]{1,0:T(8,128)(2,1)} %get-tuple-element.102), channel_id=1, source_target_pairs={{0,1},{1,0},{2,3},{3,2},{4,5},{5,4},{6,7},{7,6},{8,9},{9,8},{10,11... | collective-permute-start | bytes 3145736 | tf_op jit(solution)/shard_map/ppermute | solution.py:32
  20.9 22.4 %collective-permute-start.6 = (bf16[256,1024]{1,0:T(8,128)(2,1)}, bf16[256,1024]{1,0:T(8,128)(2,1)S(1)}, u32[]{:S(2)}, u32[]{:S(2)}) collective-permute-start(bf16[256,1024]{1,0:T(8,128)(2,1)} %collective-permute-done.5), channel_id=1, source_target_pairs={{0,2},{1,3},{2,0},{3,1},{4,6},{5,7},{6,4},{7,5},{8,10},{9,11},{10,... | collective-permute-start | bytes 1572872 | tf_op jit(solution)/shard_map/ppermute | solution.py:32
  23.0 20.3 %collective-permute-start.8 = (bf16[256,1024]{1,0:T(8,128)(2,1)}, bf16[256,1024]{1,0:T(8,128)(2,1)S(1)}, u32[]{:S(2)}, u32[]{:S(2)}) collective-permute-start(bf16[256,1024]{1,0:T(8,128)(2,1)} %collective-permute-done.7), channel_id=1, source_target_pairs={{0,0},{1,1},{2,4},{3,5},{4,2},{5,3},{6,6},{7,7},{8,8},{9,9},{10,12... | collective-permute-start | bytes 1572872 | tf_op jit(solution)/shard_map/ppermute | solution.py:40
  32.1 25.4 %collective-permute-start.1 = (bf16[256,1024]{1,0:T(8,128)(2,1)}, bf16[256,1024]{1,0:T(8,128)(2,1)S(1)}, u32[]{:S(2)}, u32[]{:S(2)}) collective-permute-start(bf16[256,1024]{1,0:T(8,128)(2,1)} %collective-permute-done), channel_id=1, source_target_pairs={{0,2},{1,3},{2,0},{3,1},{4,6},{5,7},{6,4},{7,5},{8,10},{9,11},{10,... | collective-permute-start | bytes 1572872 | tf_op jit(solution)/shard_map/ppermute | solution.py:32
  36.9 20.6 %collective-permute-start.3 = (bf16[256,1024]{1,0:T(8,128)(2,1)}, bf16[256,1024]{1,0:T(8,128)(2,1)}, u32[]{:S(2)}, u32[]{:S(2)}) collective-permute-start(bf16[256,1024]{1,0:T(8,128)(2,1)} %collective-permute-done.2), channel_id=1, source_target_pairs={{0,0},{1,1},{2,4},{3,5},{4,2},{5,3},{6,6},{7,7},{8,8},{9,9},{10,12... | collective-permute-start | bytes 1572872 | tf_op jit(solution)/shard_map/ppermute | solution.py:40
  43.3 45.2 %collective-permute-start.11 = (bf16[512,512]{1,0:T(8,128)(2,1)S(1)}, bf16[512,512]{1,0:T(8,128)(2,1)}, u32[]{:S(2)}, u32[]{:S(2)}) collective-permute-start(bf16[512,512]{1,0:T(8,128)(2,1)S(1)} %get-tuple-element.68), channel_id=1, source_target_pairs={{0,0},{1,1},{2,4},{3,5},{4,2},{5,3},{6,6},{7,7},{8,8},{9,9},{10,12... | collective-permute-start | bytes 1572872 | tf_op jit(solution)/shard_map/ppermute | solution.py:40
  61.2 7.1 %collective-permute-start.14 = (f32[2,64,1024]{2,1,0:T(8,128)S(1)}, f32[2,64,1024]{2,1,0:T(8,128)S(1)}, u32[]{:S(2)}, u32[]{:S(2)}) collective-permute-start(f32[2,64,1024]{2,1,0:T(8,128)S(1)} %get-tuple-element.109), channel_id=1, source_target_pairs={{0,8},{8,0},{16,24},{24,16},{1,9},{9,1},{17,25},{25,17},{2,10},{10... | collective-permute-start | bytes 1572872 | tf_op jit(solution)/shard_map/ppermute | solution.py:32
  62.1 14.8 %collective-permute-start.13 = (bf16[256,1024]{1,0:T(8,128)(2,1)S(1)}, bf16[256,1024]{1,0:T(8,128)(2,1)S(1)}, u32[]{:S(2)}, u32[]{:S(2)}) collective-permute-start(bf16[256,1024]{1,0:T(8,128)(2,1)S(1)} %copy-done.26), channel_id=1, source_target_pairs={{0,2},{1,3},{2,0},{3,1},{4,6},{5,7},{6,4},{7,5},{8,10},{9,11},{10,... | collective-permute-start | bytes 1572872 | tf_op jit(solution)/shard_map/ppermute | solution.py:32
  63.6 23.3 %collective-permute-start.10 = (bf16[256,1024]{1,0:T(8,128)(2,1)}, bf16[256,1024]{1,0:T(8,128)(2,1)}, u32[]{:S(2)}, u32[]{:S(2)}) collective-permute-start(bf16[256,1024]{1,0:T(8,128)(2,1)} %collective-permute-done.3), channel_id=1, source_target_pairs={{0,2},{1,3},{2,0},{3,1},{4,6},{5,7},{6,4},{7,5},{8,10},{9,11},{10,... | collective-permute-start | bytes 1572872 | tf_op jit(solution)/shard_map/ppermute | solution.py:32
  68.2 12.0 %collective-permute-start.15 = (f32[2,64,1024]{2,1,0:T(8,128)S(1)}, f32[2,64,1024]{2,1,0:T(8,128)S(1)}, u32[]{:S(2)}, u32[]{:S(2)}) collective-permute-start(f32[2,64,1024]{2,1,0:T(8,128)S(1)} %get-tuple-element.107), channel_id=1, source_target_pairs={{0,8},{8,0},{16,24},{24,16},{1,9},{9,1},{17,25},{25,17},{2,10},{10... | collective-permute-start | bytes 1572872 | tf_op jit(solution)/shard_map/ppermute | solution.py:32
  68.3 20.2 %collective-permute-start.12 = (bf16[512,512]{1,0:T(8,128)(2,1)S(1)}, bf16[512,512]{1,0:T(8,128)(2,1)S(1)}, u32[]{:S(2)}, u32[]{:S(2)}) collective-permute-start(bf16[512,512]{1,0:T(8,128)(2,1)S(1)} %get-tuple-element.76), channel_id=1, source_target_pairs={{0,0},{1,1},{2,4},{3,5},{4,2},{5,3},{6,6},{7,7},{8,8},{9,9},{10,12... | collective-permute-start | bytes 1572872 | tf_op jit(solution)/shard_map/ppermute | solution.py:40
  77.8 10.7 %collective-permute-start.16 = (f32[64,1024]{1,0:T(8,128)}, f32[64,1024]{1,0:T(8,128)}, u32[]{:S(2)}, u32[]{:S(2)}) collective-permute-start(f32[64,1024]{1,0:T(8,128)} %get-tuple-element.121), channel_id=1, source_target_pairs={{0,16},{8,24},{16,0},{24,8},{1,17},{9,25},{17,1},{25,9},{2,18},{10... | collective-permute-start | bytes 786440 | tf_op jit(solution)/shard_map/ppermute | solution.py:32
  80.3 19.9 %collective-permute-start.19 = (bf16[512,512]{1,0:T(8,128)(2,1)S(1)}, bf16[512,512]{1,0:T(8,128)(2,1)}, u32[]{:S(2)}, u32[]{:S(2)}) collective-permute-start(bf16[512,512]{1,0:T(8,128)(2,1)S(1)} %get-tuple-element.68), channel_id=1, source_target_pairs={{0,1},{1,0},{2,3},{3,2},{4,5},{5,4},{6,7},{7,6},{8,9},{9,8},{10,11... | collective-permute-start | bytes 1572872 | tf_op jit(solution)/shard_map/ppermute | solution.py:32
  87.0 17.2 %collective-permute-start.18 = (bf16[512,512]{1,0:T(8,128)(2,1)S(1)}, bf16[512,512]{1,0:T(8,128)(2,1)}, u32[]{:S(2)}, u32[]{:S(2)}) collective-permute-start(bf16[512,512]{1,0:T(8,128)(2,1)S(1)} %get-tuple-element.68), channel_id=1, source_target_pairs={{0,2},{1,3},{2,0},{3,1},{4,6},{5,7},{6,4},{7,5},{8,10},{9,11},{10,... | collective-permute-start | bytes 1572872 | tf_op jit(solution)/shard_map/ppermute | solution.py:32
  89.5 12.3 %collective-permute-start.21 = (f32[64,1024]{1,0:T(8,128)}, f32[64,1024]{1,0:T(8,128)}, u32[]{:S(2)}, u32[]{:S(2)}) collective-permute-start(f32[64,1024]{1,0:T(8,128)} %get-tuple-element.119), channel_id=1, source_target_pairs={{0,16},{8,24},{16,0},{24,8},{1,17},{9,25},{17,1},{25,9},{2,18},{10... | collective-permute-start | bytes 786440 | tf_op jit(solution)/shard_map/ppermute | solution.py:32
  96.2 9.3 %collective-permute-start.20 = (f32[2,64,1024]{2,1,0:T(8,128)}, f32[2,64,1024]{2,1,0:T(8,128)}, u32[]{:S(2)}, u32[]{:S(2)}) collective-permute-start(f32[2,64,1024]{2,1,0:T(8,128)} %get-tuple-element.105), channel_id=1, source_target_pairs={{0,8},{8,0},{16,24},{24,16},{1,9},{9,1},{17,25},{25,17},{2,10},{10... | collective-permute-start | bytes 1572872 | tf_op jit(solution)/shard_map/ppermute | solution.py:32
  100.1 28.2 %copy-start.5 = (f32[64,1024]{1,0:T(8,128)S(1)}, f32[64,1024]{1,0:T(8,128)}, u32[]{:S(2)}) copy-start(f32[64,1024]{1,0:T(8,128)} %get-tuple-element.74) | copy-start | bytes 786436
  100.2 8.5 %collective-permute-start.29 = (f32[2,64,1024]{2,1,0:T(8,128)}, f32[2,64,1024]{2,1,0:T(8,128)S(1)}, u32[]{:S(2)}, u32[]{:S(2)}) collective-permute-start(f32[2,64,1024]{2,1,0:T(8,128)} %get-tuple-element.103), channel_id=1, source_target_pairs={{0,8},{8,0},{16,24},{24,16},{1,9},{9,1},{17,25},{25,17},{2,10},{10... | collective-permute-start | bytes 1572872 | tf_op jit(solution)/shard_map/ppermute | solution.py:32
  100.2 27.4 %collective-permute-start.26 = (bf16[512,512]{1,0:T(8,128)(2,1)S(1)}, bf16[512,512]{1,0:T(8,128)(2,1)S(1)}, u32[]{:S(2)}, u32[]{:S(2)}) collective-permute-start(bf16[512,512]{1,0:T(8,128)(2,1)S(1)} %get-tuple-element.76), channel_id=1, source_target_pairs={{0,1},{1,0},{2,3},{3,2},{4,5},{5,4},{6,7},{7,6},{8,9},{9,8},{10,11... | collective-permute-start | bytes 1572872 | tf_op jit(solution)/shard_map/ppermute | solution.py:32
  101.8 28.4 %collective-permute-start.25 = (bf16[512,512]{1,0:T(8,128)(2,1)S(1)}, bf16[512,512]{1,0:T(8,128)(2,1)}, u32[]{:S(2)}, u32[]{:S(2)}) collective-permute-start(bf16[512,512]{1,0:T(8,128)(2,1)S(1)} %get-tuple-element.76), channel_id=1, source_target_pairs={{0,2},{1,3},{2,0},{3,1},{4,6},{5,7},{6,4},{7,5},{8,10},{9,11},{10,... | collective-permute-start | bytes 1572872 | tf_op jit(solution)/shard_map/ppermute | solution.py:32
  104.2 18.0 %collective-permute-start.27 = (f32[64,1024]{1,0:T(8,128)}, f32[64,1024]{1,0:T(8,128)S(1)}, u32[]{:S(2)}, u32[]{:S(2)}) collective-permute-start(f32[64,1024]{1,0:T(8,128)} %add.299), channel_id=1, source_target_pairs={{0,2},{1,3},{2,0},{3,1},{4,6},{5,7},{6,4},{7,5},{8,10},{9,11},{10,... | collective-permute-start | bytes 786440 | tf_op jit(solution)/shard_map/ppermute | solution.py:32
  107.4 22.8 %collective-permute-start.28 = (f32[64,1024]{1,0:T(8,128)}, f32[64,1024]{1,0:T(8,128)}, u32[]{:S(2)}, u32[]{:S(2)}) collective-permute-start(f32[64,1024]{1,0:T(8,128)} %get-tuple-element.117), channel_id=1, source_target_pairs={{0,16},{8,24},{16,0},{24,8},{1,17},{9,25},{17,1},{25,9},{2,18},{10... | collective-permute-start | bytes 786440 | tf_op jit(solution)/shard_map/ppermute | solution.py:32
  108.7 24.1 %collective-permute-start.17 = (bf16[512,512]{1,0:T(8,128)(2,1)}, bf16[512,512]{1,0:T(8,128)(2,1)}, u32[]{:S(2)}, u32[]{:S(2)}) collective-permute-start(bf16[512,512]{1,0:T(8,128)(2,1)} %collective-permute-done.11), channel_id=1, source_target_pairs={{0,2},{1,3},{2,0},{3,1},{4,6},{5,7},{6,4},{7,5},{8,10},{9,11},{10,... | collective-permute-start | bytes 1572872 | tf_op jit(solution)/shard_map/ppermute | solution.py:32
  122.2 28.2 %collective-permute-start.22 = (bf16[512,512]{1,0:T(8,128)(2,1)}, bf16[512,512]{1,0:T(8,128)(2,1)}, u32[]{:S(2)}, u32[]{:S(2)}) collective-permute-start(bf16[512,512]{1,0:T(8,128)(2,1)} %collective-permute-done.18), channel_id=1, source_target_pairs={{0,0},{1,1},{2,4},{3,5},{4,2},{5,3},{6,6},{7,7},{8,8},{9,9},{10,12... | collective-permute-start | bytes 1572872 | tf_op jit(solution)/shard_map/ppermute | solution.py:40
  127.6 24.8 %collective-permute-start.23 = (bf16[512,512]{1,0:T(8,128)(2,1)}, bf16[512,512]{1,0:T(8,128)(2,1)}, u32[]{:S(2)}, u32[]{:S(2)}) collective-permute-start(bf16[512,512]{1,0:T(8,128)(2,1)} %collective-permute-done.18), channel_id=1, source_target_pairs={{0,1},{1,0},{2,3},{3,2},{4,5},{5,4},{6,7},{7,6},{8,9},{9,8},{10,11... | collective-permute-start | bytes 1572872 | tf_op jit(solution)/shard_map/ppermute | solution.py:32
  130.2 18.1 %collective-permute-start.24 = (f32[64,1024]{1,0:T(8,128)}, f32[64,1024]{1,0:T(8,128)}, u32[]{:S(2)}, u32[]{:S(2)}) collective-permute-start(f32[64,1024]{1,0:T(8,128)} %add.298), channel_id=1, source_target_pairs={{0,4},{1,5},{2,6},{3,7},{4,0},{5,1},{6,2},{7,3},{8,12},{9,13},{10,... | collective-permute-start | bytes 786440 | tf_op jit(solution)/shard_map/ppermute | solution.py:32
  130.2 23.2 %copy-start.12 = (bf16[1,64,4096]{2,1,0:T(8,128)(2,1)S(1)}, bf16[1,64,4096]{2,1,0:T(8,128)(2,1)}, u32[]{:S(2)}) copy-start(bf16[1,64,4096]{2,1,0:T(8,128)(2,1)} %param.10) | copy-start | bytes 1572868
  130.3 19.6 %collective-permute-start.30 = (f32[64,1024]{1,0:T(8,128)S(1)}, f32[64,1024]{1,0:T(8,128)}, u32[]{:S(2)}, u32[]{:S(2)}) collective-permute-start(f32[64,1024]{1,0:T(8,128)S(1)} %get-tuple-element.115), channel_id=1, source_target_pairs={{0,16},{8,24},{16,0},{24,8},{1,17},{9,25},{17,1},{25,9},{2,18},{10... | collective-permute-start | bytes 786440 | tf_op jit(solution)/shard_map/ppermute | solution.py:32
  132.8 22.7 %collective-permute-start.31 = (bf16[512,512]{1,0:T(8,128)(2,1)S(1)}, bf16[512,512]{1,0:T(8,128)(2,1)S(1)}, u32[]{:S(2)}, u32[]{:S(2)}) collective-permute-start(bf16[512,512]{1,0:T(8,128)(2,1)S(1)} %copy-done.14), channel_id=1, source_target_pairs={{0,2},{1,3},{2,0},{3,1},{4,6},{5,7},{6,4},{7,5},{8,10},{9,11},{10,... | collective-permute-start | bytes 1572872 | tf_op jit(solution)/shard_map/ppermute | solution.py:32
  148.2 13.3 %collective-permute-start.32 = (bf16[512,512]{1,0:T(8,128)(2,1)}, bf16[512,512]{1,0:T(8,128)(2,1)S(1)}, u32[]{:S(2)}, u32[]{:S(2)}) collective-permute-start(bf16[512,512]{1,0:T(8,128)(2,1)} %collective-permute-done.25), channel_id=1, source_target_pairs={{0,0},{1,1},{2,4},{3,5},{4,2},{5,3},{6,6},{7,7},{8,8},{9,9},{10,12... | collective-permute-start | bytes 1572872 | tf_op jit(solution)/shard_map/ppermute | solution.py:40
  149.9 11.6 %collective-permute-start.33 = (bf16[512,512]{1,0:T(8,128)(2,1)}, bf16[512,512]{1,0:T(8,128)(2,1)S(1)}, u32[]{:S(2)}, u32[]{:S(2)}) collective-permute-start(bf16[512,512]{1,0:T(8,128)(2,1)} %collective-permute-done.25), channel_id=1, source_target_pairs={{0,1},{1,0},{2,3},{3,2},{4,5},{5,4},{6,7},{7,6},{8,9},{9,8},{10,11... | collective-permute-start | bytes 1572872 | tf_op jit(solution)/shard_map/ppermute | solution.py:32
  150.4 11.0 %collective-permute-start.34 = (f32[64,1024]{1,0:T(8,128)S(1)}, f32[64,1024]{1,0:T(8,128)S(1)}, u32[]{:S(2)}, u32[]{:S(2)}) collective-permute-start(f32[64,1024]{1,0:T(8,128)S(1)} %add.322), channel_id=1, source_target_pairs={{0,6},{1,7},{2,4},{3,5},{4,2},{5,3},{6,0},{7,1},{8,14},{9,15},{10,... | collective-permute-start | bytes 786440 | tf_op jit(solution)/shard_map/ppermute | solution.py:32
  153.5 21.3 %collective-permute-start.39 = (bf16[512,512]{1,0:T(8,128)(2,1)}, bf16[512,512]{1,0:T(8,128)(2,1)S(1)}, u32[]{:S(2)}, u32[]{:S(2)}) collective-permute-start(bf16[512,512]{1,0:T(8,128)(2,1)} %collective-permute-done.22), channel_id=1, source_target_pairs={{0,2},{1,3},{2,0},{3,1},{4,6},{5,7},{6,4},{7,5},{8,10},{9,11},{10,... | collective-permute-start | bytes 1572872 | tf_op jit(solution)/shard_map/ppermute | solution.py:32
  161.9 14.4 %collective-permute-start.36 = (bf16[64,4096]{1,0:T(8,128)(2,1)S(1)}, bf16[64,4096]{1,0:T(8,128)(2,1)S(1)}, u32[]{:S(2)}, u32[]{:S(2)}) collective-permute-start(bf16[64,4096]{1,0:T(8,128)(2,1)S(1)} %multiply_convert_fusion), channel_id=1, source_target_pairs={{0,16},{8,24},{16,0},{24,8},{1,17},{9,25},{17,1},{25,9},{2,18},{10... | collective-permute-start | bytes 1572872 | tf_op jit(solution)/shard_map/ppermute | solution.py:32
  163.6 33.0 %collective-permute-start.38 = (bf16[512,512]{1,0:T(8,128)(2,1)S(1)}, bf16[512,512]{1,0:T(8,128)(2,1)S(1)}, u32[]{:S(2)}, u32[]{:S(2)}) collective-permute-start(bf16[512,512]{1,0:T(8,128)(2,1)S(1)} %broadcast_select_fusion.3), channel_id=1, source_target_pairs={{0,1},{1,0},{2,3},{3,2},{4,5},{5,4},{6,7},{7,6},{8,9},{9,8},{10,11... | collective-permute-start | bytes 1572872 | tf_op jit(solution)/shard_map/ppermute | solution.py:32
  165.1 23.7 %collective-permute-start.35 = (bf16[64,4096]{1,0:T(8,128)(2,1)S(1)}, bf16[64,4096]{1,0:T(8,128)(2,1)S(1)}, u32[]{:S(2)}, u32[]{:S(2)}) collective-permute-start(bf16[64,4096]{1,0:T(8,128)(2,1)S(1)} %multiply_convert_fusion), channel_id=1, source_target_pairs={{0,8},{8,0},{16,24},{24,16},{1,9},{9,1},{17,25},{25,17},{2,10},{10... | collective-permute-start | bytes 1572872 | tf_op jit(solution)/shard_map/ppermute | solution.py:32
  165.1 22.1 %collective-permute-start.42 = (bf16[512,512]{1,0:T(8,128)(2,1)S(1)}, bf16[512,512]{1,0:T(8,128)(2,1)S(1)}, u32[]{:S(2)}, u32[]{:S(2)}) collective-permute-start(bf16[512,512]{1,0:T(8,128)(2,1)S(1)} %collective-permute-done.32), channel_id=1, source_target_pairs={{0,2},{1,3},{2,0},{3,1},{4,6},{5,7},{6,4},{7,5},{8,10},{9,11},{10,... | collective-permute-start | bytes 1572872 | tf_op jit(solution)/shard_map/ppermute | solution.py:32
  174.8 29.3 %collective-permute-start.41 = (bf16[512,512]{1,0:T(8,128)(2,1)S(1)}, bf16[512,512]{1,0:T(8,128)(2,1)S(1)}, u32[]{:S(2)}, u32[]{:S(2)}) collective-permute-start(bf16[512,512]{1,0:T(8,128)(2,1)S(1)} %broadcast_select_fusion.1), channel_id=1, source_target_pairs={{0,1},{1,0},{2,3},{3,2},{4,5},{5,4},{6,7},{7,6},{8,9},{9,8},{10,11... | collective-permute-start | bytes 1572872 | tf_op jit(solution)/shard_map/ppermute | solution.py:32
  176.3 13.1 %collective-permute-start.37 = (bf16[64,4096]{1,0:T(8,128)(2,1)S(1)}, bf16[64,4096]{1,0:T(8,128)(2,1)S(1)}, u32[]{:S(2)}, u32[]{:S(2)}) collective-permute-start(bf16[64,4096]{1,0:T(8,128)(2,1)S(1)} %collective-permute-done.36), channel_id=1, source_target_pairs={{0,8},{8,0},{16,24},{24,16},{1,9},{9,1},{17,25},{25,17},{2,10},{10... | collective-permute-start | bytes 1572872 | tf_op jit(solution)/shard_map/ppermute | solution.py:32
  187.3 14.8 %collective-permute-start.40 = (bf16[512,512]{1,0:T(8,128)(2,1)S(1)}, bf16[512,512]{1,0:T(8,128)(2,1)S(1)}, u32[]{:S(2)}, u32[]{:S(2)}) collective-permute-start(bf16[512,512]{1,0:T(8,128)(2,1)S(1)} %broadcast_select_fusion.2), channel_id=1, source_target_pairs={{0,1},{1,0},{2,3},{3,2},{4,5},{5,4},{6,7},{7,6},{8,9},{9,8},{10,11... | collective-permute-start | bytes 1572872 | tf_op jit(solution)/shard_map/ppermute | solution.py:32
  188.8 23.4 %collective-permute-start.43 = (bf16[512,512]{1,0:T(8,128)(2,1)S(1)}, bf16[512,512]{1,0:T(8,128)(2,1)S(1)}, u32[]{:S(2)}, u32[]{:S(2)}) collective-permute-start(bf16[512,512]{1,0:T(8,128)(2,1)S(1)} %broadcast_select_fusion), channel_id=1, source_target_pairs={{0,1},{1,0},{2,3},{3,2},{4,5},{5,4},{6,7},{7,6},{8,9},{9,8},{10,11... | collective-permute-start | bytes 1572872 | tf_op jit(solution)/shard_map/ppermute | solution.py:32
  215.6 2.7 %collective-permute-start.44 = (f32[64,4096]{1,0:T(8,128)S(1)}, f32[64,4096]{1,0:T(8,128)S(1)}, u32[]{:S(2)}, u32[]{:S(2)}) collective-permute-start(f32[64,4096]{1,0:T(8,128)S(1)} %fusion.85), channel_id=1, source_target_pairs={{0,8},{8,0},{16,24},{24,16},{1,9},{9,1},{17,25},{25,17},{2,10},{10... | collective-permute-start | bytes 3145736 | tf_op jit(solution)/shard_map/ppermute | solution.py:32
  219.2 14.0 %collective-permute-start.45 = (f32[32,4096]{1,0:T(8,128)S(1)}, f32[32,4096]{1,0:T(8,128)S(1)}, u32[]{:S(2)}, u32[]{:S(2)}) collective-permute-start(f32[32,4096]{1,0:T(8,128)S(1)} %dynamic-slice_bitcast_fusion), channel_id=1, source_target_pairs={{0,16},{8,24},{16,0},{24,8},{1,17},{9,25},{17,1},{25,9},{2,18},{10... | collective-permute-start | bytes 1572872 | tf_op jit(solution)/shard_map/ppermute | solution.py:32
  (30 other events, 174.8 us)

commit v3 on v1

v3 whole, which is shorter than its diff:
```python
import math

import jax
import jax.numpy as jnp
from jax import lax
from jax.experimental import pallas as pl
from jax.experimental.pallas import tpu as pltpu
from jax.sharding import PartitionSpec as P

HD = 256
TILE = 256
F32, BF16 = jnp.float32, jnp.bfloat16
CHEAP = pl.CostEstimate(flops=1, bytes_accessed=1, transcendentals=0)
SOME = pl.CostEstimate(flops=1, bytes_accessed=1_800_000, transcendentals=0)


class Line:
    def __init__(self, name, total, size, stride):
        self.name, self.total, self.size, self.stride = name, total, size, stride
        self.at = (lax.axis_index(name) // stride) % size

    def place(self, index):
        return (index // self.stride) % self.size

    def shift(self, value, step):
        pairs = [
            (i, i + step * self.stride)
            for i in range(self.total)
            if 0 <= self.place(i) + step < self.size
        ]
        return lax.ppermute(value, self.name, pairs)

    def swap(self, value, mask):
        pairs = [
            (i, i + ((self.place(i) ^ mask) - self.place(i)) * self.stride)
            for i in range(self.total)
        ]
        return lax.ppermute(value, self.name, pairs)

    def cross(self, value):
        return self.turn(value, (0, 2, 1, 3))

    def ends(self, value):
        return self.turn(value, (3, 1, 2, 0))

    def turn(self, value, order):
        pairs = [
            (i, i + (order[self.place(i)] - self.place(i)) * self.stride) for i in range(self.total)
        ]
        return lax.ppermute(value, self.name, pairs)

    def gather(self, pieces):
        return [pieces] + [[self.swap(p, m) for p in pieces] for m in range(1, self.size)]


def tick(*groups):
    sizes = [len(g) for g in groups]
    flat = lax.optimization_barrier(tuple(v for g in groups for v in g))
    out, at = [], 0
    for size in sizes:
        out.append(list(flat[at : at + size]))
        at += size
    return out


def local(body, outs, *operands, scratch=(), cost=CHEAP, left=0):
    vmem = pl.BlockSpec(memory_space=pltpu.VMEM)
    stay = pl.BlockSpec(memory_space=pltpu.HBM)
    return pl.pallas_call(
        body,
        out_shape=[jax.ShapeDtypeStruct(shape, kind) for shape, kind in outs],
        in_specs=[pl.BlockSpec(memory_space=pltpu.SMEM)] + [stay] * left
        + [vmem] * (len(operands) - 1 - left),
        out_specs=[vmem] * len(outs),
        scratch_shapes=list(scratch),
        cost_estimate=cost,
        compiler_params=pltpu.CompilerParams(vmem_limit_bytes=12 << 20),
    )(*operands)


def mlp_part(at, pieces, downs, shape, first=0, sofar=None):
    ny, nc, rows = shape
    ways, halves = len(pieces[0]), len(pieces)
    flat = [p for half in pieces for p in half]
    total = ny * nc * rows
    depth = pieces[0][0].shape[1]
    block = downs[0].shape[1]
    before = list(sofar or ())

    def body(at_ref, *refs):
        lhs, refs = refs[: ways * halves], refs[ways * halves :]
        d0, d1 = refs[:2]
        adds, (mine, theirs, taken, sems) = refs[2:-4], refs[-4:]
        inner = (at_ref[0] == 1) | (at_ref[0] == 2)

        def fetch(h, way):
            cols = pl.ds(h * depth, depth)
            return pltpu.make_async_copy(lhs[ways * h + way], taken.at[:, cols], sems.at[h])

        for h in range(halves):
            if ways == 1:
                fetch(h, 0).start()
                continue

            @pl.when(inner)
            def _():
                fetch(h, 0).start()

            @pl.when(jnp.logical_not(inner))
            def _():
                fetch(h, 1).start()

        for h in range(halves):
            fetch(h, 0).wait()

        here = at_ref[3] == 0
        deep = slice(first * depth, (first + halves) * depth)
        for j, down in enumerate((d0, d1)):

            @pl.loop(0, block // TILE)
            def _(t):
                part = jnp.dot(
                    taken[...],
                    down[deep, pl.ds(pl.multiple_of(t * TILE, TILE), TILE)],
                    preferred_element_type=F32,
                )
                cols = pl.ds(pl.multiple_of(j * block + t * TILE, TILE), TILE)
                for i in range(ny):
                    to = slice(i * rows, (i + 1) * rows)
                    one = part[(2 * i) * rows : (2 * i + 1) * rows]
                    two = part[(2 * i + 1) * rows : (2 * i + 2) * rows]
                    own, far = jnp.where(here, one, two), jnp.where(here, two, one)
                    if adds:
                        own, far = own + adds[0][to, cols], far + adds[1][to, cols]
                    mine[to, cols] = own
                    theirs[to, cols] = far

    out = ((ny * rows, 2 * block), F32)
    return local(
        body, [out, out], at, *flat, *downs, *before,
        scratch=[pltpu.VMEM((total, halves * depth), BF16), pltpu.SemaphoreType.DMA((halves,))],
        cost=SOME, left=len(flat),
    )


def core_add(at, mine, theirs):
    rows, cols = mine.shape[0] // 2, mine.shape[1]

    def body(at_ref, mine_ref, theirs_ref, keep, send):
        first = at_ref[2] == 0
        one = mine_ref[:rows] + theirs_ref[:rows]
        two = mine_ref[rows:] + theirs_ref[rows:]
        keep[...] = jnp.where(first, one, two)
        send[...] = jnp.where(first, two, one)

    return local(body, [((rows, cols), F32)] * 2, at, mine, theirs)


def norm_part(at, keep, came, others, stream, gain):
    rows, cols = keep.shape
    block = cols // 2

    def body(at_ref, keep_ref, came_ref, q10, q11, q2, q3, stream_ref, gain_ref, near, far, resid):
        zat, xat = at_ref[0], at_ref[1]
        square = jnp.zeros((rows, 1), F32)
        starts = []
        for m, ref in enumerate((None, (q10, q11), q2, q3)):
            for k in range(2):
                start = pl.multiple_of(((zat ^ m) * 2 + (xat ^ k)) * block, block)
                starts.append(start)
                here = slice(k * block, (k + 1) * block)
                if m == 0:
                    add = keep_ref[:, here] + came_ref[:, here]
                else:
                    add = ref[k][...] if m == 1 else ref[:, here]
                value = stream_ref[:, pl.ds(start, block)].astype(F32) + add
                square = square + jnp.sum(value * value, axis=-1, keepdims=True)
                at = (2 * m + k) * block
                resid[:, at : at + block] = value
        scale = lax.rsqrt(square / (8 * block) + 1e-06)
        for m, (ref, half) in enumerate(((near, 0), (far, 0), (far, 1), (near, 1))):
            for k in range(2):
                at = (2 * m + k) * block
                row = gain_ref[:, pl.ds(starts[2 * m + k], block)].astype(F32)
                to = (2 * half + k) * block
                ref[:, to : to + block] = (resid[:, at : at + block] * scale * row).astype(BF16)

    out = ((rows, 4 * block), BF16)
    return local(
        body, [out, out], at, keep, came, *others, stream, gain,
        scratch=[pltpu.VMEM((rows, 8 * block), F32)],
    )


def kv_part(at, rows, weights):
    count, width = rows.shape
    depth, cols = weights[0].shape

    def body(at_ref, *refs):
        (lhs, out, held, sems) = refs[4:]
        loads = [pltpu.make_async_copy(refs[p], held.at[p], sems.at[p]) for p in range(4)]
        for load in loads:
            load.start()
        for p, load in enumerate(loads):
            load.wait()
            for t in range(cols // TILE):
                here = slice(t * TILE, (t + 1) * TILE)
                part = jnp.dot(
                    lhs[:, p * depth : (p + 1) * depth],
                    held[p, :, here],
                    preferred_element_type=F32,
                )
                out[:, here] = part if p == 0 else out[:, here] + part

    return local(
        body, [((count, cols), F32)], at, *weights, rows,
        scratch=[pltpu.VMEM((4, depth, cols), BF16), pltpu.SemaphoreType.DMA((4,))],
        left=4,
    )[0]


def woven(z, x, y, c, hidden, down, kv, stream, gain, rows):
    E, O, X, Y = (lambda v: z.swap(v, 1)), z.cross, (lambda v: x.swap(v, 1)), (lambda v: y.swap(v, 1))
    C = lambda v: c.swap(v, 1)
    at = jnp.stack([z.at, x.at, y.at, c.at]).astype(jnp.int32)
    inner = (z.at == 1) | (z.at == 2)
    half = hidden.shape[1] // 2
    ha, hb = hidden[:, :half], hidden[:, half:]
    k, v = kv
    product = lambda pieces, xd, **more: mlp_part(at, pieces, (down, xd), (2, 2, rows), **more)

    e1a, o1a, xd = E(ha), O(ha), X(down)
    e1b, o1b = E(hb), O(hb)
    e2a, o2a = E(o1a), O(e1a)
    e2b, o2b = E(o1b), O(e1b)
    e3a, e3b = E(o2a), E(o2b)

    (o2a,), (k, v) = tick((o2a,), (k, v))
    ok, ov, xk0 = O(k), O(v), X(k)
    (e2a, o2a, e2b, o2b, xd), (k, v) = tick((e2a, o2a, e2b, o2b, xd), (k, v))
    m1, h1 = product(((e1a,), (e1b,)), xd)
    m2, h2 = product(((o2a, e2a), (o2b, e2b)), xd)
    m0, h0 = product(((ha,), (hb,)), xd)
    part3 = product(((o1a, e3a),), xd)

    done = (m1, h1, m2, h2, m0, h0, e3b, ok, ov, xk0, *part3)
    (m1, h1, m2, h2, m0, h0, e3b, ok, ov, xk0, *part3), (k, v) = tick(done, (k, v))
    fk, fv = z.ends(k), z.ends(v)
    xv0 = X(v)
    h1, h2, h0 = C(h1), C(h2), C(h0)
    m3, h3 = product(((o1b, e3b),), xd, first=1, sofar=part3)

    (h1, h2, h0, m3, h3), = tick((h1, h2, h0, m3, h3))
    h3 = C(h3)
    k2, s2 = core_add(at, m2, h2)
    s2 = Y(s2)
    k1, s1 = core_add(at, m1, h1)
    k0, s0 = core_add(at, m0, h0)

    (h3, k1, s1, k0, s0), = tick((h3, k1, s1, k0, s0))
    k3, s3 = core_add(at, m3, h3)
    s3 = Y(s3)

    (s2,), (s1, s0) = tick((s2,), (s1, s0))
    q2 = z.swap(k2 + s2, 2)
    s1 = Y(s1)

    (s3, fk, xv0), (s0,) = tick((s3, fk, xv0), (s0,))
    q3 = z.swap(k3 + s3, 3)
    s0 = Y(s0)
    kk = jnp.where(inner, ok, fk)
    xkk = X(kk)

    (s1, fv), = tick((s1, fv))
    q1 = k1 + s1
    q1 = [z.swap(part, 1) for part in jnp.split(q1, 2, axis=1)]
    vv = jnp.where(inner, ov, fv)

    (q2, q3, s0, xkk), q1, (vv,) = tick((q2, q3, s0, xkk), q1, (vv,))
    xvv = X(vv)
    mine, other = norm_part(at, k0, s0, (*q1, q2, q3), stream, gain)
    near, far = E(other), Y(mine)
    (near, far), = tick((near, far))
    nearfar = Y(near)
    near2, mine2, far2 = C(near), C(mine), C(far)
    (nearfar, near2, mine2, far2), = tick((nearfar, near2, mine2, far2))
    pair = jnp.concatenate([near, near2, nearfar, C(nearfar)], axis=0)
    own = [jnp.concatenate([mine, mine2, far, far2], axis=0)]
    wk, wv = (k, xk0, kk, xkk), (v, xv0, vv, xvv)
    keys = E(kv_part(at, pair, wk))
    values = kv_part(at, pair, wv)
    (values,), (own,) = tick((values,), own)
    values = E(values)
    return kv_part(at, own, wk) + keys, kv_part(at, own, wv) + values


def on_device(
    mlp_hidden, encoder_stream, down_proj, final_gain, kv_proj, queries, out_proj, enc_len, dec_pad
):
    seq, dp = lax.axis_size("seq"), lax.axis_size("dp")
    nx = 1 << ((dp.bit_length() - 1) // 2)
    nz = dp // nx
    nc = 2
    ny = seq // nc
    z = Line("dp", dp, nz, nx)
    x = Line("dp", dp, nx, 1)
    y = Line("seq", seq, ny, nc)
    c = Line("seq", seq, nc, 1)

    hidden = mlp_hidden[0]
    enc_total, depth = hidden.shape
    rows = enc_total // seq
    block = down_proj.shape[1]
    width = block * dp
    dot = lambda a, b: jnp.dot(a, b, preferred_element_type=jnp.float32)

    half = depth // 2
    halves = [hidden[:, :half], hidden[:, half:]]
    downs = [down_proj[:half], down_proj[half:]]
    kv_local = [kv_proj[:, 0], kv_proj[:, 1]]

    def seq_core(part):
        part = part.reshape(ny, nc, rows, nx * block)
        pick = lambda i: lax.dynamic_index_in_dim(part, i, 1, keepdims=False)
        return pick(c.at), c.swap(pick(1 - c.at), 1)

    def seq_y(mine, theirs):
        part = mine + theirs
        total = lax.dynamic_index_in_dim(part, y.at, 0, keepdims=False)
        others = [
            y.swap(lax.dynamic_index_in_dim(part, y.at ^ k, 0, keepdims=False), k)
            for k in range(1, ny)
        ]
        return [total] + others

    stream = encoder_stream[0]
    gain = final_gain.astype(jnp.float32)

    def norm(summed):
        resid, gains = [], []
        for m in range(nz):
            for k in range(nx):
                start = ((z.at ^ m) * nx + (x.at ^ k)) * block
                piece = lax.dynamic_slice_in_dim(stream, start, block, 1).astype(jnp.float32)
                resid.append(piece + summed[m][:, k * block : (k + 1) * block])
                gains.append(lax.dynamic_slice_in_dim(gain, start, block, 0))
        resid = jnp.concatenate(resid, axis=1)
        gains = jnp.concatenate(gains, axis=0)
        spread = jnp.sum(resid * resid, axis=-1, keepdims=True) / width
        return (resid * lax.rsqrt(spread + 1e-06) * gains).astype(jnp.bfloat16)

    places = []
    for k in range(ny):
        for j in range(nc):
            start = ((y.at ^ k) * nc + (c.at ^ j)) * rows
            places.append(start + jnp.arange(rows, dtype=jnp.int32))
    visible = jnp.concatenate(places) < enc_len[0]

    if (nz, nx, ny) == (4, 2, 2):
        keys, values = woven(
            z, x, y, c, hidden, down_proj, kv_local, stream, final_gain[None], rows
        )
    else:
        hidden_slots = z.gather(halves)
        down_slots = x.gather(downs)
        kv_slots = [x.gather(slot) for slot in z.gather(kv_local)]
        weights = [jnp.concatenate([s[p] for s in down_slots], axis=1) for p in range(2)]
        summed = []
        for m in range(nz):
            part = dot(hidden_slots[m][0], weights[0]) + dot(hidden_slots[m][1], weights[1])
            total = sum(seq_y(*seq_core(part)))
            summed.append(total if m == 0 else z.swap(total, m))
        encoded = []
        for (far,) in y.gather([norm(summed)]):
            encoded += [far, c.swap(far, 1)]
        encoded = jnp.concatenate(encoded, axis=0)
        keys = values = 0.0
        for m in range(nz):
            for k in range(nx):
                at = (m * nx + k) * block
                piece = encoded[:, at : at + block]
                keys = keys + dot(piece, kv_slots[m][k][0])
                values = values + dot(piece, kv_slots[m][k][1])
    keys = keys.astype(jnp.bfloat16)
    values = values.astype(jnp.bfloat16)

    heads_here = queries.shape[2] // HD
    dec_rows = queries.shape[1]
    attended = []
    for h in range(heads_here):
        cols = slice(h * HD, (h + 1) * HD)
        scores = lax.dot_general(
            queries[0][:, cols], keys[:, cols], (((1,), (1,)), ((), ())),
            preferred_element_type=jnp.float32,
        ) / math.sqrt(HD)
        scores = jnp.where(visible[None, :], scores, -jnp.inf)
        expo = jnp.exp(scores - jnp.max(scores, axis=-1, keepdims=True))
        attention = (expo / jnp.sum(expo, axis=-1, keepdims=True)).astype(jnp.bfloat16)
        attended.append(dot(attention, values[:, cols]).astype(jnp.bfloat16))
    attended = jnp.concatenate(attended, axis=1)
    row_live = jnp.arange(dec_rows, dtype=jnp.int32) < dec_rows - dec_pad[0]
    attended = jnp.where(row_live[:, None], attended, jnp.zeros_like(attended))

    out_rows = dec_rows // seq
    att = attended.reshape(ny, nc, out_rows, heads_here * HD)
    pick = lambda i: lax.dynamic_index_in_dim(att, i, 1, keepdims=False).reshape(
        ny * out_rows, heads_here * HD
    )
    part = dot(pick(c.at), out_proj) + c.swap(dot(pick(1 - c.at), out_proj), 1)
    part = part.reshape(ny, out_rows, width)
    total = lax.dynamic_index_in_dim(part, y.at, 0, keepdims=False)
    for k in range(1, ny):
        other = lax.dynamic_index_in_dim(part, y.at ^ k, 0, keepdims=False).astype(BF16)
        total = total + y.swap(other, k).astype(F32)
    return total.astype(jnp.bfloat16)[None]


def solution(mesh):
    placed = (
        P("dp", None, "seq"),
        P("dp", "seq", None),
        P("seq", "dp"),
        P(),
        P("dp", None, "seq"),
        P("dp", None, "seq"),
        P("seq", None),
        P("dp"),
        P("dp"),
    )
    return jax.shard_map(
        on_device, mesh=mesh, in_specs=placed, out_specs=P("dp", "seq", None), check_vma=False
    )
```

time: 322 us -> 201 us (0.62)
  waiting for transfers between devices: 182 us -> 80.1 us
  Pallas kernels: 0 us -> 27.3 us
  starting transfers between devices: 87.8 us -> 64.7 us
  matrix products: 27.3 us -> 4.73 us
    ppermute x25 -> x34, waiting for transfers between devices: 137 us -> 72.6 us  [swap(): return lax.ppermute(value, self.name, pairs)]
    ppermute x24 -> x8, starting transfers between devices: 66 us -> 15.3 us  [turn(): return lax.ppermute(value, self.name, pairs)]
    ppermute x24 -> x8, waiting for transfers between devices: 44.9 us -> 7.42 us  [turn(): return lax.ppermute(value, self.name, pairs)]
    ppermute x25 -> x34, starting transfers between devices: 21.8 us -> 49.4 us  [swap(): return lax.ppermute(value, self.name, pairs)]
    pallas_call x0 -> x14, Pallas kernels: none -> 27.3 us  [local(): pl.pallas_call(body, out_shape=[jax.ShapeDtypeStruct(shape, kind) for sha...]
    dot_general x36 -> x4, matrix products: 26.9 us -> 4.29 us  [on_device(): dot = lambda a, b: jnp.dot(a, b, preferred_element_type=jnp.float32)]
    unnamed x21 -> x65, local copies, waits for them, and re-layouts: 1.52 us -> 10.3 us
    slice x2, local copies, waits for them, and re-layouts: 6.85 us -> 2.75 us  [the longest x1 1.48 us: on_device(): kv_local = [kv_proj[:, 0], kv_proj[:, 1]]]
  transfers between devices with their start and end apart: 49 -> 42, of which waited for: 23 -> 19; matrix products, arithmetic and copies ran while one was open for 13% -> 6% of each run, Pallas kernels for 0% -> 13%
where the time goes in v3:
time: 201 us; the launch traced here: 200 us
  waiting for transfers between devices  80.1 us (40%)
  starting transfers between devices  64.7 us (32%)
  Pallas kernels  27.3 us (14%)
  local copies, waits for them, and re-layouts  13.4 us (7%)
  other arithmetic  7.92 us (4%)
  matrix products  4.73 us (2%)
    ppermute x34, waiting for transfers between devices, swap(): return lax.ppermute(value, self.name, pairs)  72.6 us
    ppermute x34, starting transfers between devices, swap(): return lax.ppermute(value, self.name, pairs)  49.4 us
    pallas_call x14, Pallas kernels, local(): pl.pallas_call(body, out_shape=[jax.ShapeDtypeStruct(shape, kind) for sha...  27.3 us
    ppermute x8, starting transfers between devices, turn(): return lax.ppermute(value, self.name, pairs)  15.3 us
    unnamed x65, local copies, waits for them, and re-layouts  10.3 us
    ppermute x8, waiting for transfers between devices, turn(): return lax.ppermute(value, self.name, pairs)  7.42 us
    dot_general x4, matrix products, on_device(): dot = lambda a, b: jnp.dot(a, b, preferred_element_type=jnp.float32)  4.29 us
  transfers between devices with their start and end apart: 42, of which 19 were waited for; matrix products, arithmetic and copies ran while one was open for 6% of the time, Pallas kernels for 13%

profile of v3, /device:TPU:0, one launch (start us, length us, event | category | flops | bytes accessed | tf_op | source)
XLA Modules:
  0.0 200.1 jit_solution(13170099295511935208)
XLA Ops:
  0.0 2.9 %collective-permute-start.8 = (bf16[2048,512]{1,0:T(8,128)(2,1)}, bf16[2048,512]{1,0:T(8,128)(2,1)S(1)}, u32[]{:S(2)}, u32[]{:S(2)}) collective-permute-start(bf16[2048,512]{1,0:T(8,128)(2,1)} %refs_2_.7), channel_id=1, source_target_pairs={{0,1},{1,0},{2,3},{3,2},{4,5},{5,4},{6,7},{7,6},{8,9},{9,8},{10,11... | collective-permute-start | bytes 6291464 | tf_op jit(solution)/shard_map/ppermute | solution.py:38
  4.2 1.6 collective-permute-start
  9.3 9.8 %collective-permute-done.refs_0_ = bf16[256,1024]{1,0:T(8,128)(2,1)S(1)} collective-permute-done((bf16[256,1024]{1,0:T(8,128)(2,1)S(1)}, bf16[256,1024]{1,0:T(8,128)(2,1)S(1)}, u32[]{:S(2)}, u32[]{:S(2)}) %collective-permute-start) | collective-permute-done | bytes 524320 | tf_op jit(solution)/shard_map/ppermute | solution.py:38
  19.1 1.5 collective-permute-start.4
  20.6 8.3 %collective-permute-done.1.refs_1_ = bf16[256,1024]{1,0:T(8,128)(2,1)S(1)} collective-permute-done((bf16[256,1024]{1,0:T(8,128)(2,1)S(1)}, bf16[256,1024]{1,0:T(8,128)(2,1)S(1)}, u32[]{:S(2)}, u32[]{:S(2)}) %collective-permute-start.1) | collective-permute-done | bytes 524320 | tf_op jit(solution)/shard_map/ppermute | solution.py:38
  30.4 3.7 %collective-permute-start.3 = (bf16[256,1024]{1,0:T(8,128)(2,1)S(1)}, bf16[256,1024]{1,0:T(8,128)(2,1)S(1)}, u32[]{:S(2)}, u32[]{:S(2)}) collective-permute-start(bf16[256,1024]{1,0:T(8,128)(2,1)S(1)} %collective-permute-done.2.refs_0_), channel_id=1, source_target_pairs={{0,2},{1,3},{2,0},{3,1},{4,6},{5,7},{6,4},{7,5},{8,10},{9,11},{10,... | collective-permute-start | bytes 1572872 | tf_op jit(solution)/shard_map/ppermute | solution.py:38
  34.0 1.8 collective-permute-start.6
  35.9 1.5 fusion.17
  37.7 1.6 collective-permute-start.10
  39.8 7.0 %collective-permute-done.3.refs_1_ = bf16[256,1024]{1,0:T(8,128)(2,1)S(1)} collective-permute-done((bf16[256,1024]{1,0:T(8,128)(2,1)S(1)}, bf16[256,1024]{1,0:T(8,128)(2,1)S(1)}, u32[]{:S(2)}, u32[]{:S(2)}) %collective-permute-start.3) | collective-permute-done | bytes 524320 | tf_op jit(solution)/shard_map/ppermute | solution.py:38
  47.7 12.1 %collective-permute-start.13 = (bf16[256,1024]{1,0:T(8,128)(2,1)}, bf16[256,1024]{1,0:T(8,128)(2,1)}, u32[]{:S(2)}, u32[]{:S(2)}) collective-permute-start(bf16[256,1024]{1,0:T(8,128)(2,1)} %collective-permute-done.4.refs_0_), channel_id=1, source_target_pairs={{0,2},{1,3},{2,0},{3,1},{4,6},{5,7},{6,4},{7,5},{8,10},{9,11},{10,... | collective-permute-start | bytes 1572872 | tf_op jit(solution)/shard_map/ppermute | solution.py:38
  60.6 1.4 collective-permute-start.11
  63.4 2.0 %collective-permute-start.9 = (bf16[256,1024]{1,0:T(8,128)(2,1)}, bf16[256,1024]{1,0:T(8,128)(2,1)}, u32[]{:S(2)}, u32[]{:S(2)}) collective-permute-start(bf16[256,1024]{1,0:T(8,128)(2,1)} %collective-permute-done.7.refs_2_), channel_id=1, source_target_pairs={{0,2},{1,3},{2,0},{3,1},{4,6},{5,7},{6,4},{7,5},{8,10},{9,11},{10,... | collective-permute-start | bytes 1572872 | tf_op jit(solution)/shard_map/ppermute | solution.py:38
  65.5 1.6 copy-done.2
  69.2 2.5 %shard_map.93 = (f32[128,1024]{1,0:T(8,128)S(1)}, f32[128,1024]{1,0:T(8,128)S(1)}) custom-call(s32[4]{0:T(128)S(1)} %pad_add_fusion.at_ref, bf16[256,1024]{1,0:T(8,128)(2,1)S(1)} %copy-done.11, bf16[256,1024]{1,0:T(8,128)(2,1)S(1)} %copy-done.9, bf16[2048,512]{1,0:T(8,128)(2,1)S(1)} %copy-done, bf16[2048,512]{1,0:T(8,128)(2,1)S(1)} %copy-done.2), custom_call_target="tpu_custom_call" | custom-call | flops 1 | bytes 1800000 | tf_op jit(solution)/shard_map/pallas_call | solution.py:69
  71.7 2.5 %shard_map.92 = (f32[128,1024]{1,0:T(8,128)S(1)}, f32[128,1024]{1,0:T(8,128)S(1)}) custom-call(s32[4]{0:T(128)S(1)} %pad_add_fusion.at_ref, bf16[256,1024]{1,0:T(8,128)(2,1)} %collective-permute-done.4.refs_0_, bf16[256,1024]{1,0:T(8,128)(2,1)S(1)} %copy-done.15, bf16[256,1024]{1,0:T(8,128)(2,1)} %collective-permute-done.7.refs_2_, ...), custom_call_target="tpu_custom_call" | custom-call | flops 1 | bytes 1800000 | tf_op jit(solution)/shard_map/pallas_call | solution.py:69
  74.2 2.5 %shard_map.91 = (f32[128,1024]{1,0:T(8,128)S(1)}, f32[128,1024]{1,0:T(8,128)S(1)}) custom-call(s32[4]{0:T(128)S(1)} %pad_add_fusion.at_ref, bf16[256,1024]{1,0:T(8,128)(2,1)S(1)} %copy-done.20, bf16[256,1024]{1,0:T(8,128)(2,1)S(1)} %copy-done.24, bf16[2048,512]{1,0:T(8,128)(2,1)S(1)} %copy-done, bf16[2048,512]{1,0:T(8,128)(2,1)S(1)} %copy-done.2), custom_call_target="tpu_custom_call" | custom-call | flops 1 | bytes 1800000 | tf_op jit(solution)/shard_map/pallas_call | solution.py:69
  76.7 2.8 %shard_map.94 = (f32[128,1024]{1,0:T(8,128)S(1)}, f32[128,1024]{1,0:T(8,128)S(1)}) custom-call(s32[4]{0:T(128)S(1)} %pad_add_fusion.at_ref, bf16[256,1024]{1,0:T(8,128)(2,1)S(1)} %copy-done.22, bf16[256,1024]{1,0:T(8,128)(2,1)} %collective-permute-done.13.refs_1_, bf16[2048,512]{1,0:T(8,128)(2,1)S(1)} %copy-done, bf16[2048,512]{1,0:T(8,128)(2,1)S(1)} %copy-done.2), custom_call_target="tpu_custom_call" | custom-call | flops 1 | bytes 1800000 | tf_op jit(solution)/shard_map/pallas_call | solution.py:69
  80.2 2.8 %shard_map.95 = (f32[128,1024]{1,0:T(8,128)S(1)}, f32[128,1024]{1,0:T(8,128)S(1)}) custom-call(s32[4]{0:T(128)S(1)} %pad_add_fusion.at_ref, bf16[256,1024]{1,0:T(8,128)(2,1)S(1)} %copy-done.13, bf16[256,1024]{1,0:T(8,128)(2,1)} %collective-permute-done.9.refs_1_, bf16[2048,512]{1,0:T(8,128)(2,1)S(1)} %copy-done, bf16[2048,512]{1,0:T(8,128)(2,1)S(1)} %copy-done.2, ...), custom_call_target="tpu_custom_call" | custom-call | flops 1 | bytes 1800000 | tf_op jit(solution)/shard_map/pallas_call | solution.py:69
  83.6 4.1 %collective-permute-start.19 = (bf16[512,512]{1,0:T(8,128)(2,1)S(1)}, bf16[512,512]{1,0:T(8,128)(2,1)}, u32[]{:S(2)}, u32[]{:S(2)}) collective-permute-start(bf16[512,512]{1,0:T(8,128)(2,1)S(1)} %get-tuple-element.101.refs_0_), channel_id=1, source_target_pairs={{0,6},{1,7},{2,2},{3,3},{4,4},{5,5},{6,0},{7,1},{8,14},{9,15},{10,... | collective-permute-start | bytes 1572872 | tf_op jit(solution)/shard_map/ppermute | solution.py:50
  89.7 1.6 collective-permute-start.21
  94.4 3.9 %collective-permute-start.27 = (bf16[512,512]{1,0:T(8,128)(2,1)S(1)}, bf16[512,512]{1,0:T(8,128)(2,1)}, u32[]{:S(2)}, u32[]{:S(2)}) collective-permute-start(bf16[512,512]{1,0:T(8,128)(2,1)S(1)} %get-tuple-element.124.refs_0_), channel_id=1, source_target_pairs={{0,6},{1,7},{2,2},{3,3},{4,4},{5,5},{6,0},{7,1},{8,14},{9,15},{10,... | collective-permute-start | bytes 1572872 | tf_op jit(solution)/shard_map/ppermute | solution.py:50
  99.1 1.5 collective-permute-start.26
  102.2 2.6 %collective-permute-done.18 = f32[64,1024]{1,0:T(8,128)} collective-permute-done((f32[64,1024]{1,0:T(8,128)S(1)}, f32[64,1024]{1,0:T(8,128)}, u32[]{:S(2)}, u32[]{:S(2)}) %collective-permute-start.18) | collective-permute-done | bytes 262176 | tf_op jit(solution)/shard_map/ppermute | solution.py:38
  106.6 6.9 %collective-permute-done.27 = bf16[512,512]{1,0:T(8,128)(2,1)} collective-permute-done((bf16[512,512]{1,0:T(8,128)(2,1)S(1)}, bf16[512,512]{1,0:T(8,128)(2,1)}, u32[]{:S(2)}, u32[]{:S(2)}) %collective-permute-start.27) | collective-permute-done | bytes 524320 | tf_op jit(solution)/shard_map/ppermute | solution.py:50
  113.6 2.0 %collective-permute-start.29 = (f32[64,512]{1,0:T(8,128)S(1)}, f32[64,512]{1,0:T(8,128)S(1)}, u32[]{:S(2)}, u32[]{:S(2)}) collective-permute-start(f32[64,512]{1,0:T(8,128)S(1)} %get-tuple-element.165), channel_id=1, source_target_pairs={{0,2},{1,3},{2,0},{3,1},{4,6},{5,7},{6,4},{7,5},{8,10},{9,11},{10,... | collective-permute-start | bytes 393224 | tf_op jit(solution)/shard_map/ppermute | solution.py:38
  116.6 2.2 %collective-permute-start.23 = (f32[64,1024]{1,0:T(8,128)S(1)}, f32[64,1024]{1,0:T(8,128)S(1)}, u32[]{:S(2)}, u32[]{:S(2)}) collective-permute-start(f32[64,1024]{1,0:T(8,128)S(1)} %add.116), channel_id=1, source_target_pairs={{0,6},{1,7},{2,4},{3,5},{4,2},{5,3},{6,0},{7,1},{8,14},{9,15},{10,... | collective-permute-start | bytes 786440 | tf_op jit(solution)/shard_map/ppermute | solution.py:38
  118.9 5.8 %collective-permute-done.22.q2 = f32[64,1024]{1,0:T(8,128)S(1)} collective-permute-done((f32[64,1024]{1,0:T(8,128)S(1)}, f32[64,1024]{1,0:T(8,128)S(1)}, u32[]{:S(2)}, u32[]{:S(2)}) %collective-permute-start.22) | collective-permute-done | bytes 262176 | tf_op jit(solution)/shard_map/ppermute | solution.py:38
  124.7 1.5 collective-permute-start.24
  127.3 2.6 %collective-permute-done.28.q10 = f32[64,512]{1,0:T(8,128)S(1)} collective-permute-done((f32[64,512]{1,0:T(8,128)S(1)}, f32[64,512]{1,0:T(8,128)S(1)}, u32[]{:S(2)}, u32[]{:S(2)}) %collective-permute-start.28) | collective-permute-done | bytes 131104 | tf_op jit(solution)/shard_map/ppermute | solution.py:38
  132.7 1.6 shard_map.100
  134.3 2.8 %collective-permute-start.31 = (bf16[64,2048]{1,0:T(8,128)(2,1)S(1)}, bf16[64,2048]{1,0:T(8,128)(2,1)S(1)}, u32[]{:S(2)}, u32[]{:S(2)}) collective-permute-start(bf16[64,2048]{1,0:T(8,128)(2,1)S(1)} %get-tuple-element.151), channel_id=1, source_target_pairs={{0,2},{1,3},{2,0},{3,1},{4,6},{5,7},{6,4},{7,5},{8,10},{9,11},{10,... | collective-permute-start | bytes 786440 | tf_op jit(solution)/shard_map/ppermute | solution.py:38
  137.1 1.5 collective-permute-start.32
  138.6 5.0 %collective-permute-done.31 = bf16[64,2048]{1,0:T(8,128)(2,1)S(1)} collective-permute-done((bf16[64,2048]{1,0:T(8,128)(2,1)S(1)}, bf16[64,2048]{1,0:T(8,128)(2,1)S(1)}, u32[]{:S(2)}, u32[]{:S(2)}) %collective-permute-start.31) | collective-permute-done | bytes 262176 | tf_op jit(solution)/shard_map/ppermute | solution.py:38
  143.6 1.8 collective-permute-done.32
  145.3 1.5 collective-permute-start.33
  147.4 1.5 collective-permute-start.30
  148.9 3.6 %collective-permute-done.33 = bf16[64,2048]{1,0:T(8,128)(2,1)} collective-permute-done((bf16[64,2048]{1,0:T(8,128)(2,1)S(1)}, bf16[64,2048]{1,0:T(8,128)(2,1)}, u32[]{:S(2)}, u32[]{:S(2)}) %collective-permute-start.33) | collective-permute-done | bytes 262176 | tf_op jit(solution)/shard_map/ppermute | solution.py:38
  154.5 3.2 %shard_map.103 = f32[256,512]{1,0:T(8,128)} custom-call(s32[4]{0:T(128)S(1)} %pad_add_fusion.at_ref, bf16[512,512]{1,0:T(8,128)(2,1)S(1)} %get-tuple-element.101.refs_0_, bf16[512,512]{1,0:T(8,128)(2,1)} %collective-permute-done.12.refs_1_, bf16[512,512]{1,0:T(8,128)(2,1)S(1)} %broadcast_select_fusion.1.refs_2_, bf16[512,512]{1,0:T(8,128)(2,1)S(1)} %copy-done.6, ...), custom_call_target="tpu_custom_call" | custom-call | flops 1 | bytes 1 | tf_op jit(solution)/shard_map/pallas_call | solution.py:69
  161.4 2.0 %shard_map.101 = f32[256,512]{1,0:T(8,128)S(1)} custom-call(s32[4]{0:T(128)S(1)} %pad_add_fusion.at_ref, bf16[512,512]{1,0:T(8,128)(2,1)S(1)} %get-tuple-element.124.refs_0_, bf16[512,512]{1,0:T(8,128)(2,1)S(1)} %copy-done.4, bf16[512,512]{1,0:T(8,128)(2,1)S(1)} %broadcast_select_fusion.refs_2_, bf16[512,512]{1,0:T(8,128)(2,1)} %collective-permute-done.30.refs_3_, ...), custom_call_target="tpu_custom_call" | custom-call | flops 1 | bytes 1 | tf_op jit(solution)/shard_map/pallas_call | solution.py:69
  163.4 2.3 %shard_map.102 = f32[256,512]{1,0:T(8,128)S(1)} custom-call(s32[4]{0:T(128)S(1)} %pad_add_fusion.at_ref, bf16[512,512]{1,0:T(8,128)(2,1)S(1)} %get-tuple-element.101.refs_0_, bf16[512,512]{1,0:T(8,128)(2,1)} %collective-permute-done.12.refs_1_, bf16[512,512]{1,0:T(8,128)(2,1)S(1)} %broadcast_select_fusion.1.refs_2_, bf16[512,512]{1,0:T(8,128)(2,1)S(1)} %copy-done.7, ...), custom_call_target="tpu_custom_call" | custom-call | flops 1 | bytes 1 | tf_op jit(solution)/shard_map/pallas_call | solution.py:69
  167.0 2.0 %shard_map.104 = f32[256,512]{1,0:T(8,128)S(1)} custom-call(s32[4]{0:T(128)S(1)} %pad_add_fusion.at_ref, bf16[512,512]{1,0:T(8,128)(2,1)S(1)} %get-tuple-element.124.refs_0_, bf16[512,512]{1,0:T(8,128)(2,1)S(1)} %copy-done.4, bf16[512,512]{1,0:T(8,128)(2,1)S(1)} %broadcast_select_fusion.refs_2_, bf16[512,512]{1,0:T(8,128)(2,1)} %collective-permute-done.30.refs_3_, ...), custom_call_target="tpu_custom_call" | custom-call | flops 1 | bytes 1 | tf_op jit(solution)/shard_map/pallas_call | solution.py:69
  169.1 3.7 %collective-permute-done.38 = f32[256,512]{1,0:T(8,128)} collective-permute-done((f32[256,512]{1,0:T(8,128)}, f32[256,512]{1,0:T(8,128)}, u32[]{:S(2)}, u32[]{:S(2)}) %collective-permute-start.38) | collective-permute-done | bytes 524320 | tf_op jit(solution)/shard_map/ppermute | solution.py:38
  174.4 9.1 %collective-permute-done.39 = f32[256,512]{1,0:T(8,128)S(1)} collective-permute-done((f32[256,512]{1,0:T(8,128)S(1)}, f32[256,512]{1,0:T(8,128)S(1)}, u32[]{:S(2)}, u32[]{:S(2)}) %collective-permute-start.39) | collective-permute-done | bytes 524320 | tf_op jit(solution)/shard_map/ppermute | solution.py:38
  185.2 2.6 %collective-permute-done.40 = f32[64,4096]{1,0:T(8,128)S(1)} collective-permute-done((f32[64,4096]{1,0:T(8,128)S(1)}, f32[64,4096]{1,0:T(8,128)S(1)}, u32[]{:S(2)}, u32[]{:S(2)}) %collective-permute-start.40) | collective-permute-done | bytes 1048608 | tf_op jit(solution)/shard_map/ppermute | solution.py:38
  187.8 3.0 %convolution_add_fusion = f32[64,4096]{1,0:T(8,128)S(1)} fusion(f32[64,4096]{1,0:T(8,128)S(1)} %collective-permute-done.40, bf16[64,512]{1,0:T(8,128)(2,1)S(1)} %bitcast.37, bf16[512,4096]{1,0:T(8,128)(2,1)} %param.15), kind=kOutput, calls=%fused_computation | convolution fusion | flops 268697600 | bytes 6356992 | tf_op jit(solution)/shard_map/dot_general | solution.py:315
  190.9 1.6 collective-permute-start.41
  192.5 6.8 %collective-permute-done.41 = bf16[32,4096]{1,0:T(8,128)(2,1)S(1)} collective-permute-done((bf16[32,4096]{1,0:T(8,128)(2,1)S(1)}, bf16[32,4096]{1,0:T(8,128)(2,1)S(1)}, u32[]{:S(2)}, u32[]{:S(2)}) %collective-permute-start.41) | collective-permute-done | bytes 262176 | tf_op jit(solution)/shard_map/ppermute | solution.py:38
  (146 shorter events, 37.7 us)
Async XLA Ops:
  0.0 35.9 %copy-start.28 = (bf16[512,2,512]{2,1,0:T(2,128)(2,1)S(1)}, bf16[512,2,512]{2,1,0:T(2,128)(2,1)}, u32[]{:S(2)}) copy-start(bf16[512,2,512]{2,1,0:T(2,128)(2,1)} %param.13) | copy-start | bytes 3145732
  0.0 62.0 %collective-permute-start.8 = (bf16[2048,512]{1,0:T(8,128)(2,1)}, bf16[2048,512]{1,0:T(8,128)(2,1)S(1)}, u32[]{:S(2)}, u32[]{:S(2)}) collective-permute-start(bf16[2048,512]{1,0:T(8,128)(2,1)} %refs_2_.7), channel_id=1, source_target_pairs={{0,1},{1,0},{2,3},{3,2},{4,5},{5,4},{6,7},{7,6},{8,9},{9,8},{10,11... | collective-permute-start | bytes 6291464 | tf_op jit(solution)/shard_map/ppermute | solution.py:38
  4.2 14.9 %collective-permute-start = (bf16[256,1024]{1,0:T(8,128)(2,1)S(1)}, bf16[256,1024]{1,0:T(8,128)(2,1)S(1)}, u32[]{:S(2)}, u32[]{:S(2)}) collective-permute-start(bf16[256,1024]{1,0:T(8,128)(2,1)S(1)} %get-tuple-element.164.refs_0_), channel_id=1, source_target_pairs={{0,2},{1,3},{2,0},{3,1},{4,6},{5,7},{6,4},{7,5},{8,10},{9,11},{10,... | collective-permute-start | bytes 1572872 | tf_op jit(solution)/shard_map/ppermute | solution.py:38
  5.9 23.0 %collective-permute-start.1 = (bf16[256,1024]{1,0:T(8,128)(2,1)S(1)}, bf16[256,1024]{1,0:T(8,128)(2,1)S(1)}, u32[]{:S(2)}, u32[]{:S(2)}) collective-permute-start(bf16[256,1024]{1,0:T(8,128)(2,1)S(1)} %get-tuple-element.163.refs_1_), channel_id=1, source_target_pairs={{0,2},{1,3},{2,0},{3,1},{4,6},{5,7},{6,4},{7,5},{8,10},{9,11},{10,... | collective-permute-start | bytes 1572872 | tf_op jit(solution)/shard_map/ppermute | solution.py:38
  6.3 24.0 %collective-permute-start.2 = (bf16[256,1024]{1,0:T(8,128)(2,1)S(1)}, bf16[256,1024]{1,0:T(8,128)(2,1)S(1)}, u32[]{:S(2)}, u32[]{:S(2)}) collective-permute-start(bf16[256,1024]{1,0:T(8,128)(2,1)S(1)} %get-tuple-element.164.refs_0_), channel_id=1, source_target_pairs={{0,0},{1,1},{2,4},{3,5},{4,2},{5,3},{6,6},{7,7},{8,8},{9,9},{10,12... | collective-permute-start | bytes 1572872 | tf_op jit(solution)/shard_map/ppermute | solution.py:50
  7.8 26.3 %collective-permute-start.5 = (bf16[256,1024]{1,0:T(8,128)(2,1)S(1)}, bf16[256,1024]{1,0:T(8,128)(2,1)S(1)}, u32[]{:S(2)}, u32[]{:S(2)}) collective-permute-start(bf16[256,1024]{1,0:T(8,128)(2,1)S(1)} %get-tuple-element.163.refs_1_), channel_id=1, source_target_pairs={{0,0},{1,1},{2,4},{3,5},{4,2},{5,3},{6,6},{7,7},{8,8},{9,9},{10,12... | collective-permute-start | bytes 1572872 | tf_op jit(solution)/shard_map/ppermute | solution.py:50
  19.1 18.2 %copy-start.19 = (bf16[256,1024]{1,0:T(8,128)(2,1)}, bf16[256,1024]{1,0:T(8,128)(2,1)S(1)}, u32[]{:S(2)}) copy-start(bf16[256,1024]{1,0:T(8,128)(2,1)S(1)} %collective-permute-done.refs_0_) | copy-start | bytes 1572868
  19.1 18.6 %collective-permute-start.4 = (bf16[256,1024]{1,0:T(8,128)(2,1)S(1)}, bf16[256,1024]{1,0:T(8,128)(2,1)}, u32[]{:S(2)}, u32[]{:S(2)}) collective-permute-start(bf16[256,1024]{1,0:T(8,128)(2,1)S(1)} %collective-permute-done.refs_0_), channel_id=1, source_target_pairs={{0,0},{1,1},{2,4},{3,5},{4,2},{5,3},{6,6},{7,7},{8,8},{9,9},{10,12... | collective-permute-start | bytes 1572872 | tf_op jit(solution)/shard_map/ppermute | solution.py:50
  28.9 10.4 %collective-permute-start.7 = (bf16[256,1024]{1,0:T(8,128)(2,1)S(1)}, bf16[256,1024]{1,0:T(8,128)(2,1)}, u32[]{:S(2)}, u32[]{:S(2)}) collective-permute-start(bf16[256,1024]{1,0:T(8,128)(2,1)S(1)} %collective-permute-done.1.refs_1_), channel_id=1, source_target_pairs={{0,0},{1,1},{2,4},{3,5},{4,2},{5,3},{6,6},{7,7},{8,8},{9,9},{10,12... | collective-permute-start | bytes 1572872 | tf_op jit(solution)/shard_map/ppermute | solution.py:50
  30.4 16.5 %collective-permute-start.3 = (bf16[256,1024]{1,0:T(8,128)(2,1)S(1)}, bf16[256,1024]{1,0:T(8,128)(2,1)S(1)}, u32[]{:S(2)}, u32[]{:S(2)}) collective-permute-start(bf16[256,1024]{1,0:T(8,128)(2,1)S(1)} %collective-permute-done.2.refs_0_), channel_id=1, source_target_pairs={{0,2},{1,3},{2,0},{3,1},{4,6},{5,7},{6,4},{7,5},{8,10},{9,11},{10,... | collective-permute-start | bytes 1572872 | tf_op jit(solution)/shard_map/ppermute | solution.py:38
  34.0 25.8 %collective-permute-start.6 = (bf16[256,1024]{1,0:T(8,128)(2,1)S(1)}, bf16[256,1024]{1,0:T(8,128)(2,1)S(1)}, u32[]{:S(2)}, u32[]{:S(2)}) collective-permute-start(bf16[256,1024]{1,0:T(8,128)(2,1)S(1)} %collective-permute-done.5.refs_0_), channel_id=1, source_target_pairs={{0,2},{1,3},{2,0},{3,1},{4,6},{5,7},{6,4},{7,5},{8,10},{9,11},{10,... | collective-permute-start | bytes 1572872 | tf_op jit(solution)/shard_map/ppermute | solution.py:38
  37.4 28.1 %copy-start = (bf16[2048,512]{1,0:T(8,128)(2,1)S(1)}, bf16[2048,512]{1,0:T(8,128)(2,1)}, u32[]{:S(2)}) copy-start(bf16[2048,512]{1,0:T(8,128)(2,1)} %refs_2_.7) | copy-start | bytes 6291460
  37.7 41.8 %collective-permute-start.10 = (bf16[512,512]{1,0:T(8,128)(2,1)S(1)}, bf16[512,512]{1,0:T(8,128)(2,1)}, u32[]{:S(2)}, u32[]{:S(2)}) collective-permute-start(bf16[512,512]{1,0:T(8,128)(2,1)S(1)} %get-tuple-element.101.refs_0_), channel_id=1, source_target_pairs={{0,0},{1,1},{2,4},{3,5},{4,2},{5,3},{6,6},{7,7},{8,8},{9,9},{10,12... | collective-permute-start | bytes 1572872 | tf_op jit(solution)/shard_map/ppermute | solution.py:50
  39.3 40.2 %collective-permute-start.12 = (bf16[512,512]{1,0:T(8,128)(2,1)S(1)}, bf16[512,512]{1,0:T(8,128)(2,1)}, u32[]{:S(2)}, u32[]{:S(2)}) collective-permute-start(bf16[512,512]{1,0:T(8,128)(2,1)S(1)} %get-tuple-element.101.refs_0_), channel_id=1, source_target_pairs={{0,1},{1,0},{2,3},{3,2},{4,5},{5,4},{6,7},{7,6},{8,9},{9,8},{10,11... | collective-permute-start | bytes 1572872 | tf_op jit(solution)/shard_map/ppermute | solution.py:38
  47.7 29.0 %collective-permute-start.13 = (bf16[256,1024]{1,0:T(8,128)(2,1)}, bf16[256,1024]{1,0:T(8,128)(2,1)}, u32[]{:S(2)}, u32[]{:S(2)}) collective-permute-start(bf16[256,1024]{1,0:T(8,128)(2,1)} %collective-permute-done.4.refs_0_), channel_id=1, source_target_pairs={{0,2},{1,3},{2,0},{3,1},{4,6},{5,7},{6,4},{7,5},{8,10},{9,11},{10,... | collective-permute-start | bytes 1572872 | tf_op jit(solution)/shard_map/ppermute | solution.py:38
  60.6 18.9 %collective-permute-start.11 = (bf16[512,512]{1,0:T(8,128)(2,1)S(1)}, bf16[512,512]{1,0:T(8,128)(2,1)}, u32[]{:S(2)}, u32[]{:S(2)}) collective-permute-start(bf16[512,512]{1,0:T(8,128)(2,1)S(1)} %get-tuple-element.124.refs_0_), channel_id=1, source_target_pairs={{0,0},{1,1},{2,4},{3,5},{4,2},{5,3},{6,6},{7,7},{8,8},{9,9},{10,12... | collective-permute-start | bytes 1572872 | tf_op jit(solution)/shard_map/ppermute | solution.py:50
  63.4 16.2 %collective-permute-start.9 = (bf16[256,1024]{1,0:T(8,128)(2,1)}, bf16[256,1024]{1,0:T(8,128)(2,1)}, u32[]{:S(2)}, u32[]{:S(2)}) collective-permute-start(bf16[256,1024]{1,0:T(8,128)(2,1)} %collective-permute-done.7.refs_2_), channel_id=1, source_target_pairs={{0,2},{1,3},{2,0},{3,1},{4,6},{5,7},{6,4},{7,5},{8,10},{9,11},{10,... | collective-permute-start | bytes 1572872 | tf_op jit(solution)/shard_map/ppermute | solution.py:38
  79.6 3.5 %collective-permute-start.14 = (f32[128,1024]{1,0:T(8,128)S(1)}, f32[128,1024]{1,0:T(8,128)S(1)}, u32[]{:S(2)}, u32[]{:S(2)}) collective-permute-start(f32[128,1024]{1,0:T(8,128)S(1)} %get-tuple-element.104), channel_id=1, source_target_pairs={{0,8},{8,0},{16,24},{24,16},{1,9},{9,1},{17,25},{25,17},{2,10},{10... | collective-permute-start | bytes 1572872 | tf_op jit(solution)/shard_map/ppermute | solution.py:38
  79.6 3.4 %collective-permute-start.15 = (f32[128,1024]{1,0:T(8,128)S(1)}, f32[128,1024]{1,0:T(8,128)S(1)}, u32[]{:S(2)}, u32[]{:S(2)}) collective-permute-start(f32[128,1024]{1,0:T(8,128)S(1)} %get-tuple-element.105), channel_id=1, source_target_pairs={{0,8},{8,0},{16,24},{24,16},{1,9},{9,1},{17,25},{25,17},{2,10},{10... | collective-permute-start | bytes 1572872 | tf_op jit(solution)/shard_map/ppermute | solution.py:38
  80.1 2.9 %collective-permute-start.16 = (f32[128,1024]{1,0:T(8,128)S(1)}, f32[128,1024]{1,0:T(8,128)S(1)}, u32[]{:S(2)}, u32[]{:S(2)}) collective-permute-start(f32[128,1024]{1,0:T(8,128)S(1)} %get-tuple-element.106), channel_id=1, source_target_pairs={{0,8},{8,0},{16,24},{24,16},{1,9},{9,1},{17,25},{25,17},{2,10},{10... | collective-permute-start | bytes 1572872 | tf_op jit(solution)/shard_map/ppermute | solution.py:38
  83.1 10.1 %collective-permute-start.17 = (f32[128,1024]{1,0:T(8,128)S(1)}, f32[128,1024]{1,0:T(8,128)S(1)}, u32[]{:S(2)}, u32[]{:S(2)}) collective-permute-start(f32[128,1024]{1,0:T(8,128)S(1)} %get-tuple-element.113), channel_id=1, source_target_pairs={{0,8},{8,0},{16,24},{24,16},{1,9},{9,1},{17,25},{25,17},{2,10},{10... | collective-permute-start | bytes 1572872 | tf_op jit(solution)/shard_map/ppermute | solution.py:38
  83.6 18.6 %collective-permute-start.19 = (bf16[512,512]{1,0:T(8,128)(2,1)S(1)}, bf16[512,512]{1,0:T(8,128)(2,1)}, u32[]{:S(2)}, u32[]{:S(2)}) collective-permute-start(bf16[512,512]{1,0:T(8,128)(2,1)S(1)} %get-tuple-element.101.refs_0_), channel_id=1, source_target_pairs={{0,6},{1,7},{2,2},{3,3},{4,4},{5,5},{6,0},{7,1},{8,14},{9,15},{10,... | collective-permute-start | bytes 1572872 | tf_op jit(solution)/shard_map/ppermute | solution.py:50
  87.6 14.5 %collective-permute-start.20 = (bf16[512,512]{1,0:T(8,128)(2,1)S(1)}, bf16[512,512]{1,0:T(8,128)(2,1)S(1)}, u32[]{:S(2)}, u32[]{:S(2)}) collective-permute-start(bf16[512,512]{1,0:T(8,128)(2,1)S(1)} %get-tuple-element.124.refs_0_), channel_id=1, source_target_pairs={{0,1},{1,0},{2,3},{3,2},{4,5},{5,4},{6,7},{7,6},{8,9},{9,8},{10,11... | collective-permute-start | bytes 1572872 | tf_op jit(solution)/shard_map/ppermute | solution.py:38
  89.7 9.4 %collective-permute-start.21 = (f32[64,1024]{1,0:T(8,128)S(1)}, f32[64,1024]{1,0:T(8,128)}, u32[]{:S(2)}, u32[]{:S(2)}) collective-permute-start(f32[64,1024]{1,0:T(8,128)S(1)} %get-tuple-element.127), channel_id=1, source_target_pairs={{0,16},{8,24},{16,0},{24,8},{1,17},{9,25},{17,1},{25,9},{2,18},{10... | collective-permute-start | bytes 786440 | tf_op jit(solution)/shard_map/ppermute | solution.py:38
  93.9 10.9 %collective-permute-start.18 = (f32[64,1024]{1,0:T(8,128)S(1)}, f32[64,1024]{1,0:T(8,128)}, u32[]{:S(2)}, u32[]{:S(2)}) collective-permute-start(f32[64,1024]{1,0:T(8,128)S(1)} %get-tuple-element.123), channel_id=1, source_target_pairs={{0,16},{8,24},{16,0},{24,8},{1,17},{9,25},{17,1},{25,9},{2,18},{10... | collective-permute-start | bytes 786440 | tf_op jit(solution)/shard_map/ppermute | solution.py:38
  94.4 19.1 %collective-permute-start.27 = (bf16[512,512]{1,0:T(8,128)(2,1)S(1)}, bf16[512,512]{1,0:T(8,128)(2,1)}, u32[]{:S(2)}, u32[]{:S(2)}) collective-permute-start(bf16[512,512]{1,0:T(8,128)(2,1)S(1)} %get-tuple-element.124.refs_0_), channel_id=1, source_target_pairs={{0,6},{1,7},{2,2},{3,3},{4,4},{5,5},{6,0},{7,1},{8,14},{9,15},{10,... | collective-permute-start | bytes 1572872 | tf_op jit(solution)/shard_map/ppermute | solution.py:50
  99.1 14.4 %collective-permute-start.26 = (f32[64,1024]{1,0:T(8,128)}, f32[64,1024]{1,0:T(8,128)S(1)}, u32[]{:S(2)}, u32[]{:S(2)}) collective-permute-start(f32[64,1024]{1,0:T(8,128)} %get-tuple-element.138), channel_id=1, source_target_pairs={{0,16},{8,24},{16,0},{24,8},{1,17},{9,25},{17,1},{25,9},{2,18},{10... | collective-permute-start | bytes 786440 | tf_op jit(solution)/shard_map/ppermute | solution.py:38
  100.6 24.0 %copy-start.26 = (f32[64,1024]{1,0:T(8,128)S(1)}, f32[64,1024]{1,0:T(8,128)}, u32[]{:S(2)}) copy-start(f32[64,1024]{1,0:T(8,128)} %copy-done.25) | copy-start | bytes 786436
  102.2 22.5 %collective-permute-start.22 = (f32[64,1024]{1,0:T(8,128)S(1)}, f32[64,1024]{1,0:T(8,128)S(1)}, u32[]{:S(2)}, u32[]{:S(2)}) collective-permute-start(f32[64,1024]{1,0:T(8,128)S(1)} %add.115), channel_id=1, source_target_pairs={{0,4},{1,5},{2,6},{3,7},{4,0},{5,1},{6,2},{7,3},{8,12},{9,13},{10,... | collective-permute-start | bytes 786440 | tf_op jit(solution)/shard_map/ppermute | solution.py:38
  102.2 25.1 %copy-start.3 = (bf16[512,512]{1,0:T(8,128)(2,1)}, bf16[512,512]{1,0:T(8,128)(2,1)S(1)}, u32[]{:S(2)}) copy-start(bf16[512,512]{1,0:T(8,128)(2,1)S(1)} %collective-permute-done.20.refs_1_) | copy-start | bytes 1572868
  105.8 26.9 %copy-start.18 = (bf16[1,64,4096]{2,1,0:T(8,128)(2,1)S(1)}, bf16[1,64,4096]{2,1,0:T(8,128)(2,1)}, u32[]{:S(2)}) copy-start(bf16[1,64,4096]{2,1,0:T(8,128)(2,1)} %param.10) | copy-start | bytes 1572868
  105.8 26.9 %collective-permute-start.25 = (bf16[512,512]{1,0:T(8,128)(2,1)S(1)}, bf16[512,512]{1,0:T(8,128)(2,1)S(1)}, u32[]{:S(2)}, u32[]{:S(2)}) collective-permute-start(bf16[512,512]{1,0:T(8,128)(2,1)S(1)} %broadcast_select_fusion.1.refs_2_), channel_id=1, source_target_pairs={{0,1},{1,0},{2,3},{3,2},{4,5},{5,4},{6,7},{7,6},{8,9},{9,8},{10,11... | collective-permute-start | bytes 1572872 | tf_op jit(solution)/shard_map/ppermute | solution.py:38
  113.6 16.3 %collective-permute-start.28 = (f32[64,512]{1,0:T(8,128)S(1)}, f32[64,512]{1,0:T(8,128)S(1)}, u32[]{:S(2)}, u32[]{:S(2)}) collective-permute-start(f32[64,512]{1,0:T(8,128)S(1)} %get-tuple-element.166), channel_id=1, source_target_pairs={{0,2},{1,3},{2,0},{3,1},{4,6},{5,7},{6,4},{7,5},{8,10},{9,11},{10,... | collective-permute-start | bytes 393224 | tf_op jit(solution)/shard_map/ppermute | solution.py:38
  113.6 17.6 %collective-permute-start.29 = (f32[64,512]{1,0:T(8,128)S(1)}, f32[64,512]{1,0:T(8,128)S(1)}, u32[]{:S(2)}, u32[]{:S(2)}) collective-permute-start(f32[64,512]{1,0:T(8,128)S(1)} %get-tuple-element.165), channel_id=1, source_target_pairs={{0,2},{1,3},{2,0},{3,1},{4,6},{5,7},{6,4},{7,5},{8,10},{9,11},{10,... | collective-permute-start | bytes 393224 | tf_op jit(solution)/shard_map/ppermute | solution.py:38
  116.6 14.6 %collective-permute-start.23 = (f32[64,1024]{1,0:T(8,128)S(1)}, f32[64,1024]{1,0:T(8,128)S(1)}, u32[]{:S(2)}, u32[]{:S(2)}) collective-permute-start(f32[64,1024]{1,0:T(8,128)S(1)} %add.116), channel_id=1, source_target_pairs={{0,6},{1,7},{2,4},{3,5},{4,2},{5,3},{6,0},{7,1},{8,14},{9,15},{10,... | collective-permute-start | bytes 786440 | tf_op jit(solution)/shard_map/ppermute | solution.py:38
  124.7 8.0 %collective-permute-start.24 = (f32[64,1024]{1,0:T(8,128)S(1)}, f32[64,1024]{1,0:T(8,128)S(1)}, u32[]{:S(2)}, u32[]{:S(2)}) collective-permute-start(f32[64,1024]{1,0:T(8,128)S(1)} %copy-done.26), channel_id=1, source_target_pairs={{0,16},{8,24},{16,0},{24,8},{1,17},{9,25},{17,1},{25,9},{2,18},{10... | collective-permute-start | bytes 786440 | tf_op jit(solution)/shard_map/ppermute | solution.py:38
  134.3 9.3 %collective-permute-start.31 = (bf16[64,2048]{1,0:T(8,128)(2,1)S(1)}, bf16[64,2048]{1,0:T(8,128)(2,1)S(1)}, u32[]{:S(2)}, u32[]{:S(2)}) collective-permute-start(bf16[64,2048]{1,0:T(8,128)(2,1)S(1)} %get-tuple-element.151), channel_id=1, source_target_pairs={{0,2},{1,3},{2,0},{3,1},{4,6},{5,7},{6,4},{7,5},{8,10},{9,11},{10,... | collective-permute-start | bytes 786440 | tf_op jit(solution)/shard_map/ppermute | solution.py:38
  137.1 8.3 %collective-permute-start.32 = (bf16[64,2048]{1,0:T(8,128)(2,1)}, bf16[64,2048]{1,0:T(8,128)(2,1)}, u32[]{:S(2)}, u32[]{:S(2)}) collective-permute-start(bf16[64,2048]{1,0:T(8,128)(2,1)} %get-tuple-element.152), channel_id=1, source_target_pairs={{0,16},{8,24},{16,0},{24,8},{1,17},{9,25},{17,1},{25,9},{2,18},{10... | collective-permute-start | bytes 786440 | tf_op jit(solution)/shard_map/ppermute | solution.py:38
  138.6 10.3 %collective-permute-start.35 = (bf16[64,2048]{1,0:T(8,128)(2,1)}, bf16[64,2048]{1,0:T(8,128)(2,1)}, u32[]{:S(2)}, u32[]{:S(2)}) collective-permute-start(bf16[64,2048]{1,0:T(8,128)(2,1)} %get-tuple-element.152), channel_id=1, source_target_pairs={{0,8},{8,0},{16,24},{24,16},{1,9},{9,1},{17,25},{25,17},{2,10},{10... | collective-permute-start | bytes 786440 | tf_op jit(solution)/shard_map/ppermute | solution.py:38
  145.3 7.2 %collective-permute-start.33 = (bf16[64,2048]{1,0:T(8,128)(2,1)S(1)}, bf16[64,2048]{1,0:T(8,128)(2,1)}, u32[]{:S(2)}, u32[]{:S(2)}) collective-permute-start(bf16[64,2048]{1,0:T(8,128)(2,1)S(1)} %collective-permute-done.31), channel_id=1, source_target_pairs={{0,16},{8,24},{16,0},{24,8},{1,17},{9,25},{17,1},{25,9},{2,18},{10... | collective-permute-start | bytes 786440 | tf_op jit(solution)/shard_map/ppermute | solution.py:38
  146.9 5.6 %collective-permute-start.34 = (bf16[64,2048]{1,0:T(8,128)(2,1)S(1)}, bf16[64,2048]{1,0:T(8,128)(2,1)}, u32[]{:S(2)}, u32[]{:S(2)}) collective-permute-start(bf16[64,2048]{1,0:T(8,128)(2,1)S(1)} %collective-permute-done.31), channel_id=1, source_target_pairs={{0,8},{8,0},{16,24},{24,16},{1,9},{9,1},{17,25},{25,17},{2,10},{10... | collective-permute-start | bytes 786440 | tf_op jit(solution)/shard_map/ppermute | solution.py:38
  146.9 5.6 %collective-permute-start.36 = (bf16[64,2048]{1,0:T(8,128)(2,1)}, bf16[64,2048]{1,0:T(8,128)(2,1)}, u32[]{:S(2)}, u32[]{:S(2)}) collective-permute-start(bf16[64,2048]{1,0:T(8,128)(2,1)} %collective-permute-done.32), channel_id=1, source_target_pairs={{0,8},{8,0},{16,24},{24,16},{1,9},{9,1},{17,25},{25,17},{2,10},{10... | collective-permute-start | bytes 786440 | tf_op jit(solution)/shard_map/ppermute | solution.py:38
  147.4 14.0 %collective-permute-start.30 = (bf16[512,512]{1,0:T(8,128)(2,1)S(1)}, bf16[512,512]{1,0:T(8,128)(2,1)}, u32[]{:S(2)}, u32[]{:S(2)}) collective-permute-start(bf16[512,512]{1,0:T(8,128)(2,1)S(1)} %broadcast_select_fusion.refs_2_), channel_id=1, source_target_pairs={{0,1},{1,0},{2,3},{3,2},{4,5},{5,4},{6,7},{7,6},{8,9},{9,8},{10,11... | collective-permute-start | bytes 1572872 | tf_op jit(solution)/shard_map/ppermute | solution.py:38
  152.5 2.0 collective-permute-start.37
  157.7 15.1 %collective-permute-start.38 = (f32[256,512]{1,0:T(8,128)}, f32[256,512]{1,0:T(8,128)}, u32[]{:S(2)}, u32[]{:S(2)}) collective-permute-start(f32[256,512]{1,0:T(8,128)} %shard_map.103), channel_id=1, source_target_pairs={{0,2},{1,3},{2,0},{3,1},{4,6},{5,7},{6,4},{7,5},{8,10},{9,11},{10,... | collective-permute-start | bytes 1572872 | tf_op jit(solution)/shard_map/ppermute | solution.py:38
  165.8 17.7 %collective-permute-start.39 = (f32[256,512]{1,0:T(8,128)S(1)}, f32[256,512]{1,0:T(8,128)S(1)}, u32[]{:S(2)}, u32[]{:S(2)}) collective-permute-start(f32[256,512]{1,0:T(8,128)S(1)} %shard_map.101), channel_id=1, source_target_pairs={{0,2},{1,3},{2,0},{3,1},{4,6},{5,7},{6,4},{7,5},{8,10},{9,11},{10,... | collective-permute-start | bytes 1572872 | tf_op jit(solution)/shard_map/ppermute | solution.py:38
  185.1 2.7 %collective-permute-start.40 = (f32[64,4096]{1,0:T(8,128)S(1)}, f32[64,4096]{1,0:T(8,128)S(1)}, u32[]{:S(2)}, u32[]{:S(2)}) collective-permute-start(f32[64,4096]{1,0:T(8,128)S(1)} %fusion.22), channel_id=1, source_target_pairs={{0,8},{8,0},{16,24},{24,16},{1,9},{9,1},{17,25},{25,17},{2,10},{10... | collective-permute-start | bytes 3145736 | tf_op jit(solution)/shard_map/ppermute | solution.py:38
  190.9 8.4 %collective-permute-start.41 = (bf16[32,4096]{1,0:T(8,128)(2,1)S(1)}, bf16[32,4096]{1,0:T(8,128)(2,1)S(1)}, u32[]{:S(2)}, u32[]{:S(2)}) collective-permute-start(bf16[32,4096]{1,0:T(8,128)(2,1)S(1)} %fusion.3), channel_id=1, source_target_pairs={{0,16},{8,24},{16,0},{24,8},{1,17},{9,25},{17,1},{25,9},{2,18},{10... | collective-permute-start | bytes 786440 | tf_op jit(solution)/shard_map/ppermute | solution.py:38
  (25 other events, 102.5 us)

commit v4 on v3

--- a/solution.py
+++ b/solution.py
@@ -10,8 +10,13 @@
 HD = 256
 TILE = 256
 F32, BF16 = jnp.float32, jnp.bfloat16
-CHEAP = pl.CostEstimate(flops=1, bytes_accessed=1, transcendentals=0)
-SOME = pl.CostEstimate(flops=1, bytes_accessed=1_800_000, transcendentals=0)
+
+
+def cost(us):
+    return pl.CostEstimate(flops=1, bytes_accessed=int(1 + us * 3_500_000), transcendentals=0)
+
+
+CHEAP, SOME = cost(0), cost(0.5)
 
 
 class Line:
@@ -63,7 +68,7 @@
     return out
 
 
-def local(body, outs, *operands, scratch=(), cost=CHEAP, left=0):
+def local(body, outs, *operands, scratch=(), paced=CHEAP, left=0):
     vmem = pl.BlockSpec(memory_space=pltpu.VMEM)
     stay = pl.BlockSpec(memory_space=pltpu.HBM)
     return pl.pallas_call(
@@ -73,7 +78,7 @@
         + [vmem] * (len(operands) - 1 - left),
         out_specs=[vmem] * len(outs),
         scratch_shapes=list(scratch),
-        cost_estimate=cost,
+        cost_estimate=paced,
         compiler_params=pltpu.CompilerParams(vmem_limit_bytes=12 << 20),
     )(*operands)
 
@@ -139,11 +144,11 @@
     return local(
         body, [out, out], at, *flat, *downs, *before,
         scratch=[pltpu.VMEM((total, halves * depth), BF16), pltpu.SemaphoreType.DMA((halves,))],
-        cost=SOME, left=len(flat),
+        paced=SOME, left=len(flat),
     )
 
 
-def core_add(at, mine, theirs):
+def core_add(at, mine, theirs, sent=F32):
     rows, cols = mine.shape[0] // 2, mine.shape[1]
 
     def body(at_ref, mine_ref, theirs_ref, keep, send):
@@ -151,20 +156,20 @@
         one = mine_ref[:rows] + theirs_ref[:rows]
         two = mine_ref[rows:] + theirs_ref[rows:]
         keep[...] = jnp.where(first, one, two)
-        send[...] = jnp.where(first, two, one)
-
-    return local(body, [((rows, cols), F32)] * 2, at, mine, theirs)
+        send[...] = jnp.where(first, two, one).astype(sent)
+
+    return local(body, [((rows, cols), F32), ((rows, cols), sent)], at, mine, theirs)
 
 
 def norm_part(at, keep, came, others, stream, gain):
     rows, cols = keep.shape
     block = cols // 2
 
-    def body(at_ref, keep_ref, came_ref, q10, q11, q2, q3, stream_ref, gain_ref, near, far, resid):
+    def body(at_ref, keep_ref, came_ref, q1, q2, q3, stream_ref, gain_ref, near, far, resid):
         zat, xat = at_ref[0], at_ref[1]
         square = jnp.zeros((rows, 1), F32)
         starts = []
-        for m, ref in enumerate((None, (q10, q11), q2, q3)):
+        for m, ref in enumerate((None, q1, q2, q3)):
             for k in range(2):
                 start = pl.multiple_of(((zat ^ m) * 2 + (xat ^ k)) * block, block)
                 starts.append(start)
@@ -172,7 +177,7 @@
                 if m == 0:
                     add = keep_ref[:, here] + came_ref[:, here]
                 else:
-                    add = ref[k][...] if m == 1 else ref[:, here]
+                    add = ref[:, here]
                 value = stream_ref[:, pl.ds(start, block)].astype(F32) + add
                 square = square + jnp.sum(value * value, axis=-1, keepdims=True)
                 at = (2 * m + k) * block
@@ -192,37 +197,122 @@
     )
 
 
-def kv_part(at, rows, weights):
-    count, width = rows.shape
-    depth, cols = weights[0].shape
+def kv_part(at, rows, wk, wv, paced=CHEAP):
+    count, width = rows[0].shape
+    depth, cols = wk[0].shape
+    pieces, parts = len(rows), len(wk) + len(wv)
+    weights = [*wk, *wv]
+    total = pieces * count
 
     def body(at_ref, *refs):
-        (lhs, out, held, sems) = refs[4:]
-        loads = [pltpu.make_async_copy(refs[p], held.at[p], sems.at[p]) for p in range(4)]
-        for load in loads:
-            load.start()
+        out, stack, held, sems = refs[parts + pieces :]
+        copies = [
+            pltpu.make_async_copy(
+                refs[parts + i], stack.at[pl.ds(i * count, count)], sems.at[parts + i]
+            )
+            for i in range(pieces)
+        ]
+        loads = [pltpu.make_async_copy(refs[p], held.at[p], sems.at[p]) for p in range(parts)]
+        for copy in copies + loads:
+            copy.start()
+        for copy in copies:
+            copy.wait()
         for p, load in enumerate(loads):
             load.wait()
+            m = p % len(wk)
+            to = slice(0, total) if p < len(wk) else slice(total, 2 * total)
             for t in range(cols // TILE):
                 here = slice(t * TILE, (t + 1) * TILE)
                 part = jnp.dot(
-                    lhs[:, p * depth : (p + 1) * depth],
+                    stack[:, m * depth : (m + 1) * depth],
                     held[p, :, here],
                     preferred_element_type=F32,
                 )
-                out[:, here] = part if p == 0 else out[:, here] + part
+                out[to, here] = part if m == 0 else out[to, here] + part
 
     return local(
-        body, [((count, cols), F32)], at, *weights, rows,
-        scratch=[pltpu.VMEM((4, depth, cols), BF16), pltpu.SemaphoreType.DMA((4,))],
-        left=4,
+        body, [((2 * total, cols), F32)], at, *weights, *rows,
+        scratch=[
+            pltpu.VMEM((total, width), BF16),
+            pltpu.VMEM((parts, depth, cols), BF16),
+            pltpu.SemaphoreType.DMA((parts + pieces,)),
+        ],
+        left=parts + pieces, paced=paced,
     )[0]
 
 
-def woven(z, x, y, c, hidden, down, kv, stream, gain, rows):
+def softmax_part(at, own, came, queries, visible):
+    total, cols = own.shape[0] // 2, own.shape[1]
+    half = total // 2
+    dec = queries.shape[0]
+    heads = cols // HD
+
+    def body(at_ref, own_ref, one, two, query, seen, out, keys):
+        keys[:half] = (own_ref[:half] + one[:half]).astype(BF16)
+        keys[half:] = (own_ref[half:total] + two[:half]).astype(BF16)
+        for h in range(heads):
+            here = slice(h * HD, (h + 1) * HD)
+            scores = lax.dot_general(
+                query[:, here], keys[:, here], (((1,), (1,)), ((), ())),
+                preferred_element_type=F32,
+            ) / math.sqrt(HD)
+            scores = jnp.where(seen[...] > 0, scores, -jnp.inf)
+            expo = jnp.exp(scores - jnp.max(scores, axis=-1, keepdims=True))
+            weight = expo / jnp.sum(expo, axis=-1, keepdims=True)
+            out[h * dec : (h + 1) * dec] = weight.astype(BF16)
+
+    return local(
+        body, [((heads * dec, total), BF16)], at, own, *came, queries, visible,
+        scratch=[pltpu.VMEM((total, cols), BF16)], paced=CHEAP,
+    )[0]
+
+
+def out_part(at, own, came, weights, out_proj):
+    total, cols = own.shape[0] // 2, own.shape[1]
+    half = total // 2
+    heads = cols // HD
+    dec = weights.shape[0] // heads
+    rows = dec // 4
+    width = out_proj.shape[1]
+    wide = 512
+
+    def body(at_ref, own_ref, one, two, weight, proj, mine, theirs, values, attended, order):
+        values[:half] = (own_ref[total : total + half] + one[half:]).astype(BF16)
+        values[half:] = (own_ref[total + half :] + two[half:]).astype(BF16)
+        live = lax.broadcasted_iota(jnp.int32, (dec, HD), 0) < dec - at_ref[5]
+        for h in range(heads):
+            here = slice(h * HD, (h + 1) * HD)
+            value = jnp.dot(
+                weight[h * dec : (h + 1) * dec], values[:, here], preferred_element_type=F32
+            )
+            attended[:, here] = jnp.where(live, value, 0.0).astype(BF16)
+        first = at_ref[3] == 0
+        for i in range(2):
+            a = attended[(2 * i) * rows : (2 * i + 1) * rows]
+            b = attended[(2 * i + 1) * rows : (2 * i + 2) * rows]
+            order[i * rows : (i + 1) * rows] = jnp.where(first, a, b)
+            order[(2 + i) * rows : (3 + i) * rows] = jnp.where(first, b, a)
+
+        for t in range(width // wide):
+            here = slice(t * wide, (t + 1) * wide)
+            part = jnp.dot(order[...], proj[:, here], preferred_element_type=F32)
+            mine[:, here] = part[: 2 * rows]
+            theirs[:, here] = part[2 * rows :]
+
+    return local(
+        body, [((2 * rows, width), F32)] * 2, at, own, *came, weights, out_proj,
+        scratch=[
+            pltpu.VMEM((total, cols), BF16),
+            pltpu.VMEM((dec, cols), BF16),
+            pltpu.VMEM((dec, cols), BF16),
+        ],
+    )
+
+
+def woven(z, x, y, c, hidden, down, kv, stream, gain, rows, query, out_proj, visible, pad):
     E, O, X, Y = (lambda v: z.swap(v, 1)), z.cross, (lambda v: x.swap(v, 1)), (lambda v: y.swap(v, 1))
     C = lambda v: c.swap(v, 1)
-    at = jnp.stack([z.at, x.at, y.at, c.at]).astype(jnp.int32)
+    at = jnp.stack([z.at, x.at, y.at, c.at, z.at, pad]).astype(jnp.int32)
     inner = (z.at == 1) | (z.at == 2)
     half = hidden.shape[1] // 2
     ha, hb = hidden[:, :half], hidden[:, half:]
@@ -265,33 +355,35 @@
     q2 = z.swap(k2 + s2, 2)
     s1 = Y(s1)
 
-    (s3, fk, xv0), (s0,) = tick((s3, fk, xv0), (s0,))
+    (s3, fk, xv0), (s0, v, ov) = tick((s3, fk, xv0), (s0, v, ov))
     q3 = z.swap(k3 + s3, 3)
     s0 = Y(s0)
     kk = jnp.where(inner, ok, fk)
     xkk = X(kk)
 
-    (s1, fv), = tick((s1, fv))
-    q1 = k1 + s1
-    q1 = [z.swap(part, 1) for part in jnp.split(q1, 2, axis=1)]
+    (s1,), = tick((s1,))
+    q1 = z.swap(k1 + s1, 1)
+
     vv = jnp.where(inner, ov, fv)
-
-    (q2, q3, s0, xkk), q1, (vv,) = tick((q2, q3, s0, xkk), q1, (vv,))
     xvv = X(vv)
-    mine, other = norm_part(at, k0, s0, (*q1, q2, q3), stream, gain)
+    (q1, q2, q3, s0, xkk), = tick((q1, q2, q3, s0, xkk))
+    mine, other = norm_part(at, k0, s0, (q1, q2, q3), stream, gain)
     near, far = E(other), Y(mine)
-    (near, far), = tick((near, far))
+    (near, far, xvv), = tick((near, far, xvv))
     nearfar = Y(near)
     near2, mine2, far2 = C(near), C(mine), C(far)
-    (nearfar, near2, mine2, far2), = tick((nearfar, near2, mine2, far2))
-    pair = jnp.concatenate([near, near2, nearfar, C(nearfar)], axis=0)
-    own = [jnp.concatenate([mine, mine2, far, far2], axis=0)]
+    (near2,), = tick((near2,))
     wk, wv = (k, xk0, kk, xkk), (v, xv0, vv, xvv)
-    keys = E(kv_part(at, pair, wk))
-    values = kv_part(at, pair, wv)
-    (values,), (own,) = tick((values,), own)
-    values = E(values)
-    return kv_part(at, own, wk) + keys, kv_part(at, own, wv) + values
+    sums1 = E(kv_part(at, (near, near2), wk, wv))
+    nearfar2 = C(nearfar)
+    sums2 = kv_part(at, (nearfar, nearfar2), wk, wv, cost(1))
+    came = sums1, E(sums2)
+    (sums2,), own = tick((sums2,), (mine, mine2, far, far2))
+    sums = kv_part(at, own, wk, wv)
+    weight = softmax_part(at, sums, came, query, visible)
+    m, h = out_part(at, sums, came, weight, out_proj)
+    keep, send = core_add(at, m, C(h), BF16)
+    return (keep + Y(send).astype(F32)).astype(BF16)
 
 
 def on_device(
@@ -357,9 +449,10 @@
     visible = jnp.concatenate(places) < enc_len[0]
 
     if (nz, nx, ny) == (4, 2, 2):
-        keys, values = woven(
-            z, x, y, c, hidden, down_proj, kv_local, stream, final_gain[None], rows
-        )
+        return woven(
+            z, x, y, c, hidden, down_proj, kv_local, stream, final_gain[None], rows, queries[0],
+            out_proj, visible.astype(jnp.int32)[None], dec_pad[0],
+        )[None]
     else:
         hidden_slots = z.gather(halves)
         down_slots = x.gather(downs)

time: 201 us -> 201 us (level)
  matrix products: 4.73 us -> 0 us
  Pallas kernels: 27.3 us -> 31.6 us
  waiting for transfers between devices: 80.1 us -> 83.7 us
  other arithmetic: 7.92 us -> 5.06 us
    dot_general x6 -> x0, matrix products: 4.73 us -> none  [the longest x4 4.29 us: on_device(): dot = lambda a, b: jnp.dot(a, b, preferred_element_type=jnp.float32)]
    pallas_call x14 -> x16, Pallas kernels: 27.3 us -> 31.6 us  [local(): pl.pallas_call(body, out_shape=[jax.ShapeDtypeStruct(shape, kind) for sha...]
    ppermute x34 -> x33, waiting for transfers between devices: 72.6 us -> 76.9 us  [swap(): return lax.ppermute(value, self.name, pairs)]
    unnamed x65 -> x62, local copies, waits for them, and re-layouts: 10.3 us -> 11.7 us
    ppermute x34 -> x33, starting transfers between devices: 49.4 us -> 48.2 us  [swap(): return lax.ppermute(value, self.name, pairs)]
  transfers between devices with their start and end apart: 42 -> 41, of which waited for: 19 -> 16; matrix products, arithmetic and copies ran while one was open for 6% -> 4% of each run, Pallas kernels for 13% -> 14%
where the time goes in v4:
time: 201 us
  waiting for transfers between devices  83.7 us (42%)
  starting transfers between devices  63.4 us (32%)
  Pallas kernels  31.6 us (16%)
  local copies, waits for them, and re-layouts  14.8 us (7%)
  other arithmetic  5.06 us (3%)
    ppermute x33, waiting for transfers between devices, swap(): return lax.ppermute(value, self.name, pairs)  76.9 us
    ppermute x33, starting transfers between devices, swap(): return lax.ppermute(value, self.name, pairs)  48.2 us
    pallas_call x16, Pallas kernels, local(): pl.pallas_call(body, out_shape=[jax.ShapeDtypeStruct(shape, kind) for sha...  31.6 us
    ppermute x8, starting transfers between devices, turn(): return lax.ppermute(value, self.name, pairs)  15.2 us
    unnamed x62, local copies, waits for them, and re-layouts  11.7 us
    ppermute x8, waiting for transfers between devices, turn(): return lax.ppermute(value, self.name, pairs)  6.81 us
  transfers between devices with their start and end apart: 41, of which 16 were waited for; matrix products, arithmetic and copies ran while one was open for 4% of the time, Pallas kernels for 14%

profile of v4, /device:TPU:0, one launch (start us, length us, event | category | flops | bytes accessed | tf_op | source)
XLA Modules:
  0.0 200.6 jit_solution(14846176407082590373)
XLA Ops:
  0.0 2.9 %collective-permute-start.8 = (bf16[2048,512]{1,0:T(8,128)(2,1)}, bf16[2048,512]{1,0:T(8,128)(2,1)S(1)}, u32[]{:S(2)}, u32[]{:S(2)}) collective-permute-start(bf16[2048,512]{1,0:T(8,128)(2,1)} %refs_2_.7), channel_id=1, source_target_pairs={{0,1},{1,0},{2,3},{3,2},{4,5},{5,4},{6,7},{7,6},{8,9},{9,8},{10,11... | collective-permute-start | bytes 6291464 | tf_op jit(solution)/shard_map/ppermute | solution.py:43
  2.9 1.3 fusion.2
  4.2 1.6 collective-permute-start
  9.3 9.8 %collective-permute-done.refs_0_ = bf16[256,1024]{1,0:T(8,128)(2,1)S(1)} collective-permute-done((bf16[256,1024]{1,0:T(8,128)(2,1)S(1)}, bf16[256,1024]{1,0:T(8,128)(2,1)S(1)}, u32[]{:S(2)}, u32[]{:S(2)}) %collective-permute-start) | collective-permute-done | bytes 524320 | tf_op jit(solution)/shard_map/ppermute | solution.py:43
  19.1 1.4 collective-permute-start.4
  20.6 8.3 %collective-permute-done.1.refs_1_ = bf16[256,1024]{1,0:T(8,128)(2,1)S(1)} collective-permute-done((bf16[256,1024]{1,0:T(8,128)(2,1)S(1)}, bf16[256,1024]{1,0:T(8,128)(2,1)S(1)}, u32[]{:S(2)}, u32[]{:S(2)}) %collective-permute-start.1) | collective-permute-done | bytes 524320 | tf_op jit(solution)/shard_map/ppermute | solution.py:43
  28.9 1.5 collective-permute-start.7
  30.4 3.7 %collective-permute-start.3 = (bf16[256,1024]{1,0:T(8,128)(2,1)S(1)}, bf16[256,1024]{1,0:T(8,128)(2,1)S(1)}, u32[]{:S(2)}, u32[]{:S(2)}) collective-permute-start(bf16[256,1024]{1,0:T(8,128)(2,1)S(1)} %collective-permute-done.2.refs_0_), channel_id=1, source_target_pairs={{0,2},{1,3},{2,0},{3,1},{4,6},{5,7},{6,4},{7,5},{8,10},{9,11},{10,... | collective-permute-start | bytes 1572872 | tf_op jit(solution)/shard_map/ppermute | solution.py:43
  34.0 1.8 collective-permute-start.6
  35.9 1.5 fusion.1
  37.7 1.6 collective-permute-start.10
  39.8 7.1 %collective-permute-done.3.refs_1_ = bf16[256,1024]{1,0:T(8,128)(2,1)S(1)} collective-permute-done((bf16[256,1024]{1,0:T(8,128)(2,1)S(1)}, bf16[256,1024]{1,0:T(8,128)(2,1)S(1)}, u32[]{:S(2)}, u32[]{:S(2)}) %collective-permute-start.3) | collective-permute-done | bytes 524320 | tf_op jit(solution)/shard_map/ppermute | solution.py:43
  47.7 12.1 %collective-permute-start.13 = (bf16[256,1024]{1,0:T(8,128)(2,1)}, bf16[256,1024]{1,0:T(8,128)(2,1)}, u32[]{:S(2)}, u32[]{:S(2)}) collective-permute-start(bf16[256,1024]{1,0:T(8,128)(2,1)} %collective-permute-done.4.refs_0_), channel_id=1, source_target_pairs={{0,2},{1,3},{2,0},{3,1},{4,6},{5,7},{6,4},{7,5},{8,10},{9,11},{10,... | collective-permute-start | bytes 1572872 | tf_op jit(solution)/shard_map/ppermute | solution.py:43
  60.6 1.4 collective-permute-start.11
  62.1 1.3 copy-done.1
  63.4 2.0 %collective-permute-start.9 = (bf16[256,1024]{1,0:T(8,128)(2,1)}, bf16[256,1024]{1,0:T(8,128)(2,1)}, u32[]{:S(2)}, u32[]{:S(2)}) collective-permute-start(bf16[256,1024]{1,0:T(8,128)(2,1)} %collective-permute-done.7.refs_2_), channel_id=1, source_target_pairs={{0,2},{1,3},{2,0},{3,1},{4,6},{5,7},{6,4},{7,5},{8,10},{9,11},{10,... | collective-permute-start | bytes 1572872 | tf_op jit(solution)/shard_map/ppermute | solution.py:43
  66.2 1.6 copy-done.2
  69.8 2.4 %shard_map.93 = (f32[128,1024]{1,0:T(8,128)S(1)}, f32[128,1024]{1,0:T(8,128)S(1)}) custom-call(s32[6]{0:T(128)S(1)} %stack.20.at_ref, bf16[256,1024]{1,0:T(8,128)(2,1)S(1)} %copy-done.9, bf16[256,1024]{1,0:T(8,128)(2,1)S(1)} %copy-done.7, bf16[2048,512]{1,0:T(8,128)(2,1)S(1)} %copy-done, bf16[2048,512]{1,0:T(8,128)(2,1)S(1)} %copy-done.2), custom_call_target="tpu_custom_call" | custom-call | flops 1 | bytes 1750001 | tf_op jit(solution)/shard_map/pallas_call | solution.py:74
  72.3 2.5 %shard_map.92 = (f32[128,1024]{1,0:T(8,128)S(1)}, f32[128,1024]{1,0:T(8,128)S(1)}) custom-call(s32[6]{0:T(128)S(1)} %stack.20.at_ref, bf16[256,1024]{1,0:T(8,128)(2,1)} %collective-permute-done.4.refs_0_, bf16[256,1024]{1,0:T(8,128)(2,1)S(1)} %copy-done.13, bf16[256,1024]{1,0:T(8,128)(2,1)} %collective-permute-done.7.refs_2_, ...), custom_call_target="tpu_custom_call" | custom-call | flops 1 | bytes 1750001 | tf_op jit(solution)/shard_map/pallas_call | solution.py:74
  74.8 2.5 %shard_map.91 = (f32[128,1024]{1,0:T(8,128)S(1)}, f32[128,1024]{1,0:T(8,128)S(1)}) custom-call(s32[6]{0:T(128)S(1)} %stack.20.at_ref, bf16[256,1024]{1,0:T(8,128)(2,1)S(1)} %copy-done.18, bf16[256,1024]{1,0:T(8,128)(2,1)S(1)} %copy-done.22, bf16[2048,512]{1,0:T(8,128)(2,1)S(1)} %copy-done, bf16[2048,512]{1,0:T(8,128)(2,1)S(1)} %copy-done.2), custom_call_target="tpu_custom_call" | custom-call | flops 1 | bytes 1750001 | tf_op jit(solution)/shard_map/pallas_call | solution.py:74
  77.3 2.8 %shard_map.94 = (f32[128,1024]{1,0:T(8,128)S(1)}, f32[128,1024]{1,0:T(8,128)S(1)}) custom-call(s32[6]{0:T(128)S(1)} %stack.20.at_ref, bf16[256,1024]{1,0:T(8,128)(2,1)S(1)} %copy-done.20, bf16[256,1024]{1,0:T(8,128)(2,1)} %collective-permute-done.13.refs_1_, bf16[2048,512]{1,0:T(8,128)(2,1)S(1)} %copy-done, bf16[2048,512]{1,0:T(8,128)(2,1)S(1)} %copy-done.2), custom_call_target="tpu_custom_call" | custom-call | flops 1 | bytes 1750001 | tf_op jit(solution)/shard_map/pallas_call | solution.py:74
  80.9 2.8 %shard_map.95 = (f32[128,1024]{1,0:T(8,128)S(1)}, f32[128,1024]{1,0:T(8,128)S(1)}) custom-call(s32[6]{0:T(128)S(1)} %stack.20.at_ref, bf16[256,1024]{1,0:T(8,128)(2,1)S(1)} %copy-done.11, bf16[256,1024]{1,0:T(8,128)(2,1)} %collective-permute-done.9.refs_1_, bf16[2048,512]{1,0:T(8,128)(2,1)S(1)} %copy-done, bf16[2048,512]{1,0:T(8,128)(2,1)S(1)} %copy-done.2, ...), custom_call_target="tpu_custom_call" | custom-call | flops 1 | bytes 1750001 | tf_op jit(solution)/shard_map/pallas_call | solution.py:74
  84.2 3.4 %collective-permute-start.19 = (bf16[512,512]{1,0:T(8,128)(2,1)S(1)}, bf16[512,512]{1,0:T(8,128)(2,1)}, u32[]{:S(2)}, u32[]{:S(2)}) collective-permute-start(bf16[512,512]{1,0:T(8,128)(2,1)S(1)} %get-tuple-element.102.refs_0_), channel_id=1, source_target_pairs={{0,6},{1,7},{2,2},{3,3},{4,4},{5,5},{6,0},{7,1},{8,14},{9,15},{10,... | collective-permute-start | bytes 1572872 | tf_op jit(solution)/shard_map/ppermute | solution.py:55
  87.6 1.4 collective-permute-start.20
  89.7 1.6 collective-permute-start.21
  94.4 4.6 %collective-permute-done.21 = f32[64,1024]{1,0:T(8,128)S(1)} collective-permute-done((f32[64,1024]{1,0:T(8,128)S(1)}, f32[64,1024]{1,0:T(8,128)S(1)}, u32[]{:S(2)}, u32[]{:S(2)}) %collective-permute-start.21) | collective-permute-done | bytes 262176 | tf_op jit(solution)/shard_map/ppermute | solution.py:43
  99.0 1.5 collective-permute-start.22
  100.5 4.5 %collective-permute-start.28 = (bf16[512,512]{1,0:T(8,128)(2,1)S(1)}, bf16[512,512]{1,0:T(8,128)(2,1)}, u32[]{:S(2)}, u32[]{:S(2)}) collective-permute-start(bf16[512,512]{1,0:T(8,128)(2,1)S(1)} %get-tuple-element.142.refs_4_), channel_id=1, source_target_pairs={{0,6},{1,7},{2,2},{3,3},{4,4},{5,5},{6,0},{7,1},{8,14},{9,15},{10,... | collective-permute-start | bytes 1572872 | tf_op jit(solution)/shard_map/ppermute | solution.py:55
  107.2 1.4 collective-permute-start.25
  108.7 2.1 %collective-permute-start.23 = (f32[64,1024]{1,0:T(8,128)S(1)}, f32[64,1024]{1,0:T(8,128)S(1)}, u32[]{:S(2)}, u32[]{:S(2)}) collective-permute-start(f32[64,1024]{1,0:T(8,128)S(1)} %add.93), channel_id=1, source_target_pairs={{0,2},{1,3},{2,0},{3,1},{4,6},{5,7},{6,4},{7,5},{8,10},{9,11},{10,... | collective-permute-start | bytes 786440 | tf_op jit(solution)/shard_map/ppermute | solution.py:43
  110.8 1.1 broadcast_select_fusion.1.refs_2_
  112.5 6.8 %collective-permute-done.28 = bf16[512,512]{1,0:T(8,128)(2,1)} collective-permute-done((bf16[512,512]{1,0:T(8,128)(2,1)S(1)}, bf16[512,512]{1,0:T(8,128)(2,1)}, u32[]{:S(2)}, u32[]{:S(2)}) %collective-permute-start.28) | collective-permute-done | bytes 524320 | tf_op jit(solution)/shard_map/ppermute | solution.py:55
  120.0 1.1 broadcast_select_fusion.refs_6_
  121.1 10.8 %collective-permute-done.24.q2 = f32[64,1024]{1,0:T(8,128)S(1)} collective-permute-done((f32[64,1024]{1,0:T(8,128)S(1)}, f32[64,1024]{1,0:T(8,128)S(1)}, u32[]{:S(2)}, u32[]{:S(2)}) %collective-permute-start.24) | collective-permute-done | bytes 262176 | tf_op jit(solution)/shard_map/ppermute | solution.py:43
  133.4 5.6 %collective-permute-start.29 = (bf16[64,2048]{1,0:T(8,128)(2,1)S(1)}, bf16[64,2048]{1,0:T(8,128)(2,1)S(1)}, u32[]{:S(2)}, u32[]{:S(2)}) collective-permute-start(bf16[64,2048]{1,0:T(8,128)(2,1)S(1)} %get-tuple-element.150), channel_id=1, source_target_pairs={{0,2},{1,3},{2,0},{3,1},{4,6},{5,7},{6,4},{7,5},{8,10},{9,11},{10,... | collective-permute-start | bytes 786440 | tf_op jit(solution)/shard_map/ppermute | solution.py:43
  139.9 5.7 %collective-permute-done.31.refs_7_ = bf16[512,512]{1,0:T(8,128)(2,1)S(1)} collective-permute-done((bf16[512,512]{1,0:T(8,128)(2,1)S(1)}, bf16[512,512]{1,0:T(8,128)(2,1)S(1)}, u32[]{:S(2)}, u32[]{:S(2)}) %collective-permute-start.31) | collective-permute-done | bytes 524320 | tf_op jit(solution)/shard_map/ppermute | solution.py:43
  145.6 1.2 collective-permute-done.30.refs_10_
  148.6 6.1 %collective-permute-done.32.refs_8_ = bf16[64,2048]{1,0:T(8,128)(2,1)S(1)} collective-permute-done((bf16[64,2048]{1,0:T(8,128)(2,1)S(1)}, bf16[64,2048]{1,0:T(8,128)(2,1)S(1)}, u32[]{:S(2)}, u32[]{:S(2)}) %collective-permute-start.32) | collective-permute-done | bytes 262176 | tf_op jit(solution)/shard_map/ppermute | solution.py:43
  154.7 3.6 %shard_map.103 = f32[256,512]{1,0:T(8,128)} custom-call(s32[6]{0:T(128)S(1)} %stack.20.at_ref, bf16[512,512]{1,0:T(8,128)(2,1)S(1)} %get-tuple-element.102.refs_0_, bf16[512,512]{1,0:T(8,128)(2,1)} %collective-permute-done.12.refs_1_, bf16[512,512]{1,0:T(8,128)(2,1)S(1)} %broadcast_select_fusion.1.refs_2_, ...), custom_call_target="tpu_custom_call" | custom-call | flops 1 | bytes 1 | tf_op jit(solution)/shard_map/pallas_call | solution.py:74
  159.0 3.6 %shard_map.101 = f32[256,512]{1,0:T(8,128)} custom-call(s32[6]{0:T(128)S(1)} %stack.20.at_ref, bf16[512,512]{1,0:T(8,128)(2,1)S(1)} %get-tuple-element.102.refs_0_, bf16[512,512]{1,0:T(8,128)(2,1)} %collective-permute-done.12.refs_1_, bf16[512,512]{1,0:T(8,128)(2,1)S(1)} %broadcast_select_fusion.1.refs_2_, ...), custom_call_target="tpu_custom_call" | custom-call | flops 1 | bytes 3500001 | tf_op jit(solution)/shard_map/pallas_call | solution.py:74
  162.6 1.4 collective-permute-start.38
  168.3 3.7 %shard_map.102.own_ref = f32[512,512]{1,0:T(8,128)S(1)} custom-call(s32[6]{0:T(128)S(1)} %stack.20.at_ref, bf16[512,512]{1,0:T(8,128)(2,1)S(1)} %get-tuple-element.102.refs_0_, bf16[512,512]{1,0:T(8,128)(2,1)} %collective-permute-done.12.refs_1_, bf16[512,512]{1,0:T(8,128)(2,1)S(1)} %broadcast_select_fusion.1.refs_2_, ...), custom_call_target="tpu_custom_call" | custom-call | flops 1 | bytes 1 | tf_op jit(solution)/shard_map/pallas_call | solution.py:74
  172.0 1.3 collective-permute-done.37.one
  173.4 10.9 %collective-permute-done.38.two = f32[256,512]{1,0:T(8,128)} collective-permute-done((f32[256,512]{1,0:T(8,128)}, f32[256,512]{1,0:T(8,128)}, u32[]{:S(2)}, u32[]{:S(2)}) %collective-permute-start.38) | collective-permute-done | bytes 524320 | tf_op jit(solution)/shard_map/ppermute | solution.py:43
  184.2 1.6 shard_map.104.weight
  185.9 2.1 %shard_map.105 = (f32[64,4096]{1,0:T(8,128)S(1)}, f32[64,4096]{1,0:T(8,128)S(1)}) custom-call(s32[6]{0:T(128)S(1)} %stack.20.at_ref, f32[512,512]{1,0:T(8,128)S(1)} %shard_map.102.own_ref, f32[256,512]{1,0:T(8,128)} %collective-permute-done.37.one, f32[256,512]{1,0:T(8,128)} %collective-permute-done.38.two, bf16[256,256]{1,0:T(8,128)(2,1)S(1)} %shard_map.104.weight, ...), custom_call_target="tpu_custom_call" | custom-call | flops 1 | bytes 1 | tf_op jit(solution)/shard_map/pallas_call | solution.py:74
  188.0 2.6 %collective-permute-done.39.theirs_ref = f32[64,4096]{1,0:T(8,128)S(1)} collective-permute-done((f32[64,4096]{1,0:T(8,128)S(1)}, f32[64,4096]{1,0:T(8,128)S(1)}, u32[]{:S(2)}, u32[]{:S(2)}) %collective-permute-start.39) | collective-permute-done | bytes 1048608 | tf_op jit(solution)/shard_map/ppermute | solution.py:43
  192.4 7.4 %collective-permute-done.40 = bf16[32,4096]{1,0:T(8,128)(2,1)S(1)} collective-permute-done((bf16[32,4096]{1,0:T(8,128)(2,1)S(1)}, bf16[32,4096]{1,0:T(8,128)(2,1)S(1)}, u32[]{:S(2)}, u32[]{:S(2)}) %collective-permute-start.40) | collective-permute-done | bytes 262176 | tf_op jit(solution)/shard_map/ppermute | solution.py:43
  (126 shorter events, 27.5 us)
Async XLA Ops:
  0.0 35.9 %copy-start.28 = (bf16[512,2,512]{2,1,0:T(2,128)(2,1)S(1)}, bf16[512,2,512]{2,1,0:T(2,128)(2,1)}, u32[]{:S(2)}) copy-start(bf16[512,2,512]{2,1,0:T(2,128)(2,1)} %param.13) | copy-start | bytes 3145732
  0.0 62.0 %collective-permute-start.8 = (bf16[2048,512]{1,0:T(8,128)(2,1)}, bf16[2048,512]{1,0:T(8,128)(2,1)S(1)}, u32[]{:S(2)}, u32[]{:S(2)}) collective-permute-start(bf16[2048,512]{1,0:T(8,128)(2,1)} %refs_2_.7), channel_id=1, source_target_pairs={{0,1},{1,0},{2,3},{3,2},{4,5},{5,4},{6,7},{7,6},{8,9},{9,8},{10,11... | collective-permute-start | bytes 6291464 | tf_op jit(solution)/shard_map/ppermute | solution.py:43
  4.2 14.9 %collective-permute-start = (bf16[256,1024]{1,0:T(8,128)(2,1)S(1)}, bf16[256,1024]{1,0:T(8,128)(2,1)S(1)}, u32[]{:S(2)}, u32[]{:S(2)}) collective-permute-start(bf16[256,1024]{1,0:T(8,128)(2,1)S(1)} %get-tuple-element.166.refs_0_), channel_id=1, source_target_pairs={{0,2},{1,3},{2,0},{3,1},{4,6},{5,7},{6,4},{7,5},{8,10},{9,11},{10,... | collective-permute-start | bytes 1572872 | tf_op jit(solution)/shard_map/ppermute | solution.py:43
  5.9 23.0 %collective-permute-start.1 = (bf16[256,1024]{1,0:T(8,128)(2,1)S(1)}, bf16[256,1024]{1,0:T(8,128)(2,1)S(1)}, u32[]{:S(2)}, u32[]{:S(2)}) collective-permute-start(bf16[256,1024]{1,0:T(8,128)(2,1)S(1)} %get-tuple-element.165.refs_1_), channel_id=1, source_target_pairs={{0,2},{1,3},{2,0},{3,1},{4,6},{5,7},{6,4},{7,5},{8,10},{9,11},{10,... | collective-permute-start | bytes 1572872 | tf_op jit(solution)/shard_map/ppermute | solution.py:43
  6.3 24.1 %collective-permute-start.2 = (bf16[256,1024]{1,0:T(8,128)(2,1)S(1)}, bf16[256,1024]{1,0:T(8,128)(2,1)S(1)}, u32[]{:S(2)}, u32[]{:S(2)}) collective-permute-start(bf16[256,1024]{1,0:T(8,128)(2,1)S(1)} %get-tuple-element.166.refs_0_), channel_id=1, source_target_pairs={{0,0},{1,1},{2,4},{3,5},{4,2},{5,3},{6,6},{7,7},{8,8},{9,9},{10,12... | collective-permute-start | bytes 1572872 | tf_op jit(solution)/shard_map/ppermute | solution.py:55
  7.8 26.3 %collective-permute-start.5 = (bf16[256,1024]{1,0:T(8,128)(2,1)S(1)}, bf16[256,1024]{1,0:T(8,128)(2,1)S(1)}, u32[]{:S(2)}, u32[]{:S(2)}) collective-permute-start(bf16[256,1024]{1,0:T(8,128)(2,1)S(1)} %get-tuple-element.165.refs_1_), channel_id=1, source_target_pairs={{0,0},{1,1},{2,4},{3,5},{4,2},{5,3},{6,6},{7,7},{8,8},{9,9},{10,12... | collective-permute-start | bytes 1572872 | tf_op jit(solution)/shard_map/ppermute | solution.py:55
  19.1 18.2 %copy-start.17 = (bf16[256,1024]{1,0:T(8,128)(2,1)}, bf16[256,1024]{1,0:T(8,128)(2,1)S(1)}, u32[]{:S(2)}) copy-start(bf16[256,1024]{1,0:T(8,128)(2,1)S(1)} %collective-permute-done.refs_0_) | copy-start | bytes 1572868
  19.1 18.6 %collective-permute-start.4 = (bf16[256,1024]{1,0:T(8,128)(2,1)S(1)}, bf16[256,1024]{1,0:T(8,128)(2,1)}, u32[]{:S(2)}, u32[]{:S(2)}) collective-permute-start(bf16[256,1024]{1,0:T(8,128)(2,1)S(1)} %collective-permute-done.refs_0_), channel_id=1, source_target_pairs={{0,0},{1,1},{2,4},{3,5},{4,2},{5,3},{6,6},{7,7},{8,8},{9,9},{10,12... | collective-permute-start | bytes 1572872 | tf_op jit(solution)/shard_map/ppermute | solution.py:55
  28.9 10.4 %collective-permute-start.7 = (bf16[256,1024]{1,0:T(8,128)(2,1)S(1)}, bf16[256,1024]{1,0:T(8,128)(2,1)}, u32[]{:S(2)}, u32[]{:S(2)}) collective-permute-start(bf16[256,1024]{1,0:T(8,128)(2,1)S(1)} %collective-permute-done.1.refs_1_), channel_id=1, source_target_pairs={{0,0},{1,1},{2,4},{3,5},{4,2},{5,3},{6,6},{7,7},{8,8},{9,9},{10,12... | collective-permute-start | bytes 1572872 | tf_op jit(solution)/shard_map/ppermute | solution.py:55
  30.4 16.5 %collective-permute-start.3 = (bf16[256,1024]{1,0:T(8,128)(2,1)S(1)}, bf16[256,1024]{1,0:T(8,128)(2,1)S(1)}, u32[]{:S(2)}, u32[]{:S(2)}) collective-permute-start(bf16[256,1024]{1,0:T(8,128)(2,1)S(1)} %collective-permute-done.2.refs_0_), channel_id=1, source_target_pairs={{0,2},{1,3},{2,0},{3,1},{4,6},{5,7},{6,4},{7,5},{8,10},{9,11},{10,... | collective-permute-start | bytes 1572872 | tf_op jit(solution)/shard_map/ppermute | solution.py:43
  34.0 25.8 %collective-permute-start.6 = (bf16[256,1024]{1,0:T(8,128)(2,1)S(1)}, bf16[256,1024]{1,0:T(8,128)(2,1)S(1)}, u32[]{:S(2)}, u32[]{:S(2)}) collective-permute-start(bf16[256,1024]{1,0:T(8,128)(2,1)S(1)} %collective-permute-done.5.refs_0_), channel_id=1, source_target_pairs={{0,2},{1,3},{2,0},{3,1},{4,6},{5,7},{6,4},{7,5},{8,10},{9,11},{10,... | collective-permute-start | bytes 1572872 | tf_op jit(solution)/shard_map/ppermute | solution.py:43
  37.4 28.8 %copy-start = (bf16[2048,512]{1,0:T(8,128)(2,1)S(1)}, bf16[2048,512]{1,0:T(8,128)(2,1)}, u32[]{:S(2)}) copy-start(bf16[2048,512]{1,0:T(8,128)(2,1)} %refs_2_.7) | copy-start | bytes 6291460
  37.7 42.5 %collective-permute-start.10 = (bf16[512,512]{1,0:T(8,128)(2,1)S(1)}, bf16[512,512]{1,0:T(8,128)(2,1)}, u32[]{:S(2)}, u32[]{:S(2)}) collective-permute-start(bf16[512,512]{1,0:T(8,128)(2,1)S(1)} %get-tuple-element.102.refs_0_), channel_id=1, source_target_pairs={{0,0},{1,1},{2,4},{3,5},{4,2},{5,3},{6,6},{7,7},{8,8},{9,9},{10,12... | collective-permute-start | bytes 1572872 | tf_op jit(solution)/shard_map/ppermute | solution.py:55
  39.3 40.9 %collective-permute-start.12 = (bf16[512,512]{1,0:T(8,128)(2,1)S(1)}, bf16[512,512]{1,0:T(8,128)(2,1)}, u32[]{:S(2)}, u32[]{:S(2)}) collective-permute-start(bf16[512,512]{1,0:T(8,128)(2,1)S(1)} %get-tuple-element.102.refs_0_), channel_id=1, source_target_pairs={{0,1},{1,0},{2,3},{3,2},{4,5},{5,4},{6,7},{7,6},{8,9},{9,8},{10,11... | collective-permute-start | bytes 1572872 | tf_op jit(solution)/shard_map/ppermute | solution.py:43
  47.7 29.6 %collective-permute-start.13 = (bf16[256,1024]{1,0:T(8,128)(2,1)}, bf16[256,1024]{1,0:T(8,128)(2,1)}, u32[]{:S(2)}, u32[]{:S(2)}) collective-permute-start(bf16[256,1024]{1,0:T(8,128)(2,1)} %collective-permute-done.4.refs_0_), channel_id=1, source_target_pairs={{0,2},{1,3},{2,0},{3,1},{4,6},{5,7},{6,4},{7,5},{8,10},{9,11},{10,... | collective-permute-start | bytes 1572872 | tf_op jit(solution)/shard_map/ppermute | solution.py:43
  60.6 19.6 %collective-permute-start.11 = (bf16[512,512]{1,0:T(8,128)(2,1)S(1)}, bf16[512,512]{1,0:T(8,128)(2,1)}, u32[]{:S(2)}, u32[]{:S(2)}) collective-permute-start(bf16[512,512]{1,0:T(8,128)(2,1)S(1)} %get-tuple-element.142.refs_4_), channel_id=1, source_target_pairs={{0,0},{1,1},{2,4},{3,5},{4,2},{5,3},{6,6},{7,7},{8,8},{9,9},{10,12... | collective-permute-start | bytes 1572872 | tf_op jit(solution)/shard_map/ppermute | solution.py:55
  63.4 16.9 %collective-permute-start.9 = (bf16[256,1024]{1,0:T(8,128)(2,1)}, bf16[256,1024]{1,0:T(8,128)(2,1)}, u32[]{:S(2)}, u32[]{:S(2)}) collective-permute-start(bf16[256,1024]{1,0:T(8,128)(2,1)} %collective-permute-done.7.refs_2_), channel_id=1, source_target_pairs={{0,2},{1,3},{2,0},{3,1},{4,6},{5,7},{6,4},{7,5},{8,10},{9,11},{10,... | collective-permute-start | bytes 1572872 | tf_op jit(solution)/shard_map/ppermute | solution.py:43
  80.2 3.5 %collective-permute-start.14 = (f32[128,1024]{1,0:T(8,128)S(1)}, f32[128,1024]{1,0:T(8,128)S(1)}, u32[]{:S(2)}, u32[]{:S(2)}) collective-permute-start(f32[128,1024]{1,0:T(8,128)S(1)} %get-tuple-element.105), channel_id=1, source_target_pairs={{0,8},{8,0},{16,24},{24,16},{1,9},{9,1},{17,25},{25,17},{2,10},{10... | collective-permute-start | bytes 1572872 | tf_op jit(solution)/shard_map/ppermute | solution.py:43
  80.3 3.4 %collective-permute-start.15 = (f32[128,1024]{1,0:T(8,128)S(1)}, f32[128,1024]{1,0:T(8,128)S(1)}, u32[]{:S(2)}, u32[]{:S(2)}) collective-permute-start(f32[128,1024]{1,0:T(8,128)S(1)} %get-tuple-element.106), channel_id=1, source_target_pairs={{0,8},{8,0},{16,24},{24,16},{1,9},{9,1},{17,25},{25,17},{2,10},{10... | collective-permute-start | bytes 1572872 | tf_op jit(solution)/shard_map/ppermute | solution.py:43
  80.8 2.9 %collective-permute-start.16 = (f32[128,1024]{1,0:T(8,128)S(1)}, f32[128,1024]{1,0:T(8,128)S(1)}, u32[]{:S(2)}, u32[]{:S(2)}) collective-permute-start(f32[128,1024]{1,0:T(8,128)S(1)} %get-tuple-element.107), channel_id=1, source_target_pairs={{0,8},{8,0},{16,24},{24,16},{1,9},{9,1},{17,25},{25,17},{2,10},{10... | collective-permute-start | bytes 1572872 | tf_op jit(solution)/shard_map/ppermute | solution.py:43
  83.7 9.4 %collective-permute-start.17 = (f32[128,1024]{1,0:T(8,128)S(1)}, f32[128,1024]{1,0:T(8,128)S(1)}, u32[]{:S(2)}, u32[]{:S(2)}) collective-permute-start(f32[128,1024]{1,0:T(8,128)S(1)} %get-tuple-element.114), channel_id=1, source_target_pairs={{0,8},{8,0},{16,24},{24,16},{1,9},{9,1},{17,25},{25,17},{2,10},{10... | collective-permute-start | bytes 1572872 | tf_op jit(solution)/shard_map/ppermute | solution.py:43
  84.2 21.8 %collective-permute-start.19 = (bf16[512,512]{1,0:T(8,128)(2,1)S(1)}, bf16[512,512]{1,0:T(8,128)(2,1)}, u32[]{:S(2)}, u32[]{:S(2)}) collective-permute-start(bf16[512,512]{1,0:T(8,128)(2,1)S(1)} %get-tuple-element.102.refs_0_), channel_id=1, source_target_pairs={{0,6},{1,7},{2,2},{3,3},{4,4},{5,5},{6,0},{7,1},{8,14},{9,15},{10,... | collective-permute-start | bytes 1572872 | tf_op jit(solution)/shard_map/ppermute | solution.py:55
  87.6 18.5 %collective-permute-start.20 = (bf16[512,512]{1,0:T(8,128)(2,1)S(1)}, bf16[512,512]{1,0:T(8,128)(2,1)S(1)}, u32[]{:S(2)}, u32[]{:S(2)}) collective-permute-start(bf16[512,512]{1,0:T(8,128)(2,1)S(1)} %get-tuple-element.142.refs_4_), channel_id=1, source_target_pairs={{0,1},{1,0},{2,3},{3,2},{4,5},{5,4},{6,7},{7,6},{8,9},{9,8},{10,11... | collective-permute-start | bytes 1572872 | tf_op jit(solution)/shard_map/ppermute | solution.py:43
  89.7 9.3 %collective-permute-start.21 = (f32[64,1024]{1,0:T(8,128)S(1)}, f32[64,1024]{1,0:T(8,128)S(1)}, u32[]{:S(2)}, u32[]{:S(2)}) collective-permute-start(f32[64,1024]{1,0:T(8,128)S(1)} %get-tuple-element.128), channel_id=1, source_target_pairs={{0,16},{8,24},{16,0},{24,8},{1,17},{9,25},{17,1},{25,9},{2,18},{10... | collective-permute-start | bytes 786440 | tf_op jit(solution)/shard_map/ppermute | solution.py:43
  93.8 12.4 %collective-permute-start.18 = (f32[64,1024]{1,0:T(8,128)S(1)}, f32[64,1024]{1,0:T(8,128)}, u32[]{:S(2)}, u32[]{:S(2)}) collective-permute-start(f32[64,1024]{1,0:T(8,128)S(1)} %get-tuple-element.124), channel_id=1, source_target_pairs={{0,16},{8,24},{16,0},{24,8},{1,17},{9,25},{17,1},{25,9},{2,18},{10... | collective-permute-start | bytes 786440 | tf_op jit(solution)/shard_map/ppermute | solution.py:43
  99.0 9.7 %collective-permute-start.22 = (f32[64,1024]{1,0:T(8,128)S(1)}, f32[64,1024]{1,0:T(8,128)S(1)}, u32[]{:S(2)}, u32[]{:S(2)}) collective-permute-start(f32[64,1024]{1,0:T(8,128)S(1)} %get-tuple-element.135), channel_id=1, source_target_pairs={{0,16},{8,24},{16,0},{24,8},{1,17},{9,25},{17,1},{25,9},{2,18},{10... | collective-permute-start | bytes 786440 | tf_op jit(solution)/shard_map/ppermute | solution.py:43
  100.5 18.8 %collective-permute-start.28 = (bf16[512,512]{1,0:T(8,128)(2,1)S(1)}, bf16[512,512]{1,0:T(8,128)(2,1)}, u32[]{:S(2)}, u32[]{:S(2)}) collective-permute-start(bf16[512,512]{1,0:T(8,128)(2,1)S(1)} %get-tuple-element.142.refs_4_), channel_id=1, source_target_pairs={{0,6},{1,7},{2,2},{3,3},{4,4},{5,5},{6,0},{7,1},{8,14},{9,15},{10,... | collective-permute-start | bytes 1572872 | tf_op jit(solution)/shard_map/ppermute | solution.py:55
  106.1 25.8 %collective-permute-start.24 = (f32[64,1024]{1,0:T(8,128)S(1)}, f32[64,1024]{1,0:T(8,128)S(1)}, u32[]{:S(2)}, u32[]{:S(2)}) collective-permute-start(f32[64,1024]{1,0:T(8,128)S(1)} %add.94), channel_id=1, source_target_pairs={{0,4},{1,5},{2,6},{3,7},{4,0},{5,1},{6,2},{7,3},{8,12},{9,13},{10,... | collective-permute-start | bytes 786440 | tf_op jit(solution)/shard_map/ppermute | solution.py:43
  107.2 25.3 %copy-start.30 = (bf16[4096]{0:T(1024)(128)(2,1)S(1)}, bf16[4096]{0:T(1024)(128)(2,1)}, u32[]{:S(2)}) copy-start(bf16[4096]{0:T(1024)(128)(2,1)} %param.12) | copy-start | bytes 24580
  107.2 25.3 %copy-start.16 = (bf16[1,64,4096]{2,1,0:T(8,128)(2,1)S(1)}, bf16[1,64,4096]{2,1,0:T(8,128)(2,1)}, u32[]{:S(2)}) copy-start(bf16[1,64,4096]{2,1,0:T(8,128)(2,1)} %param.10) | copy-start | bytes 1572868
  107.2 25.3 %copy-start.26 = (f32[64,1024]{1,0:T(8,128)S(1)}, f32[64,1024]{1,0:T(8,128)}, u32[]{:S(2)}) copy-start(f32[64,1024]{1,0:T(8,128)} %copy-done.25) | copy-start | bytes 786436
  107.2 25.3 %collective-permute-start.25 = (f32[64,1024]{1,0:T(8,128)S(1)}, f32[64,1024]{1,0:T(8,128)S(1)}, u32[]{:S(2)}, u32[]{:S(2)}) collective-permute-start(f32[64,1024]{1,0:T(8,128)S(1)} %add.95), channel_id=1, source_target_pairs={{0,6},{1,7},{2,4},{3,5},{4,2},{5,3},{6,0},{7,1},{8,14},{9,15},{10,... | collective-permute-start | bytes 786440 | tf_op jit(solution)/shard_map/ppermute | solution.py:43
  108.7 23.7 %collective-permute-start.23 = (f32[64,1024]{1,0:T(8,128)S(1)}, f32[64,1024]{1,0:T(8,128)S(1)}, u32[]{:S(2)}, u32[]{:S(2)}) collective-permute-start(f32[64,1024]{1,0:T(8,128)S(1)} %add.93), channel_id=1, source_target_pairs={{0,2},{1,3},{2,0},{3,1},{4,6},{5,7},{6,4},{7,5},{8,10},{9,11},{10,... | collective-permute-start | bytes 786440 | tf_op jit(solution)/shard_map/ppermute | solution.py:43
  111.9 20.6 %collective-permute-start.27 = (bf16[512,512]{1,0:T(8,128)(2,1)S(1)}, bf16[512,512]{1,0:T(8,128)(2,1)S(1)}, u32[]{:S(2)}, u32[]{:S(2)}) collective-permute-start(bf16[512,512]{1,0:T(8,128)(2,1)S(1)} %broadcast_select_fusion.1.refs_2_), channel_id=1, source_target_pairs={{0,1},{1,0},{2,3},{3,2},{4,5},{5,4},{6,7},{7,6},{8,9},{9,8},{10,11... | collective-permute-start | bytes 1572872 | tf_op jit(solution)/shard_map/ppermute | solution.py:43
  119.3 13.2 %collective-permute-start.26 = (f32[64,1024]{1,0:T(8,128)S(1)}, f32[64,1024]{1,0:T(8,128)S(1)}, u32[]{:S(2)}, u32[]{:S(2)}) collective-permute-start(f32[64,1024]{1,0:T(8,128)S(1)} %get-tuple-element.140), channel_id=1, source_target_pairs={{0,16},{8,24},{16,0},{24,8},{1,17},{9,25},{17,1},{25,9},{2,18},{10... | collective-permute-start | bytes 786440 | tf_op jit(solution)/shard_map/ppermute | solution.py:43
  131.9 13.8 %collective-permute-start.31 = (bf16[512,512]{1,0:T(8,128)(2,1)S(1)}, bf16[512,512]{1,0:T(8,128)(2,1)S(1)}, u32[]{:S(2)}, u32[]{:S(2)}) collective-permute-start(bf16[512,512]{1,0:T(8,128)(2,1)S(1)} %broadcast_select_fusion.refs_6_), channel_id=1, source_target_pairs={{0,1},{1,0},{2,3},{3,2},{4,5},{5,4},{6,7},{7,6},{8,9},{9,8},{10,11... | collective-permute-start | bytes 1572872 | tf_op jit(solution)/shard_map/ppermute | solution.py:43
  133.4 12.3 %collective-permute-start.29 = (bf16[64,2048]{1,0:T(8,128)(2,1)S(1)}, bf16[64,2048]{1,0:T(8,128)(2,1)S(1)}, u32[]{:S(2)}, u32[]{:S(2)}) collective-permute-start(bf16[64,2048]{1,0:T(8,128)(2,1)S(1)} %get-tuple-element.150), channel_id=1, source_target_pairs={{0,2},{1,3},{2,0},{3,1},{4,6},{5,7},{6,4},{7,5},{8,10},{9,11},{10,... | collective-permute-start | bytes 786440 | tf_op jit(solution)/shard_map/ppermute | solution.py:43
  138.9 7.9 %collective-permute-start.30 = (bf16[64,2048]{1,0:T(8,128)(2,1)S(1)}, bf16[64,2048]{1,0:T(8,128)(2,1)S(1)}, u32[]{:S(2)}, u32[]{:S(2)}) collective-permute-start(bf16[64,2048]{1,0:T(8,128)(2,1)S(1)} %get-tuple-element.155.refs_8_), channel_id=1, source_target_pairs={{0,16},{8,24},{16,0},{24,8},{1,17},{9,25},{17,1},{25,9},{2,18},{10... | collective-permute-start | bytes 786440 | tf_op jit(solution)/shard_map/ppermute | solution.py:43
  147.6 7.1 %collective-permute-start.32 = (bf16[64,2048]{1,0:T(8,128)(2,1)S(1)}, bf16[64,2048]{1,0:T(8,128)(2,1)S(1)}, u32[]{:S(2)}, u32[]{:S(2)}) collective-permute-start(bf16[64,2048]{1,0:T(8,128)(2,1)S(1)} %collective-permute-done.29.refs_8_), channel_id=1, source_target_pairs={{0,16},{8,24},{16,0},{24,8},{1,17},{9,25},{17,1},{25,9},{2,18},{10... | collective-permute-start | bytes 786440 | tf_op jit(solution)/shard_map/ppermute | solution.py:43
  148.6 6.1 %collective-permute-start.36 = (bf16[64,2048]{1,0:T(8,128)(2,1)S(1)}, bf16[64,2048]{1,0:T(8,128)(2,1)S(1)}, u32[]{:S(2)}, u32[]{:S(2)}) collective-permute-start(bf16[64,2048]{1,0:T(8,128)(2,1)S(1)} %collective-permute-done.29.refs_8_), channel_id=1, source_target_pairs={{0,8},{8,0},{16,24},{24,16},{1,9},{9,1},{17,25},{25,17},{2,10},{10... | collective-permute-start | bytes 786440 | tf_op jit(solution)/shard_map/ppermute | solution.py:43
  154.6 4.4 %collective-permute-start.33 = (bf16[64,2048]{1,0:T(8,128)(2,1)S(1)}, bf16[64,2048]{1,0:T(8,128)(2,1)S(1)}, u32[]{:S(2)}, u32[]{:S(2)}) collective-permute-start(bf16[64,2048]{1,0:T(8,128)(2,1)S(1)} %collective-permute-done.32.refs_8_), channel_id=1, source_target_pairs={{0,8},{8,0},{16,24},{24,16},{1,9},{9,1},{17,25},{25,17},{2,10},{10... | collective-permute-start | bytes 786440 | tf_op jit(solution)/shard_map/ppermute | solution.py:43
  158.3 15.1 %collective-permute-start.37 = (f32[256,512]{1,0:T(8,128)}, f32[256,512]{1,0:T(8,128)}, u32[]{:S(2)}, u32[]{:S(2)}) collective-permute-start(f32[256,512]{1,0:T(8,128)} %shard_map.103), channel_id=1, source_target_pairs={{0,2},{1,3},{2,0},{3,1},{4,6},{5,7},{6,4},{7,5},{8,10},{9,11},{10,... | collective-permute-start | bytes 1572872 | tf_op jit(solution)/shard_map/ppermute | solution.py:43
  162.6 21.6 %collective-permute-start.38 = (f32[256,512]{1,0:T(8,128)}, f32[256,512]{1,0:T(8,128)}, u32[]{:S(2)}, u32[]{:S(2)}) collective-permute-start(f32[256,512]{1,0:T(8,128)} %shard_map.101), channel_id=1, source_target_pairs={{0,2},{1,3},{2,0},{3,1},{4,6},{5,7},{6,4},{7,5},{8,10},{9,11},{10,... | collective-permute-start | bytes 1572872 | tf_op jit(solution)/shard_map/ppermute | solution.py:43
  164.1 2.0 %collective-permute-start.34 = (bf16[64,2048]{1,0:T(8,128)(2,1)S(1)}, bf16[64,2048]{1,0:T(8,128)(2,1)}, u32[]{:S(2)}, u32[]{:S(2)}) collective-permute-start(bf16[64,2048]{1,0:T(8,128)(2,1)S(1)} %get-tuple-element.155.refs_8_), channel_id=1, source_target_pairs={{0,8},{8,0},{16,24},{24,16},{1,9},{9,1},{17,25},{25,17},{2,10},{10... | collective-permute-start | bytes 786440 | tf_op jit(solution)/shard_map/ppermute | solution.py:43
  164.1 2.2 %collective-permute-start.35 = (bf16[64,2048]{1,0:T(8,128)(2,1)}, bf16[64,2048]{1,0:T(8,128)(2,1)}, u32[]{:S(2)}, u32[]{:S(2)}) collective-permute-start(bf16[64,2048]{1,0:T(8,128)(2,1)} %copy-done.23), channel_id=1, source_target_pairs={{0,8},{8,0},{16,24},{24,16},{1,9},{9,1},{17,25},{25,17},{2,10},{10... | collective-permute-start | bytes 786440 | tf_op jit(solution)/shard_map/ppermute | solution.py:43
  168.3 17.6 %copy-start.5 = (bf16[512,4096]{1,0:T(8,128)(2,1)S(1)}, bf16[512,4096]{1,0:T(8,128)(2,1)}, u32[]{:S(2)}) copy-start(bf16[512,4096]{1,0:T(8,128)(2,1)} %proj.1) | copy-start | bytes 12582916
  188.0 2.7 %collective-permute-start.39 = (f32[64,4096]{1,0:T(8,128)S(1)}, f32[64,4096]{1,0:T(8,128)S(1)}, u32[]{:S(2)}, u32[]{:S(2)}) collective-permute-start(f32[64,4096]{1,0:T(8,128)S(1)} %get-tuple-element.160), channel_id=1, source_target_pairs={{0,8},{8,0},{16,24},{24,16},{1,9},{9,1},{17,25},{25,17},{2,10},{10... | collective-permute-start | bytes 3145736 | tf_op jit(solution)/shard_map/ppermute | solution.py:43
  191.4 8.4 %collective-permute-start.40 = (bf16[32,4096]{1,0:T(8,128)(2,1)S(1)}, bf16[32,4096]{1,0:T(8,128)(2,1)S(1)}, u32[]{:S(2)}, u32[]{:S(2)}) collective-permute-start(bf16[32,4096]{1,0:T(8,128)(2,1)S(1)} %get-tuple-element.162), channel_id=1, source_target_pairs={{0,16},{8,24},{16,0},{24,8},{1,17},{9,25},{17,1},{25,9},{2,18},{10... | collective-permute-start | bytes 786440 | tf_op jit(solution)/shard_map/ppermute | solution.py:43
  (24 other events, 77.3 us)

commit v5 on v4

--- a/solution.py
+++ b/solution.py
@@ -377,8 +377,8 @@
     sums1 = E(kv_part(at, (near, near2), wk, wv))
     nearfar2 = C(nearfar)
     sums2 = kv_part(at, (nearfar, nearfar2), wk, wv, cost(1))
+    (sums1, sums2), own = tick((sums1, sums2), (mine, mine2, far, far2))
     came = sums1, E(sums2)
-    (sums2,), own = tick((sums2,), (mine, mine2, far, far2))
     sums = kv_part(at, own, wk, wv)
     weight = softmax_part(at, sums, came, query, visible)
     m, h = out_part(at, sums, came, weight, out_proj)

time: 201 us -> 197 us (0.980)
  waiting for transfers between devices: 83.7 us -> 77.8 us
  local copies, waits for them, and re-layouts: 14.8 us -> 18.3 us
    ppermute x33, waiting for transfers between devices: 76.9 us -> 71 us  [swap(): return lax.ppermute(value, self.name, pairs)]
    unnamed x62 -> x74, local copies, waits for them, and re-layouts: 11.7 us -> 15.2 us
  transfers between devices with their start and end apart: 41 -> 41, of which waited for: 16 -> 16; matrix products, arithmetic and copies ran while one was open for 4% -> 4% of each run, Pallas kernels for 14% -> 13%
where the time goes in v5:
time: 197 us; the launch traced here: 196 us
  waiting for transfers between devices  77.8 us (39%)
  starting transfers between devices  62 us (31%)
  Pallas kernels  30.5 us (15%)
  local copies, waits for them, and re-layouts  18.3 us (9%)
  other arithmetic  5.06 us (3%)
    ppermute x33, waiting for transfers between devices, swap(): return lax.ppermute(value, self.name, pairs)  71 us
    ppermute x33, starting transfers between devices, swap(): return lax.ppermute(value, self.name, pairs)  46.8 us
    pallas_call x16, Pallas kernels, local(): pl.pallas_call(body, out_shape=[jax.ShapeDtypeStruct(shape, kind) for sha...  30.5 us
    ppermute x8, starting transfers between devices, turn(): return lax.ppermute(value, self.name, pairs)  15.3 us
    unnamed x74, local copies, waits for them, and re-layouts  15.2 us
    ppermute x8, waiting for transfers between devices, turn(): return lax.ppermute(value, self.name, pairs)  6.8 us
  transfers between devices with their start and end apart: 41, of which 16 were waited for; matrix products, arithmetic and copies ran while one was open for 4% of the time, Pallas kernels for 13%

profile of v5, /device:TPU:0, one launch (start us, length us, event | category | flops | bytes accessed | tf_op | source)
XLA Modules:
  0.0 195.5 jit_solution(13353504415566046072)
XLA Ops:
  0.0 2.9 %collective-permute-start.8 = (bf16[2048,512]{1,0:T(8,128)(2,1)}, bf16[2048,512]{1,0:T(8,128)(2,1)S(1)}, u32[]{:S(2)}, u32[]{:S(2)}) collective-permute-start(bf16[2048,512]{1,0:T(8,128)(2,1)} %refs_2_.7), channel_id=1, source_target_pairs={{0,1},{1,0},{2,3},{3,2},{4,5},{5,4},{6,7},{7,6},{8,9},{9,8},{10,11... | collective-permute-start | bytes 6291464 | tf_op jit(solution)/shard_map/ppermute | solution.py:43
  2.9 1.3 fusion.2
  4.2 1.6 collective-permute-start
  9.4 9.8 %collective-permute-done.refs_0_ = bf16[256,1024]{1,0:T(8,128)(2,1)S(1)} collective-permute-done((bf16[256,1024]{1,0:T(8,128)(2,1)S(1)}, bf16[256,1024]{1,0:T(8,128)(2,1)S(1)}, u32[]{:S(2)}, u32[]{:S(2)}) %collective-permute-start) | collective-permute-done | bytes 524320 | tf_op jit(solution)/shard_map/ppermute | solution.py:43
  19.1 1.4 collective-permute-start.4
  20.6 8.3 %collective-permute-done.1.refs_1_ = bf16[256,1024]{1,0:T(8,128)(2,1)S(1)} collective-permute-done((bf16[256,1024]{1,0:T(8,128)(2,1)S(1)}, bf16[256,1024]{1,0:T(8,128)(2,1)S(1)}, u32[]{:S(2)}, u32[]{:S(2)}) %collective-permute-start.1) | collective-permute-done | bytes 524320 | tf_op jit(solution)/shard_map/ppermute | solution.py:43
  28.9 1.5 collective-permute-start.7
  30.4 3.7 %collective-permute-start.3 = (bf16[256,1024]{1,0:T(8,128)(2,1)S(1)}, bf16[256,1024]{1,0:T(8,128)(2,1)S(1)}, u32[]{:S(2)}, u32[]{:S(2)}) collective-permute-start(bf16[256,1024]{1,0:T(8,128)(2,1)S(1)} %collective-permute-done.2.refs_0_), channel_id=1, source_target_pairs={{0,2},{1,3},{2,0},{3,1},{4,6},{5,7},{6,4},{7,5},{8,10},{9,11},{10,... | collective-permute-start | bytes 1572872 | tf_op jit(solution)/shard_map/ppermute | solution.py:43
  34.0 1.8 collective-permute-start.6
  35.9 1.5 fusion.1
  37.7 1.6 collective-permute-start.10
  39.8 7.0 %collective-permute-done.3.refs_1_ = bf16[256,1024]{1,0:T(8,128)(2,1)S(1)} collective-permute-done((bf16[256,1024]{1,0:T(8,128)(2,1)S(1)}, bf16[256,1024]{1,0:T(8,128)(2,1)S(1)}, u32[]{:S(2)}, u32[]{:S(2)}) %collective-permute-start.3) | collective-permute-done | bytes 524320 | tf_op jit(solution)/shard_map/ppermute | solution.py:43
  47.7 12.1 %collective-permute-start.13 = (bf16[256,1024]{1,0:T(8,128)(2,1)}, bf16[256,1024]{1,0:T(8,128)(2,1)}, u32[]{:S(2)}, u32[]{:S(2)}) collective-permute-start(bf16[256,1024]{1,0:T(8,128)(2,1)} %collective-permute-done.4.refs_0_), channel_id=1, source_target_pairs={{0,2},{1,3},{2,0},{3,1},{4,6},{5,7},{6,4},{7,5},{8,10},{9,11},{10,... | collective-permute-start | bytes 1572872 | tf_op jit(solution)/shard_map/ppermute | solution.py:43
  60.6 1.5 collective-permute-start.11
  62.1 1.3 copy-done.1
  63.4 2.0 %collective-permute-start.9 = (bf16[256,1024]{1,0:T(8,128)(2,1)}, bf16[256,1024]{1,0:T(8,128)(2,1)}, u32[]{:S(2)}, u32[]{:S(2)}) collective-permute-start(bf16[256,1024]{1,0:T(8,128)(2,1)} %collective-permute-done.7.refs_2_), channel_id=1, source_target_pairs={{0,2},{1,3},{2,0},{3,1},{4,6},{5,7},{6,4},{7,5},{8,10},{9,11},{10,... | collective-permute-start | bytes 1572872 | tf_op jit(solution)/shard_map/ppermute | solution.py:43
  66.2 1.6 copy-done.2
  69.8 2.4 %shard_map.93 = (f32[128,1024]{1,0:T(8,128)S(1)}, f32[128,1024]{1,0:T(8,128)S(1)}) custom-call(s32[6]{0:T(128)S(1)} %stack.20.at_ref, bf16[256,1024]{1,0:T(8,128)(2,1)S(1)} %copy-done.11, bf16[256,1024]{1,0:T(8,128)(2,1)S(1)} %copy-done.9, bf16[2048,512]{1,0:T(8,128)(2,1)S(1)} %copy-done, bf16[2048,512]{1,0:T(8,128)(2,1)S(1)} %copy-done.2), custom_call_target="tpu_custom_call" | custom-call | flops 1 | bytes 1750001 | tf_op jit(solution)/shard_map/pallas_call | solution.py:74
  72.3 2.5 %shard_map.92 = (f32[128,1024]{1,0:T(8,128)S(1)}, f32[128,1024]{1,0:T(8,128)S(1)}) custom-call(s32[6]{0:T(128)S(1)} %stack.20.at_ref, bf16[256,1024]{1,0:T(8,128)(2,1)} %collective-permute-done.4.refs_0_, bf16[256,1024]{1,0:T(8,128)(2,1)S(1)} %copy-done.15, bf16[256,1024]{1,0:T(8,128)(2,1)} %collective-permute-done.7.refs_2_, ...), custom_call_target="tpu_custom_call" | custom-call | flops 1 | bytes 1750001 | tf_op jit(solution)/shard_map/pallas_call | solution.py:74
  74.9 2.5 %shard_map.91 = (f32[128,1024]{1,0:T(8,128)S(1)}, f32[128,1024]{1,0:T(8,128)S(1)}) custom-call(s32[6]{0:T(128)S(1)} %stack.20.at_ref, bf16[256,1024]{1,0:T(8,128)(2,1)S(1)} %copy-done.20, bf16[256,1024]{1,0:T(8,128)(2,1)S(1)} %copy-done.24, bf16[2048,512]{1,0:T(8,128)(2,1)S(1)} %copy-done, bf16[2048,512]{1,0:T(8,128)(2,1)S(1)} %copy-done.2), custom_call_target="tpu_custom_call" | custom-call | flops 1 | bytes 1750001 | tf_op jit(solution)/shard_map/pallas_call | solution.py:74
  77.3 2.8 %shard_map.94 = (f32[128,1024]{1,0:T(8,128)S(1)}, f32[128,1024]{1,0:T(8,128)S(1)}) custom-call(s32[6]{0:T(128)S(1)} %stack.20.at_ref, bf16[256,1024]{1,0:T(8,128)(2,1)S(1)} %copy-done.22, bf16[256,1024]{1,0:T(8,128)(2,1)} %collective-permute-done.13.refs_1_, bf16[2048,512]{1,0:T(8,128)(2,1)S(1)} %copy-done, bf16[2048,512]{1,0:T(8,128)(2,1)S(1)} %copy-done.2), custom_call_target="tpu_custom_call" | custom-call | flops 1 | bytes 1750001 | tf_op jit(solution)/shard_map/pallas_call | solution.py:74
  80.9 2.8 %shard_map.95 = (f32[128,1024]{1,0:T(8,128)S(1)}, f32[128,1024]{1,0:T(8,128)S(1)}) custom-call(s32[6]{0:T(128)S(1)} %stack.20.at_ref, bf16[256,1024]{1,0:T(8,128)(2,1)S(1)} %copy-done.13, bf16[256,1024]{1,0:T(8,128)(2,1)} %collective-permute-done.9.refs_1_, bf16[2048,512]{1,0:T(8,128)(2,1)S(1)} %copy-done, bf16[2048,512]{1,0:T(8,128)(2,1)S(1)} %copy-done.2, ...), custom_call_target="tpu_custom_call" | custom-call | flops 1 | bytes 1750001 | tf_op jit(solution)/shard_map/pallas_call | solution.py:74
  84.3 3.4 %collective-permute-start.19 = (bf16[512,512]{1,0:T(8,128)(2,1)S(1)}, bf16[512,512]{1,0:T(8,128)(2,1)}, u32[]{:S(2)}, u32[]{:S(2)}) collective-permute-start(bf16[512,512]{1,0:T(8,128)(2,1)S(1)} %get-tuple-element.104.refs_0_), channel_id=1, source_target_pairs={{0,6},{1,7},{2,2},{3,3},{4,4},{5,5},{6,0},{7,1},{8,14},{9,15},{10,... | collective-permute-start | bytes 1572872 | tf_op jit(solution)/shard_map/ppermute | solution.py:55
  87.6 1.4 collective-permute-start.20
  89.7 1.6 collective-permute-start.21
  94.4 4.6 %collective-permute-done.21 = f32[64,1024]{1,0:T(8,128)S(1)} collective-permute-done((f32[64,1024]{1,0:T(8,128)S(1)}, f32[64,1024]{1,0:T(8,128)S(1)}, u32[]{:S(2)}, u32[]{:S(2)}) %collective-permute-start.21) | collective-permute-done | bytes 262176 | tf_op jit(solution)/shard_map/ppermute | solution.py:43
  99.0 1.5 collective-permute-start.22
  100.5 4.6 %collective-permute-start.28 = (bf16[512,512]{1,0:T(8,128)(2,1)S(1)}, bf16[512,512]{1,0:T(8,128)(2,1)}, u32[]{:S(2)}, u32[]{:S(2)}) collective-permute-start(bf16[512,512]{1,0:T(8,128)(2,1)S(1)} %get-tuple-element.144.refs_4_), channel_id=1, source_target_pairs={{0,6},{1,7},{2,2},{3,3},{4,4},{5,5},{6,0},{7,1},{8,14},{9,15},{10,... | collective-permute-start | bytes 1572872 | tf_op jit(solution)/shard_map/ppermute | solution.py:55
  107.2 1.4 collective-permute-start.25
  108.8 2.1 %collective-permute-start.23 = (f32[64,1024]{1,0:T(8,128)S(1)}, f32[64,1024]{1,0:T(8,128)S(1)}, u32[]{:S(2)}, u32[]{:S(2)}) collective-permute-start(f32[64,1024]{1,0:T(8,128)S(1)} %add.93), channel_id=1, source_target_pairs={{0,2},{1,3},{2,0},{3,1},{4,6},{5,7},{6,4},{7,5},{8,10},{9,11},{10,... | collective-permute-start | bytes 786440 | tf_op jit(solution)/shard_map/ppermute | solution.py:43
  110.8 1.1 broadcast_select_fusion.1.refs_2_
  112.5 6.8 %collective-permute-done.28 = bf16[512,512]{1,0:T(8,128)(2,1)} collective-permute-done((bf16[512,512]{1,0:T(8,128)(2,1)S(1)}, bf16[512,512]{1,0:T(8,128)(2,1)}, u32[]{:S(2)}, u32[]{:S(2)}) %collective-permute-start.28) | collective-permute-done | bytes 524320 | tf_op jit(solution)/shard_map/ppermute | solution.py:55
  120.0 1.1 broadcast_select_fusion.refs_6_
  121.1 10.8 %collective-permute-done.24.q2 = f32[64,1024]{1,0:T(8,128)S(1)} collective-permute-done((f32[64,1024]{1,0:T(8,128)S(1)}, f32[64,1024]{1,0:T(8,128)S(1)}, u32[]{:S(2)}, u32[]{:S(2)}) %collective-permute-start.24) | collective-permute-done | bytes 262176 | tf_op jit(solution)/shard_map/ppermute | solution.py:43
  133.4 5.6 %collective-permute-start.29 = (bf16[64,2048]{1,0:T(8,128)(2,1)S(1)}, bf16[64,2048]{1,0:T(8,128)(2,1)S(1)}, u32[]{:S(2)}, u32[]{:S(2)}) collective-permute-start(bf16[64,2048]{1,0:T(8,128)(2,1)S(1)} %get-tuple-element.152), channel_id=1, source_target_pairs={{0,2},{1,3},{2,0},{3,1},{4,6},{5,7},{6,4},{7,5},{8,10},{9,11},{10,... | collective-permute-start | bytes 786440 | tf_op jit(solution)/shard_map/ppermute | solution.py:43
  139.9 5.7 %collective-permute-done.31.refs_7_ = bf16[512,512]{1,0:T(8,128)(2,1)S(1)} collective-permute-done((bf16[512,512]{1,0:T(8,128)(2,1)S(1)}, bf16[512,512]{1,0:T(8,128)(2,1)S(1)}, u32[]{:S(2)}, u32[]{:S(2)}) %collective-permute-start.31) | collective-permute-done | bytes 524320 | tf_op jit(solution)/shard_map/ppermute | solution.py:43
  145.7 1.2 collective-permute-done.30.refs_10_
  148.4 2.8 %shard_map.101 = f32[256,512]{1,0:T(8,128)S(1)} custom-call(s32[6]{0:T(128)S(1)} %stack.20.at_ref, bf16[512,512]{1,0:T(8,128)(2,1)S(1)} %get-tuple-element.104.refs_0_, bf16[512,512]{1,0:T(8,128)(2,1)} %collective-permute-done.12.refs_1_, bf16[512,512]{1,0:T(8,128)(2,1)S(1)} %broadcast_select_fusion.1.refs_2_, ...), custom_call_target="tpu_custom_call" | custom-call | flops 1 | bytes 1 | tf_op jit(solution)/shard_map/pallas_call | solution.py:74
  151.7 3.9 %collective-permute-done.34.refs_8_ = bf16[64,2048]{1,0:T(8,128)(2,1)S(1)} collective-permute-done((bf16[64,2048]{1,0:T(8,128)(2,1)S(1)}, bf16[64,2048]{1,0:T(8,128)(2,1)S(1)}, u32[]{:S(2)}, u32[]{:S(2)}) %collective-permute-start.34) | collective-permute-done | bytes 262176 | tf_op jit(solution)/shard_map/ppermute | solution.py:43
  157.2 3.6 %shard_map.102 = f32[256,512]{1,0:T(8,128)} custom-call(s32[6]{0:T(128)S(1)} %stack.20.at_ref, bf16[512,512]{1,0:T(8,128)(2,1)S(1)} %get-tuple-element.104.refs_0_, bf16[512,512]{1,0:T(8,128)(2,1)} %collective-permute-done.12.refs_1_, bf16[512,512]{1,0:T(8,128)(2,1)S(1)} %broadcast_select_fusion.1.refs_2_, ...), custom_call_target="tpu_custom_call" | custom-call | flops 1 | bytes 3500001 | tf_op jit(solution)/shard_map/pallas_call | solution.py:74
  162.2 3.1 %collective-permute-done.33.one = f32[256,512]{1,0:T(8,128)S(1)} collective-permute-done((f32[256,512]{1,0:T(8,128)S(1)}, f32[256,512]{1,0:T(8,128)S(1)}, u32[]{:S(2)}, u32[]{:S(2)}) %collective-permute-start.33) | collective-permute-done | bytes 524320 | tf_op jit(solution)/shard_map/ppermute | solution.py:43
  171.1 3.7 %shard_map.103.own_ref = f32[512,512]{1,0:T(8,128)S(1)} custom-call(s32[6]{0:T(128)S(1)} %stack.20.at_ref, bf16[512,512]{1,0:T(8,128)(2,1)S(1)} %get-tuple-element.104.refs_0_, bf16[512,512]{1,0:T(8,128)(2,1)} %collective-permute-done.12.refs_1_, bf16[512,512]{1,0:T(8,128)(2,1)S(1)} %broadcast_select_fusion.1.refs_2_, ...), custom_call_target="tpu_custom_call" | custom-call | flops 1 | bytes 1 | tf_op jit(solution)/shard_map/pallas_call | solution.py:74
  174.8 4.8 %collective-permute-done.38.two = f32[256,512]{1,0:T(8,128)} collective-permute-done((f32[256,512]{1,0:T(8,128)}, f32[256,512]{1,0:T(8,128)}, u32[]{:S(2)}, u32[]{:S(2)}) %collective-permute-start.38) | collective-permute-done | bytes 524320 | tf_op jit(solution)/shard_map/ppermute | solution.py:43
  179.5 1.5 shard_map.104.weight
  181.0 1.9 shard_map.105
  183.0 2.6 %collective-permute-done.39.theirs_ref = f32[64,4096]{1,0:T(8,128)S(1)} collective-permute-done((f32[64,4096]{1,0:T(8,128)S(1)}, f32[64,4096]{1,0:T(8,128)S(1)}, u32[]{:S(2)}, u32[]{:S(2)}) %collective-permute-start.39) | collective-permute-done | bytes 1048608 | tf_op jit(solution)/shard_map/ppermute | solution.py:43
  186.4 1.0 collective-permute-start.40
  187.4 7.4 %collective-permute-done.40 = bf16[32,4096]{1,0:T(8,128)(2,1)S(1)} collective-permute-done((bf16[32,4096]{1,0:T(8,128)(2,1)S(1)}, bf16[32,4096]{1,0:T(8,128)(2,1)S(1)}, u32[]{:S(2)}, u32[]{:S(2)}) %collective-permute-start.40) | collective-permute-done | bytes 262176 | tf_op jit(solution)/shard_map/ppermute | solution.py:43
  (138 shorter events, 30.5 us)
Async XLA Ops:
  0.0 35.9 %copy-start.34 = (bf16[512,2,512]{2,1,0:T(2,128)(2,1)S(1)}, bf16[512,2,512]{2,1,0:T(2,128)(2,1)}, u32[]{:S(2)}) copy-start(bf16[512,2,512]{2,1,0:T(2,128)(2,1)} %param.13) | copy-start | bytes 3145732
  0.0 62.1 %collective-permute-start.8 = (bf16[2048,512]{1,0:T(8,128)(2,1)}, bf16[2048,512]{1,0:T(8,128)(2,1)S(1)}, u32[]{:S(2)}, u32[]{:S(2)}) collective-permute-start(bf16[2048,512]{1,0:T(8,128)(2,1)} %refs_2_.7), channel_id=1, source_target_pairs={{0,1},{1,0},{2,3},{3,2},{4,5},{5,4},{6,7},{7,6},{8,9},{9,8},{10,11... | collective-permute-start | bytes 6291464 | tf_op jit(solution)/shard_map/ppermute | solution.py:43
  4.2 14.9 %collective-permute-start = (bf16[256,1024]{1,0:T(8,128)(2,1)S(1)}, bf16[256,1024]{1,0:T(8,128)(2,1)S(1)}, u32[]{:S(2)}, u32[]{:S(2)}) collective-permute-start(bf16[256,1024]{1,0:T(8,128)(2,1)S(1)} %get-tuple-element.170.refs_0_), channel_id=1, source_target_pairs={{0,2},{1,3},{2,0},{3,1},{4,6},{5,7},{6,4},{7,5},{8,10},{9,11},{10,... | collective-permute-start | bytes 1572872 | tf_op jit(solution)/shard_map/ppermute | solution.py:43
  5.9 23.0 %collective-permute-start.1 = (bf16[256,1024]{1,0:T(8,128)(2,1)S(1)}, bf16[256,1024]{1,0:T(8,128)(2,1)S(1)}, u32[]{:S(2)}, u32[]{:S(2)}) collective-permute-start(bf16[256,1024]{1,0:T(8,128)(2,1)S(1)} %get-tuple-element.169.refs_1_), channel_id=1, source_target_pairs={{0,2},{1,3},{2,0},{3,1},{4,6},{5,7},{6,4},{7,5},{8,10},{9,11},{10,... | collective-permute-start | bytes 1572872 | tf_op jit(solution)/shard_map/ppermute | solution.py:43
  6.3 24.1 %collective-permute-start.2 = (bf16[256,1024]{1,0:T(8,128)(2,1)S(1)}, bf16[256,1024]{1,0:T(8,128)(2,1)S(1)}, u32[]{:S(2)}, u32[]{:S(2)}) collective-permute-start(bf16[256,1024]{1,0:T(8,128)(2,1)S(1)} %get-tuple-element.170.refs_0_), channel_id=1, source_target_pairs={{0,0},{1,1},{2,4},{3,5},{4,2},{5,3},{6,6},{7,7},{8,8},{9,9},{10,12... | collective-permute-start | bytes 1572872 | tf_op jit(solution)/shard_map/ppermute | solution.py:55
  7.8 26.3 %collective-permute-start.5 = (bf16[256,1024]{1,0:T(8,128)(2,1)S(1)}, bf16[256,1024]{1,0:T(8,128)(2,1)S(1)}, u32[]{:S(2)}, u32[]{:S(2)}) collective-permute-start(bf16[256,1024]{1,0:T(8,128)(2,1)S(1)} %get-tuple-element.169.refs_1_), channel_id=1, source_target_pairs={{0,0},{1,1},{2,4},{3,5},{4,2},{5,3},{6,6},{7,7},{8,8},{9,9},{10,12... | collective-permute-start | bytes 1572872 | tf_op jit(solution)/shard_map/ppermute | solution.py:55
  19.1 18.2 %copy-start.19 = (bf16[256,1024]{1,0:T(8,128)(2,1)}, bf16[256,1024]{1,0:T(8,128)(2,1)S(1)}, u32[]{:S(2)}) copy-start(bf16[256,1024]{1,0:T(8,128)(2,1)S(1)} %collective-permute-done.refs_0_) | copy-start | bytes 1572868
  19.1 18.6 %collective-permute-start.4 = (bf16[256,1024]{1,0:T(8,128)(2,1)S(1)}, bf16[256,1024]{1,0:T(8,128)(2,1)}, u32[]{:S(2)}, u32[]{:S(2)}) collective-permute-start(bf16[256,1024]{1,0:T(8,128)(2,1)S(1)} %collective-permute-done.refs_0_), channel_id=1, source_target_pairs={{0,0},{1,1},{2,4},{3,5},{4,2},{5,3},{6,6},{7,7},{8,8},{9,9},{10,12... | collective-permute-start | bytes 1572872 | tf_op jit(solution)/shard_map/ppermute | solution.py:55
  28.9 10.4 %collective-permute-start.7 = (bf16[256,1024]{1,0:T(8,128)(2,1)S(1)}, bf16[256,1024]{1,0:T(8,128)(2,1)}, u32[]{:S(2)}, u32[]{:S(2)}) collective-permute-start(bf16[256,1024]{1,0:T(8,128)(2,1)S(1)} %collective-permute-done.1.refs_1_), channel_id=1, source_target_pairs={{0,0},{1,1},{2,4},{3,5},{4,2},{5,3},{6,6},{7,7},{8,8},{9,9},{10,12... | collective-permute-start | bytes 1572872 | tf_op jit(solution)/shard_map/ppermute | solution.py:55
  30.4 16.5 %collective-permute-start.3 = (bf16[256,1024]{1,0:T(8,128)(2,1)S(1)}, bf16[256,1024]{1,0:T(8,128)(2,1)S(1)}, u32[]{:S(2)}, u32[]{:S(2)}) collective-permute-start(bf16[256,1024]{1,0:T(8,128)(2,1)S(1)} %collective-permute-done.2.refs_0_), channel_id=1, source_target_pairs={{0,2},{1,3},{2,0},{3,1},{4,6},{5,7},{6,4},{7,5},{8,10},{9,11},{10,... | collective-permute-start | bytes 1572872 | tf_op jit(solution)/shard_map/ppermute | solution.py:43
  34.0 25.8 %collective-permute-start.6 = (bf16[256,1024]{1,0:T(8,128)(2,1)S(1)}, bf16[256,1024]{1,0:T(8,128)(2,1)S(1)}, u32[]{:S(2)}, u32[]{:S(2)}) collective-permute-start(bf16[256,1024]{1,0:T(8,128)(2,1)S(1)} %collective-permute-done.5.refs_0_), channel_id=1, source_target_pairs={{0,2},{1,3},{2,0},{3,1},{4,6},{5,7},{6,4},{7,5},{8,10},{9,11},{10,... | collective-permute-start | bytes 1572872 | tf_op jit(solution)/shard_map/ppermute | solution.py:43
  37.4 28.8 %copy-start = (bf16[2048,512]{1,0:T(8,128)(2,1)S(1)}, bf16[2048,512]{1,0:T(8,128)(2,1)}, u32[]{:S(2)}) copy-start(bf16[2048,512]{1,0:T(8,128)(2,1)} %refs_2_.7) | copy-start | bytes 6291460
  37.7 42.5 %collective-permute-start.10 = (bf16[512,512]{1,0:T(8,128)(2,1)S(1)}, bf16[512,512]{1,0:T(8,128)(2,1)}, u32[]{:S(2)}, u32[]{:S(2)}) collective-permute-start(bf16[512,512]{1,0:T(8,128)(2,1)S(1)} %get-tuple-element.104.refs_0_), channel_id=1, source_target_pairs={{0,0},{1,1},{2,4},{3,5},{4,2},{5,3},{6,6},{7,7},{8,8},{9,9},{10,12... | collective-permute-start | bytes 1572872 | tf_op jit(solution)/shard_map/ppermute | solution.py:55
  39.3 40.9 %collective-permute-start.12 = (bf16[512,512]{1,0:T(8,128)(2,1)S(1)}, bf16[512,512]{1,0:T(8,128)(2,1)}, u32[]{:S(2)}, u32[]{:S(2)}) collective-permute-start(bf16[512,512]{1,0:T(8,128)(2,1)S(1)} %get-tuple-element.104.refs_0_), channel_id=1, source_target_pairs={{0,1},{1,0},{2,3},{3,2},{4,5},{5,4},{6,7},{7,6},{8,9},{9,8},{10,11... | collective-permute-start | bytes 1572872 | tf_op jit(solution)/shard_map/ppermute | solution.py:43
  47.7 29.6 %collective-permute-start.13 = (bf16[256,1024]{1,0:T(8,128)(2,1)}, bf16[256,1024]{1,0:T(8,128)(2,1)}, u32[]{:S(2)}, u32[]{:S(2)}) collective-permute-start(bf16[256,1024]{1,0:T(8,128)(2,1)} %collective-permute-done.4.refs_0_), channel_id=1, source_target_pairs={{0,2},{1,3},{2,0},{3,1},{4,6},{5,7},{6,4},{7,5},{8,10},{9,11},{10,... | collective-permute-start | bytes 1572872 | tf_op jit(solution)/shard_map/ppermute | solution.py:43
  60.6 19.6 %collective-permute-start.11 = (bf16[512,512]{1,0:T(8,128)(2,1)S(1)}, bf16[512,512]{1,0:T(8,128)(2,1)}, u32[]{:S(2)}, u32[]{:S(2)}) collective-permute-start(bf16[512,512]{1,0:T(8,128)(2,1)S(1)} %get-tuple-element.144.refs_4_), channel_id=1, source_target_pairs={{0,0},{1,1},{2,4},{3,5},{4,2},{5,3},{6,6},{7,7},{8,8},{9,9},{10,12... | collective-permute-start | bytes 1572872 | tf_op jit(solution)/shard_map/ppermute | solution.py:55
  63.4 16.8 %collective-permute-start.9 = (bf16[256,1024]{1,0:T(8,128)(2,1)}, bf16[256,1024]{1,0:T(8,128)(2,1)}, u32[]{:S(2)}, u32[]{:S(2)}) collective-permute-start(bf16[256,1024]{1,0:T(8,128)(2,1)} %collective-permute-done.7.refs_2_), channel_id=1, source_target_pairs={{0,2},{1,3},{2,0},{3,1},{4,6},{5,7},{6,4},{7,5},{8,10},{9,11},{10,... | collective-permute-start | bytes 1572872 | tf_op jit(solution)/shard_map/ppermute | solution.py:43
  80.2 3.5 %collective-permute-start.14 = (f32[128,1024]{1,0:T(8,128)S(1)}, f32[128,1024]{1,0:T(8,128)S(1)}, u32[]{:S(2)}, u32[]{:S(2)}) collective-permute-start(f32[128,1024]{1,0:T(8,128)S(1)} %get-tuple-element.107), channel_id=1, source_target_pairs={{0,8},{8,0},{16,24},{24,16},{1,9},{9,1},{17,25},{25,17},{2,10},{10... | collective-permute-start | bytes 1572872 | tf_op jit(solution)/shard_map/ppermute | solution.py:43
  80.3 3.4 %collective-permute-start.15 = (f32[128,1024]{1,0:T(8,128)S(1)}, f32[128,1024]{1,0:T(8,128)S(1)}, u32[]{:S(2)}, u32[]{:S(2)}) collective-permute-start(f32[128,1024]{1,0:T(8,128)S(1)} %get-tuple-element.108), channel_id=1, source_target_pairs={{0,8},{8,0},{16,24},{24,16},{1,9},{9,1},{17,25},{25,17},{2,10},{10... | collective-permute-start | bytes 1572872 | tf_op jit(solution)/shard_map/ppermute | solution.py:43
  80.8 2.9 %collective-permute-start.16 = (f32[128,1024]{1,0:T(8,128)S(1)}, f32[128,1024]{1,0:T(8,128)S(1)}, u32[]{:S(2)}, u32[]{:S(2)}) collective-permute-start(f32[128,1024]{1,0:T(8,128)S(1)} %get-tuple-element.109), channel_id=1, source_target_pairs={{0,8},{8,0},{16,24},{24,16},{1,9},{9,1},{17,25},{25,17},{2,10},{10... | collective-permute-start | bytes 1572872 | tf_op jit(solution)/shard_map/ppermute | solution.py:43
  83.8 9.4 %collective-permute-start.17 = (f32[128,1024]{1,0:T(8,128)S(1)}, f32[128,1024]{1,0:T(8,128)S(1)}, u32[]{:S(2)}, u32[]{:S(2)}) collective-permute-start(f32[128,1024]{1,0:T(8,128)S(1)} %get-tuple-element.116), channel_id=1, source_target_pairs={{0,8},{8,0},{16,24},{24,16},{1,9},{9,1},{17,25},{25,17},{2,10},{10... | collective-permute-start | bytes 1572872 | tf_op jit(solution)/shard_map/ppermute | solution.py:43
  84.3 21.8 %collective-permute-start.19 = (bf16[512,512]{1,0:T(8,128)(2,1)S(1)}, bf16[512,512]{1,0:T(8,128)(2,1)}, u32[]{:S(2)}, u32[]{:S(2)}) collective-permute-start(bf16[512,512]{1,0:T(8,128)(2,1)S(1)} %get-tuple-element.104.refs_0_), channel_id=1, source_target_pairs={{0,6},{1,7},{2,2},{3,3},{4,4},{5,5},{6,0},{7,1},{8,14},{9,15},{10,... | collective-permute-start | bytes 1572872 | tf_op jit(solution)/shard_map/ppermute | solution.py:55
  87.6 18.5 %collective-permute-start.20 = (bf16[512,512]{1,0:T(8,128)(2,1)S(1)}, bf16[512,512]{1,0:T(8,128)(2,1)S(1)}, u32[]{:S(2)}, u32[]{:S(2)}) collective-permute-start(bf16[512,512]{1,0:T(8,128)(2,1)S(1)} %get-tuple-element.144.refs_4_), channel_id=1, source_target_pairs={{0,1},{1,0},{2,3},{3,2},{4,5},{5,4},{6,7},{7,6},{8,9},{9,8},{10,11... | collective-permute-start | bytes 1572872 | tf_op jit(solution)/shard_map/ppermute | solution.py:43
  89.7 9.3 %collective-permute-start.21 = (f32[64,1024]{1,0:T(8,128)S(1)}, f32[64,1024]{1,0:T(8,128)S(1)}, u32[]{:S(2)}, u32[]{:S(2)}) collective-permute-start(f32[64,1024]{1,0:T(8,128)S(1)} %get-tuple-element.130), channel_id=1, source_target_pairs={{0,16},{8,24},{16,0},{24,8},{1,17},{9,25},{17,1},{25,9},{2,18},{10... | collective-permute-start | bytes 786440 | tf_op jit(solution)/shard_map/ppermute | solution.py:43
  93.8 12.4 %collective-permute-start.18 = (f32[64,1024]{1,0:T(8,128)S(1)}, f32[64,1024]{1,0:T(8,128)}, u32[]{:S(2)}, u32[]{:S(2)}) collective-permute-start(f32[64,1024]{1,0:T(8,128)S(1)} %get-tuple-element.126), channel_id=1, source_target_pairs={{0,16},{8,24},{16,0},{24,8},{1,17},{9,25},{17,1},{25,9},{2,18},{10... | collective-permute-start | bytes 786440 | tf_op jit(solution)/shard_map/ppermute | solution.py:43
  99.0 9.7 %collective-permute-start.22 = (f32[64,1024]{1,0:T(8,128)S(1)}, f32[64,1024]{1,0:T(8,128)S(1)}, u32[]{:S(2)}, u32[]{:S(2)}) collective-permute-start(f32[64,1024]{1,0:T(8,128)S(1)} %get-tuple-element.137), channel_id=1, source_target_pairs={{0,16},{8,24},{16,0},{24,8},{1,17},{9,25},{17,1},{25,9},{2,18},{10... | collective-permute-start | bytes 786440 | tf_op jit(solution)/shard_map/ppermute | solution.py:43
  100.5 18.8 %collective-permute-start.28 = (bf16[512,512]{1,0:T(8,128)(2,1)S(1)}, bf16[512,512]{1,0:T(8,128)(2,1)}, u32[]{:S(2)}, u32[]{:S(2)}) collective-permute-start(bf16[512,512]{1,0:T(8,128)(2,1)S(1)} %get-tuple-element.144.refs_4_), channel_id=1, source_target_pairs={{0,6},{1,7},{2,2},{3,3},{4,4},{5,5},{6,0},{7,1},{8,14},{9,15},{10,... | collective-permute-start | bytes 1572872 | tf_op jit(solution)/shard_map/ppermute | solution.py:55
  106.1 25.8 %collective-permute-start.24 = (f32[64,1024]{1,0:T(8,128)S(1)}, f32[64,1024]{1,0:T(8,128)S(1)}, u32[]{:S(2)}, u32[]{:S(2)}) collective-permute-start(f32[64,1024]{1,0:T(8,128)S(1)} %add.94), channel_id=1, source_target_pairs={{0,4},{1,5},{2,6},{3,7},{4,0},{5,1},{6,2},{7,3},{8,12},{9,13},{10,... | collective-permute-start | bytes 786440 | tf_op jit(solution)/shard_map/ppermute | solution.py:43
  107.2 25.3 %copy-start.36 = (bf16[4096]{0:T(1024)(128)(2,1)S(1)}, bf16[4096]{0:T(1024)(128)(2,1)}, u32[]{:S(2)}) copy-start(bf16[4096]{0:T(1024)(128)(2,1)} %param.12) | copy-start | bytes 24580
  107.2 25.3 %copy-start.18 = (bf16[1,64,4096]{2,1,0:T(8,128)(2,1)S(1)}, bf16[1,64,4096]{2,1,0:T(8,128)(2,1)}, u32[]{:S(2)}) copy-start(bf16[1,64,4096]{2,1,0:T(8,128)(2,1)} %param.10) | copy-start | bytes 1572868
  107.2 25.3 %copy-start.32 = (f32[64,1024]{1,0:T(8,128)S(1)}, f32[64,1024]{1,0:T(8,128)}, u32[]{:S(2)}) copy-start(f32[64,1024]{1,0:T(8,128)} %copy-done.31) | copy-start | bytes 786436
  107.2 25.2 %collective-permute-start.25 = (f32[64,1024]{1,0:T(8,128)S(1)}, f32[64,1024]{1,0:T(8,128)S(1)}, u32[]{:S(2)}, u32[]{:S(2)}) collective-permute-start(f32[64,1024]{1,0:T(8,128)S(1)} %add.95), channel_id=1, source_target_pairs={{0,6},{1,7},{2,4},{3,5},{4,2},{5,3},{6,0},{7,1},{8,14},{9,15},{10,... | collective-permute-start | bytes 786440 | tf_op jit(solution)/shard_map/ppermute | solution.py:43
  108.8 23.7 %collective-permute-start.23 = (f32[64,1024]{1,0:T(8,128)S(1)}, f32[64,1024]{1,0:T(8,128)S(1)}, u32[]{:S(2)}, u32[]{:S(2)}) collective-permute-start(f32[64,1024]{1,0:T(8,128)S(1)} %add.93), channel_id=1, source_target_pairs={{0,2},{1,3},{2,0},{3,1},{4,6},{5,7},{6,4},{7,5},{8,10},{9,11},{10,... | collective-permute-start | bytes 786440 | tf_op jit(solution)/shard_map/ppermute | solution.py:43
  111.9 20.5 %collective-permute-start.27 = (bf16[512,512]{1,0:T(8,128)(2,1)S(1)}, bf16[512,512]{1,0:T(8,128)(2,1)S(1)}, u32[]{:S(2)}, u32[]{:S(2)}) collective-permute-start(bf16[512,512]{1,0:T(8,128)(2,1)S(1)} %broadcast_select_fusion.1.refs_2_), channel_id=1, source_target_pairs={{0,1},{1,0},{2,3},{3,2},{4,5},{5,4},{6,7},{7,6},{8,9},{9,8},{10,11... | collective-permute-start | bytes 1572872 | tf_op jit(solution)/shard_map/ppermute | solution.py:43
  119.3 13.2 %collective-permute-start.26 = (f32[64,1024]{1,0:T(8,128)S(1)}, f32[64,1024]{1,0:T(8,128)S(1)}, u32[]{:S(2)}, u32[]{:S(2)}) collective-permute-start(f32[64,1024]{1,0:T(8,128)S(1)} %get-tuple-element.142), channel_id=1, source_target_pairs={{0,16},{8,24},{16,0},{24,8},{1,17},{9,25},{17,1},{25,9},{2,18},{10... | collective-permute-start | bytes 786440 | tf_op jit(solution)/shard_map/ppermute | solution.py:43
  131.9 13.8 %collective-permute-start.31 = (bf16[512,512]{1,0:T(8,128)(2,1)S(1)}, bf16[512,512]{1,0:T(8,128)(2,1)S(1)}, u32[]{:S(2)}, u32[]{:S(2)}) collective-permute-start(bf16[512,512]{1,0:T(8,128)(2,1)S(1)} %broadcast_select_fusion.refs_6_), channel_id=1, source_target_pairs={{0,1},{1,0},{2,3},{3,2},{4,5},{5,4},{6,7},{7,6},{8,9},{9,8},{10,11... | collective-permute-start | bytes 1572872 | tf_op jit(solution)/shard_map/ppermute | solution.py:43
  133.4 12.3 %collective-permute-start.29 = (bf16[64,2048]{1,0:T(8,128)(2,1)S(1)}, bf16[64,2048]{1,0:T(8,128)(2,1)S(1)}, u32[]{:S(2)}, u32[]{:S(2)}) collective-permute-start(bf16[64,2048]{1,0:T(8,128)(2,1)S(1)} %get-tuple-element.152), channel_id=1, source_target_pairs={{0,2},{1,3},{2,0},{3,1},{4,6},{5,7},{6,4},{7,5},{8,10},{9,11},{10,... | collective-permute-start | bytes 786440 | tf_op jit(solution)/shard_map/ppermute | solution.py:43
  138.9 7.9 %collective-permute-start.30 = (bf16[64,2048]{1,0:T(8,128)(2,1)S(1)}, bf16[64,2048]{1,0:T(8,128)(2,1)S(1)}, u32[]{:S(2)}, u32[]{:S(2)}) collective-permute-start(bf16[64,2048]{1,0:T(8,128)(2,1)S(1)} %get-tuple-element.157.refs_8_), channel_id=1, source_target_pairs={{0,16},{8,24},{16,0},{24,8},{1,17},{9,25},{17,1},{25,9},{2,18},{10... | collective-permute-start | bytes 786440 | tf_op jit(solution)/shard_map/ppermute | solution.py:43
  145.6 11.5 %copy-start.3 = (bf16[512,512]{1,0:T(8,128)(2,1)}, bf16[512,512]{1,0:T(8,128)(2,1)S(1)}, u32[]{:S(2)}) copy-start(bf16[512,512]{1,0:T(8,128)(2,1)S(1)} %collective-permute-done.31.refs_7_) | copy-start | bytes 1572868
  146.9 1.5 collective-permute-start.32
  146.9 8.7 %collective-permute-start.34 = (bf16[64,2048]{1,0:T(8,128)(2,1)S(1)}, bf16[64,2048]{1,0:T(8,128)(2,1)S(1)}, u32[]{:S(2)}, u32[]{:S(2)}) collective-permute-start(bf16[64,2048]{1,0:T(8,128)(2,1)S(1)} %collective-permute-done.29.refs_8_), channel_id=1, source_target_pairs={{0,16},{8,24},{16,0},{24,8},{1,17},{9,25},{17,1},{25,9},{2,18},{10... | collective-permute-start | bytes 786440 | tf_op jit(solution)/shard_map/ppermute | solution.py:43
  151.3 14.0 %collective-permute-start.33 = (f32[256,512]{1,0:T(8,128)S(1)}, f32[256,512]{1,0:T(8,128)S(1)}, u32[]{:S(2)}, u32[]{:S(2)}) collective-permute-start(f32[256,512]{1,0:T(8,128)S(1)} %shard_map.101), channel_id=1, source_target_pairs={{0,2},{1,3},{2,0},{3,1},{4,6},{5,7},{6,4},{7,5},{8,10},{9,11},{10,... | collective-permute-start | bytes 1572872 | tf_op jit(solution)/shard_map/ppermute | solution.py:43
  155.6 1.5 collective-permute-start.35
  155.6 5.2 %collective-permute-start.36 = (bf16[64,2048]{1,0:T(8,128)(2,1)S(1)}, bf16[64,2048]{1,0:T(8,128)(2,1)S(1)}, u32[]{:S(2)}, u32[]{:S(2)}) collective-permute-start(bf16[64,2048]{1,0:T(8,128)(2,1)S(1)} %get-tuple-element.157.refs_8_), channel_id=1, source_target_pairs={{0,8},{8,0},{16,24},{24,16},{1,9},{9,1},{17,25},{25,17},{2,10},{10... | collective-permute-start | bytes 786440 | tf_op jit(solution)/shard_map/ppermute | solution.py:43
  156.1 5.4 %collective-permute-start.37 = (bf16[64,2048]{1,0:T(8,128)(2,1)S(1)}, bf16[64,2048]{1,0:T(8,128)(2,1)S(1)}, u32[]{:S(2)}, u32[]{:S(2)}) collective-permute-start(bf16[64,2048]{1,0:T(8,128)(2,1)S(1)} %collective-permute-done.30.refs_10_), channel_id=1, source_target_pairs={{0,8},{8,0},{16,24},{24,16},{1,9},{9,1},{17,25},{25,17},{2,10},{10... | collective-permute-start | bytes 786440 | tf_op jit(solution)/shard_map/ppermute | solution.py:43
  166.1 13.5 %collective-permute-start.38 = (f32[256,512]{1,0:T(8,128)}, f32[256,512]{1,0:T(8,128)}, u32[]{:S(2)}, u32[]{:S(2)}) collective-permute-start(f32[256,512]{1,0:T(8,128)} %shard_map.102), channel_id=1, source_target_pairs={{0,2},{1,3},{2,0},{3,1},{4,6},{5,7},{6,4},{7,5},{8,10},{9,11},{10,... | collective-permute-start | bytes 1572872 | tf_op jit(solution)/shard_map/ppermute | solution.py:43
  182.9 2.7 %collective-permute-start.39 = (f32[64,4096]{1,0:T(8,128)S(1)}, f32[64,4096]{1,0:T(8,128)S(1)}, u32[]{:S(2)}, u32[]{:S(2)}) collective-permute-start(f32[64,4096]{1,0:T(8,128)S(1)} %get-tuple-element.164), channel_id=1, source_target_pairs={{0,8},{8,0},{16,24},{24,16},{1,9},{9,1},{17,25},{25,17},{2,10},{10... | collective-permute-start | bytes 3145736 | tf_op jit(solution)/shard_map/ppermute | solution.py:43
  186.4 8.4 %collective-permute-start.40 = (bf16[32,4096]{1,0:T(8,128)(2,1)S(1)}, bf16[32,4096]{1,0:T(8,128)(2,1)S(1)}, u32[]{:S(2)}, u32[]{:S(2)}) collective-permute-start(bf16[32,4096]{1,0:T(8,128)(2,1)S(1)} %get-tuple-element.166), channel_id=1, source_target_pairs={{0,16},{8,24},{16,0},{24,8},{1,17},{9,25},{17,1},{25,9},{2,18},{10... | collective-permute-start | bytes 786440 | tf_op jit(solution)/shard_map/ppermute | solution.py:43
  (30 other events, 87.5 us)

commit v6 on v5

--- a/solution.py
+++ b/solution.py
@@ -150,15 +150,17 @@
 
 def core_add(at, mine, theirs, sent=F32):
     rows, cols = mine.shape[0] // 2, mine.shape[1]
-
-    def body(at_ref, mine_ref, theirs_ref, keep, send):
+    if not isinstance(theirs, (list, tuple)):
+        theirs = [theirs[:rows], theirs[rows:]]
+
+    def body(at_ref, mine_ref, low, high, keep, send):
         first = at_ref[2] == 0
-        one = mine_ref[:rows] + theirs_ref[:rows]
-        two = mine_ref[rows:] + theirs_ref[rows:]
+        one = mine_ref[:rows] + low[...]
+        two = mine_ref[rows:] + high[...]
         keep[...] = jnp.where(first, one, two)
         send[...] = jnp.where(first, two, one).astype(sent)
 
-    return local(body, [((rows, cols), F32), ((rows, cols), sent)], at, mine, theirs)
+    return local(body, [((rows, cols), F32), ((rows, cols), sent)], at, mine, *theirs)
 
 
 def norm_part(at, keep, came, others, stream, gain):
@@ -328,6 +330,7 @@
     (o2a,), (k, v) = tick((o2a,), (k, v))
     ok, ov, xk0 = O(k), O(v), X(k)
     (e2a, o2a, e2b, o2b, xd), (k, v) = tick((e2a, o2a, e2b, o2b, xd), (k, v))
+    fk = z.ends(k)
     m1, h1 = product(((e1a,), (e1b,)), xd)
     m2, h2 = product(((o2a, e2a), (o2b, e2b)), xd)
     m0, h0 = product(((ha,), (hb,)), xd)
@@ -335,13 +338,14 @@
 
     done = (m1, h1, m2, h2, m0, h0, e3b, ok, ov, xk0, *part3)
     (m1, h1, m2, h2, m0, h0, e3b, ok, ov, xk0, *part3), (k, v) = tick(done, (k, v))
-    fk, fv = z.ends(k), z.ends(v)
+    fv = z.ends(v)
     xv0 = X(v)
-    h1, h2, h0 = C(h1), C(h2), C(h0)
     m3, h3 = product(((o1b, e3b),), xd, first=1, sofar=part3)
 
-    (h1, h2, h0, m3, h3), = tick((h1, h2, h0, m3, h3))
-    h3 = C(h3)
+    sides = [C(part) for h in (h1, h2, h0) for part in jnp.split(h, 2, axis=0)]
+    sides, (m3, h3, fk) = tick(sides, (m3, h3, fk))
+    h1, h2, h0 = sides[:2], sides[2:4], sides[4:]
+    h3 = [C(part) for part in jnp.split(h3, 2, axis=0)]
     k2, s2 = core_add(at, m2, h2)
     s2 = Y(s2)
     k1, s1 = core_add(at, m1, h1)
@@ -361,7 +365,7 @@
     kk = jnp.where(inner, ok, fk)
     xkk = X(kk)
 
-    (s1,), = tick((s1,))
+    (s1, fv), = tick((s1, fv))
     q1 = z.swap(k1 + s1, 1)
 
     vv = jnp.where(inner, ov, fv)
@@ -382,7 +386,7 @@
     sums = kv_part(at, own, wk, wv)
     weight = softmax_part(at, sums, came, query, visible)
     m, h = out_part(at, sums, came, weight, out_proj)
-    keep, send = core_add(at, m, C(h), BF16)
+    keep, send = core_add(at, m, [C(part) for part in jnp.split(h, 2, axis=0)], BF16)
     return (keep + Y(send).astype(F32)).astype(BF16)
 
 

time: 197 us -> 194 us (0.985)
  waiting for transfers between devices: 77.8 us -> 73.5 us
  starting transfers between devices: 62 us -> 65 us
    ppermute x33 -> x38, starting transfers between devices: 46.8 us -> 50.8 us  [swap(): return lax.ppermute(value, self.name, pairs)]
    ppermute x8, waiting for transfers between devices: 6.8 us -> 3.38 us  [turn(): return lax.ppermute(value, self.name, pairs)]
    ppermute x33 -> x38, waiting for transfers between devices: 71 us -> 70.1 us  [swap(): return lax.ppermute(value, self.name, pairs)]
    unnamed x74 -> x76, local copies, waits for them, and re-layouts: 15.2 us -> 14.4 us
  transfers between devices with their start and end apart: 41 -> 46, of which waited for: 16 -> 21; matrix products, arithmetic and copies ran while one was open for 4% -> 3% of each run, Pallas kernels for 13% -> 14%
where the time goes in v6:
time: 194 us; the launch traced here: 193 us
  waiting for transfers between devices  73.5 us (38%)
  starting transfers between devices  65 us (34%)
  Pallas kernels  30.4 us (16%)
  local copies, waits for them, and re-layouts  17.8 us (9%)
  other arithmetic  4.01 us (2%)
  between operations  1.98 us (1%)
    ppermute x38, waiting for transfers between devices, swap(): return lax.ppermute(value, self.name, pairs)  70.1 us
    ppermute x38, starting transfers between devices, swap(): return lax.ppermute(value, self.name, pairs)  50.8 us
    pallas_call x16, Pallas kernels, local(): pl.pallas_call(body, out_shape=[jax.ShapeDtypeStruct(shape, kind) for sha...  30.4 us
    unnamed x76, local copies, waits for them, and re-layouts  14.4 us
    ppermute x8, starting transfers between devices, turn(): return lax.ppermute(value, self.name, pairs)  14.2 us
  transfers between devices with their start and end apart: 46, of which 21 were waited for; matrix products, arithmetic and copies ran while one was open for 3% of the time, Pallas kernels for 14%

profile of v6, /device:TPU:0, one launch (start us, length us, event | category | flops | bytes accessed | tf_op | source)
XLA Modules:
  0.0 192.6 jit_solution(7382204797683146584)
XLA Ops:
  0.0 2.9 %collective-permute-start.8 = (bf16[2048,512]{1,0:T(8,128)(2,1)}, bf16[2048,512]{1,0:T(8,128)(2,1)S(1)}, u32[]{:S(2)}, u32[]{:S(2)}) collective-permute-start(bf16[2048,512]{1,0:T(8,128)(2,1)} %refs_2_.7), channel_id=1, source_target_pairs={{0,1},{1,0},{2,3},{3,2},{4,5},{5,4},{6,7},{7,6},{8,9},{9,8},{10,11... | collective-permute-start | bytes 6291464 | tf_op jit(solution)/shard_map/ppermute | solution.py:43
  2.9 1.3 fusion.3
  4.2 1.6 collective-permute-start
  9.3 9.8 %collective-permute-done.refs_0_ = bf16[256,1024]{1,0:T(8,128)(2,1)S(1)} collective-permute-done((bf16[256,1024]{1,0:T(8,128)(2,1)S(1)}, bf16[256,1024]{1,0:T(8,128)(2,1)S(1)}, u32[]{:S(2)}, u32[]{:S(2)}) %collective-permute-start) | collective-permute-done | bytes 524320 | tf_op jit(solution)/shard_map/ppermute | solution.py:43
  19.1 1.4 collective-permute-start.4
  20.6 8.3 %collective-permute-done.1.refs_1_ = bf16[256,1024]{1,0:T(8,128)(2,1)S(1)} collective-permute-done((bf16[256,1024]{1,0:T(8,128)(2,1)S(1)}, bf16[256,1024]{1,0:T(8,128)(2,1)S(1)}, u32[]{:S(2)}, u32[]{:S(2)}) %collective-permute-start.1) | collective-permute-done | bytes 524320 | tf_op jit(solution)/shard_map/ppermute | solution.py:43
  28.9 1.5 collective-permute-start.7
  30.4 3.7 %collective-permute-start.3 = (bf16[256,1024]{1,0:T(8,128)(2,1)S(1)}, bf16[256,1024]{1,0:T(8,128)(2,1)S(1)}, u32[]{:S(2)}, u32[]{:S(2)}) collective-permute-start(bf16[256,1024]{1,0:T(8,128)(2,1)S(1)} %collective-permute-done.2.refs_0_), channel_id=1, source_target_pairs={{0,2},{1,3},{2,0},{3,1},{4,6},{5,7},{6,4},{7,5},{8,10},{9,11},{10,... | collective-permute-start | bytes 1572872 | tf_op jit(solution)/shard_map/ppermute | solution.py:43
  34.0 1.8 collective-permute-start.6
  35.9 1.5 fusion.2
  37.7 1.6 collective-permute-start.10
  39.3 19.1 %collective-permute-start.13 = (bf16[256,1024]{1,0:T(8,128)(2,1)}, bf16[256,1024]{1,0:T(8,128)(2,1)}, u32[]{:S(2)}, u32[]{:S(2)}) collective-permute-start(bf16[256,1024]{1,0:T(8,128)(2,1)} %collective-permute-done.4.refs_0_), channel_id=1, source_target_pairs={{0,2},{1,3},{2,0},{3,1},{4,6},{5,7},{6,4},{7,5},{8,10},{9,11},{10,... | collective-permute-start | bytes 1572872 | tf_op jit(solution)/shard_map/ppermute | solution.py:43
  60.6 1.4 collective-permute-start.11
  62.0 1.3 copy-done.1
  63.3 2.0 %collective-permute-start.9 = (bf16[256,1024]{1,0:T(8,128)(2,1)}, bf16[256,1024]{1,0:T(8,128)(2,1)}, u32[]{:S(2)}, u32[]{:S(2)}) collective-permute-start(bf16[256,1024]{1,0:T(8,128)(2,1)} %collective-permute-done.7.refs_2_), channel_id=1, source_target_pairs={{0,2},{1,3},{2,0},{3,1},{4,6},{5,7},{6,4},{7,5},{8,10},{9,11},{10,... | collective-permute-start | bytes 1572872 | tf_op jit(solution)/shard_map/ppermute | solution.py:43
  66.1 1.6 copy-done.2
  69.8 2.5 %shard_map.93 = (f32[128,1024]{1,0:T(8,128)S(1)}, f32[128,1024]{1,0:T(8,128)S(1)}) custom-call(s32[6]{0:T(128)S(1)} %stack.20.at_ref, bf16[256,1024]{1,0:T(8,128)(2,1)S(1)} %copy-done.11, bf16[256,1024]{1,0:T(8,128)(2,1)S(1)} %copy-done.9, bf16[2048,512]{1,0:T(8,128)(2,1)S(1)} %copy-done, bf16[2048,512]{1,0:T(8,128)(2,1)S(1)} %copy-done.2), custom_call_target="tpu_custom_call" | custom-call | flops 1 | bytes 1750001 | tf_op jit(solution)/shard_map/pallas_call | solution.py:74
  72.3 2.5 %shard_map.92 = (f32[128,1024]{1,0:T(8,128)S(1)}, f32[128,1024]{1,0:T(8,128)S(1)}) custom-call(s32[6]{0:T(128)S(1)} %stack.20.at_ref, bf16[256,1024]{1,0:T(8,128)(2,1)} %collective-permute-done.4.refs_0_, bf16[256,1024]{1,0:T(8,128)(2,1)S(1)} %copy-done.15, bf16[256,1024]{1,0:T(8,128)(2,1)} %collective-permute-done.7.refs_2_, ...), custom_call_target="tpu_custom_call" | custom-call | flops 1 | bytes 1750001 | tf_op jit(solution)/shard_map/pallas_call | solution.py:74
  74.8 2.5 %shard_map.91 = (f32[128,1024]{1,0:T(8,128)S(1)}, f32[128,1024]{1,0:T(8,128)S(1)}) custom-call(s32[6]{0:T(128)S(1)} %stack.20.at_ref, bf16[256,1024]{1,0:T(8,128)(2,1)S(1)} %copy-done.22, bf16[256,1024]{1,0:T(8,128)(2,1)S(1)} %copy-done.24, bf16[2048,512]{1,0:T(8,128)(2,1)S(1)} %copy-done, bf16[2048,512]{1,0:T(8,128)(2,1)S(1)} %copy-done.2), custom_call_target="tpu_custom_call" | custom-call | flops 1 | bytes 1750001 | tf_op jit(solution)/shard_map/pallas_call | solution.py:74
  77.3 3.3 %collective-permute-start.20 = (bf16[512,512]{1,0:T(8,128)(2,1)S(1)}, bf16[512,512]{1,0:T(8,128)(2,1)S(1)}, u32[]{:S(2)}, u32[]{:S(2)}) collective-permute-start(bf16[512,512]{1,0:T(8,128)(2,1)S(1)} %get-tuple-element.111.refs_0_), channel_id=1, source_target_pairs={{0,6},{1,7},{2,2},{3,3},{4,4},{5,5},{6,0},{7,1},{8,14},{9,15},{10,... | collective-permute-start | bytes 1572872 | tf_op jit(solution)/shard_map/ppermute | solution.py:55
  80.6 2.8 %shard_map.94 = (f32[128,1024]{1,0:T(8,128)S(1)}, f32[128,1024]{1,0:T(8,128)S(1)}) custom-call(s32[6]{0:T(128)S(1)} %stack.20.at_ref, bf16[256,1024]{1,0:T(8,128)(2,1)S(1)} %copy-done.20, bf16[256,1024]{1,0:T(8,128)(2,1)} %collective-permute-done.13.refs_1_, bf16[2048,512]{1,0:T(8,128)(2,1)S(1)} %copy-done, bf16[2048,512]{1,0:T(8,128)(2,1)S(1)} %copy-done.2), custom_call_target="tpu_custom_call" | custom-call | flops 1 | bytes 1750001 | tf_op jit(solution)/shard_map/pallas_call | solution.py:74
  85.6 2.8 %shard_map.95 = (f32[128,1024]{1,0:T(8,128)S(1)}, f32[128,1024]{1,0:T(8,128)S(1)}) custom-call(s32[6]{0:T(128)S(1)} %stack.20.at_ref, bf16[256,1024]{1,0:T(8,128)(2,1)S(1)} %copy-done.13, bf16[256,1024]{1,0:T(8,128)(2,1)} %collective-permute-done.9.refs_1_, bf16[2048,512]{1,0:T(8,128)(2,1)S(1)} %copy-done, bf16[2048,512]{1,0:T(8,128)(2,1)S(1)} %copy-done.2, ...), custom_call_target="tpu_custom_call" | custom-call | flops 1 | bytes 1750001 | tf_op jit(solution)/shard_map/pallas_call | solution.py:74
  88.5 2.9 %collective-permute-done.20 = bf16[512,512]{1,0:T(8,128)(2,1)S(1)} collective-permute-done((bf16[512,512]{1,0:T(8,128)(2,1)S(1)}, bf16[512,512]{1,0:T(8,128)(2,1)S(1)}, u32[]{:S(2)}, u32[]{:S(2)}) %collective-permute-start.20) | collective-permute-done | bytes 524320 | tf_op jit(solution)/shard_map/ppermute | solution.py:55
  93.3 1.6 collective-permute-start.25
  94.9 3.6 %collective-permute-start.27 = (bf16[512,512]{1,0:T(8,128)(2,1)S(1)}, bf16[512,512]{1,0:T(8,128)(2,1)}, u32[]{:S(2)}, u32[]{:S(2)}) collective-permute-start(bf16[512,512]{1,0:T(8,128)(2,1)S(1)} %get-tuple-element.157.refs_4_), channel_id=1, source_target_pairs={{0,6},{1,7},{2,2},{3,3},{4,4},{5,5},{6,0},{7,1},{8,14},{9,15},{10,... | collective-permute-start | bytes 1572872 | tf_op jit(solution)/shard_map/ppermute | solution.py:55
  101.4 1.5 collective-permute-start.26
  103.0 2.9 %collective-permute-done.24.refs_5_ = bf16[512,512]{1,0:T(8,128)(2,1)S(1)} collective-permute-done((bf16[512,512]{1,0:T(8,128)(2,1)S(1)}, bf16[512,512]{1,0:T(8,128)(2,1)S(1)}, u32[]{:S(2)}, u32[]{:S(2)}) %collective-permute-start.24) | collective-permute-done | bytes 524320 | tf_op jit(solution)/shard_map/ppermute | solution.py:43
  106.0 3.9 %collective-permute-done.23 = f32[64,1024]{1,0:T(8,128)} collective-permute-done((f32[64,1024]{1,0:T(8,128)S(1)}, f32[64,1024]{1,0:T(8,128)}, u32[]{:S(2)}, u32[]{:S(2)}) %collective-permute-start.23) | collective-permute-done | bytes 262176 | tf_op jit(solution)/shard_map/ppermute | solution.py:43
  110.8 2.3 %collective-permute-start.30 = (f32[64,1024]{1,0:T(8,128)S(1)}, f32[64,1024]{1,0:T(8,128)S(1)}, u32[]{:S(2)}, u32[]{:S(2)}) collective-permute-start(f32[64,1024]{1,0:T(8,128)S(1)} %add.95), channel_id=1, source_target_pairs={{0,6},{1,7},{2,4},{3,5},{4,2},{5,3},{6,0},{7,1},{8,14},{9,15},{10,... | collective-permute-start | bytes 786440 | tf_op jit(solution)/shard_map/ppermute | solution.py:43
  114.8 1.4 collective-permute-start.32
  116.8 1.1 broadcast_select_fusion.refs_6_
  117.9 11.0 %collective-permute-done.29.q2 = f32[64,1024]{1,0:T(8,128)S(1)} collective-permute-done((f32[64,1024]{1,0:T(8,128)S(1)}, f32[64,1024]{1,0:T(8,128)S(1)}, u32[]{:S(2)}, u32[]{:S(2)}) %collective-permute-start.29) | collective-permute-done | bytes 262176 | tf_op jit(solution)/shard_map/ppermute | solution.py:43
  128.9 1.4 collective-permute-start.35
  130.3 2.0 %collective-permute-done.28.q1 = f32[64,1024]{1,0:T(8,128)S(1)} collective-permute-done((f32[64,1024]{1,0:T(8,128)S(1)}, f32[64,1024]{1,0:T(8,128)S(1)}, u32[]{:S(2)}, u32[]{:S(2)}) %collective-permute-start.28) | collective-permute-done | bytes 262176 | tf_op jit(solution)/shard_map/ppermute | solution.py:43
  133.2 2.7 %collective-permute-start.33 = (bf16[64,2048]{1,0:T(8,128)(2,1)S(1)}, bf16[64,2048]{1,0:T(8,128)(2,1)S(1)}, u32[]{:S(2)}, u32[]{:S(2)}) collective-permute-start(bf16[64,2048]{1,0:T(8,128)(2,1)S(1)} %get-tuple-element.166), channel_id=1, source_target_pairs={{0,2},{1,3},{2,0},{3,1},{4,6},{5,7},{6,4},{7,5},{8,10},{9,11},{10,... | collective-permute-start | bytes 786440 | tf_op jit(solution)/shard_map/ppermute | solution.py:43
  136.5 6.2 %collective-permute-done.35.refs_7_ = bf16[512,512]{1,0:T(8,128)(2,1)S(1)} collective-permute-done((bf16[512,512]{1,0:T(8,128)(2,1)S(1)}, bf16[512,512]{1,0:T(8,128)(2,1)S(1)}, u32[]{:S(2)}, u32[]{:S(2)}) %collective-permute-start.35) | collective-permute-done | bytes 524320 | tf_op jit(solution)/shard_map/ppermute | solution.py:43
  142.7 1.2 collective-permute-done.34.refs_10_
  145.4 2.8 %shard_map.101 = f32[256,512]{1,0:T(8,128)S(1)} custom-call(s32[6]{0:T(128)S(1)} %stack.20.at_ref, bf16[512,512]{1,0:T(8,128)(2,1)S(1)} %get-tuple-element.111.refs_0_, bf16[512,512]{1,0:T(8,128)(2,1)} %collective-permute-done.12.refs_1_, bf16[512,512]{1,0:T(8,128)(2,1)S(1)} %broadcast_select_fusion.1.refs_2_, ...), custom_call_target="tpu_custom_call" | custom-call | flops 1 | bytes 1 | tf_op jit(solution)/shard_map/pallas_call | solution.py:74
  148.7 3.9 %collective-permute-done.38.refs_8_ = bf16[64,2048]{1,0:T(8,128)(2,1)S(1)} collective-permute-done((bf16[64,2048]{1,0:T(8,128)(2,1)S(1)}, bf16[64,2048]{1,0:T(8,128)(2,1)S(1)}, u32[]{:S(2)}, u32[]{:S(2)}) %collective-permute-start.38) | collective-permute-done | bytes 262176 | tf_op jit(solution)/shard_map/ppermute | solution.py:43
  154.2 3.6 %shard_map.102 = f32[256,512]{1,0:T(8,128)} custom-call(s32[6]{0:T(128)S(1)} %stack.20.at_ref, bf16[512,512]{1,0:T(8,128)(2,1)S(1)} %get-tuple-element.111.refs_0_, bf16[512,512]{1,0:T(8,128)(2,1)} %collective-permute-done.12.refs_1_, bf16[512,512]{1,0:T(8,128)(2,1)S(1)} %broadcast_select_fusion.1.refs_2_, ...), custom_call_target="tpu_custom_call" | custom-call | flops 1 | bytes 3500001 | tf_op jit(solution)/shard_map/pallas_call | solution.py:74
  159.2 3.1 %collective-permute-done.37.one = f32[256,512]{1,0:T(8,128)S(1)} collective-permute-done((f32[256,512]{1,0:T(8,128)S(1)}, f32[256,512]{1,0:T(8,128)S(1)}, u32[]{:S(2)}, u32[]{:S(2)}) %collective-permute-start.37) | collective-permute-done | bytes 524320 | tf_op jit(solution)/shard_map/ppermute | solution.py:43
  164.2 1.0 copy-done.4
  168.1 3.7 %shard_map.103.own_ref = f32[512,512]{1,0:T(8,128)S(1)} custom-call(s32[6]{0:T(128)S(1)} %stack.20.at_ref, bf16[512,512]{1,0:T(8,128)(2,1)S(1)} %get-tuple-element.111.refs_0_, bf16[512,512]{1,0:T(8,128)(2,1)} %collective-permute-done.12.refs_1_, bf16[512,512]{1,0:T(8,128)(2,1)S(1)} %broadcast_select_fusion.1.refs_2_, ...), custom_call_target="tpu_custom_call" | custom-call | flops 1 | bytes 1 | tf_op jit(solution)/shard_map/pallas_call | solution.py:74
  171.8 4.8 %collective-permute-done.42.two = f32[256,512]{1,0:T(8,128)} collective-permute-done((f32[256,512]{1,0:T(8,128)}, f32[256,512]{1,0:T(8,128)}, u32[]{:S(2)}, u32[]{:S(2)}) %collective-permute-start.42) | collective-permute-done | bytes 524320 | tf_op jit(solution)/shard_map/ppermute | solution.py:43
  176.6 1.5 shard_map.104.weight
  178.0 1.9 shard_map.105
  180.6 1.4 collective-permute-done.43.low
  184.2 7.7 %collective-permute-done.45 = bf16[32,4096]{1,0:T(8,128)(2,1)S(1)} collective-permute-done((bf16[32,4096]{1,0:T(8,128)(2,1)S(1)}, bf16[32,4096]{1,0:T(8,128)(2,1)S(1)}, u32[]{:S(2)}, u32[]{:S(2)}) %collective-permute-start.45) | collective-permute-done | bytes 262176 | tf_op jit(solution)/shard_map/ppermute | solution.py:43
  (155 shorter events, 32.1 us)
Async XLA Ops:
  0.0 35.9 %copy-start.34 = (bf16[512,2,512]{2,1,0:T(2,128)(2,1)S(1)}, bf16[512,2,512]{2,1,0:T(2,128)(2,1)}, u32[]{:S(2)}) copy-start(bf16[512,2,512]{2,1,0:T(2,128)(2,1)} %param.13) | copy-start | bytes 3145732
  0.0 62.0 %collective-permute-start.8 = (bf16[2048,512]{1,0:T(8,128)(2,1)}, bf16[2048,512]{1,0:T(8,128)(2,1)S(1)}, u32[]{:S(2)}, u32[]{:S(2)}) collective-permute-start(bf16[2048,512]{1,0:T(8,128)(2,1)} %refs_2_.7), channel_id=1, source_target_pairs={{0,1},{1,0},{2,3},{3,2},{4,5},{5,4},{6,7},{7,6},{8,9},{9,8},{10,11... | collective-permute-start | bytes 6291464 | tf_op jit(solution)/shard_map/ppermute | solution.py:43
  4.2 14.9 %collective-permute-start = (bf16[256,1024]{1,0:T(8,128)(2,1)S(1)}, bf16[256,1024]{1,0:T(8,128)(2,1)S(1)}, u32[]{:S(2)}, u32[]{:S(2)}) collective-permute-start(bf16[256,1024]{1,0:T(8,128)(2,1)S(1)} %get-tuple-element.186.refs_0_), channel_id=1, source_target_pairs={{0,2},{1,3},{2,0},{3,1},{4,6},{5,7},{6,4},{7,5},{8,10},{9,11},{10,... | collective-permute-start | bytes 1572872 | tf_op jit(solution)/shard_map/ppermute | solution.py:43
  5.9 23.0 %collective-permute-start.1 = (bf16[256,1024]{1,0:T(8,128)(2,1)S(1)}, bf16[256,1024]{1,0:T(8,128)(2,1)S(1)}, u32[]{:S(2)}, u32[]{:S(2)}) collective-permute-start(bf16[256,1024]{1,0:T(8,128)(2,1)S(1)} %get-tuple-element.185.refs_1_), channel_id=1, source_target_pairs={{0,2},{1,3},{2,0},{3,1},{4,6},{5,7},{6,4},{7,5},{8,10},{9,11},{10,... | collective-permute-start | bytes 1572872 | tf_op jit(solution)/shard_map/ppermute | solution.py:43
  6.3 24.1 %collective-permute-start.2 = (bf16[256,1024]{1,0:T(8,128)(2,1)S(1)}, bf16[256,1024]{1,0:T(8,128)(2,1)S(1)}, u32[]{:S(2)}, u32[]{:S(2)}) collective-permute-start(bf16[256,1024]{1,0:T(8,128)(2,1)S(1)} %get-tuple-element.186.refs_0_), channel_id=1, source_target_pairs={{0,0},{1,1},{2,4},{3,5},{4,2},{5,3},{6,6},{7,7},{8,8},{9,9},{10,12... | collective-permute-start | bytes 1572872 | tf_op jit(solution)/shard_map/ppermute | solution.py:55
  7.8 26.3 %collective-permute-start.5 = (bf16[256,1024]{1,0:T(8,128)(2,1)S(1)}, bf16[256,1024]{1,0:T(8,128)(2,1)S(1)}, u32[]{:S(2)}, u32[]{:S(2)}) collective-permute-start(bf16[256,1024]{1,0:T(8,128)(2,1)S(1)} %get-tuple-element.185.refs_1_), channel_id=1, source_target_pairs={{0,0},{1,1},{2,4},{3,5},{4,2},{5,3},{6,6},{7,7},{8,8},{9,9},{10,12... | collective-permute-start | bytes 1572872 | tf_op jit(solution)/shard_map/ppermute | solution.py:55
  19.1 18.6 %collective-permute-start.4 = (bf16[256,1024]{1,0:T(8,128)(2,1)S(1)}, bf16[256,1024]{1,0:T(8,128)(2,1)}, u32[]{:S(2)}, u32[]{:S(2)}) collective-permute-start(bf16[256,1024]{1,0:T(8,128)(2,1)S(1)} %collective-permute-done.refs_0_), channel_id=1, source_target_pairs={{0,0},{1,1},{2,4},{3,5},{4,2},{5,3},{6,6},{7,7},{8,8},{9,9},{10,12... | collective-permute-start | bytes 1572872 | tf_op jit(solution)/shard_map/ppermute | solution.py:55
  28.9 10.4 %collective-permute-start.7 = (bf16[256,1024]{1,0:T(8,128)(2,1)S(1)}, bf16[256,1024]{1,0:T(8,128)(2,1)}, u32[]{:S(2)}, u32[]{:S(2)}) collective-permute-start(bf16[256,1024]{1,0:T(8,128)(2,1)S(1)} %collective-permute-done.1.refs_1_), channel_id=1, source_target_pairs={{0,0},{1,1},{2,4},{3,5},{4,2},{5,3},{6,6},{7,7},{8,8},{9,9},{10,12... | collective-permute-start | bytes 1572872 | tf_op jit(solution)/shard_map/ppermute | solution.py:55
  30.4 28.1 %collective-permute-start.3 = (bf16[256,1024]{1,0:T(8,128)(2,1)S(1)}, bf16[256,1024]{1,0:T(8,128)(2,1)S(1)}, u32[]{:S(2)}, u32[]{:S(2)}) collective-permute-start(bf16[256,1024]{1,0:T(8,128)(2,1)S(1)} %collective-permute-done.2.refs_0_), channel_id=1, source_target_pairs={{0,2},{1,3},{2,0},{3,1},{4,6},{5,7},{6,4},{7,5},{8,10},{9,11},{10,... | collective-permute-start | bytes 1572872 | tf_op jit(solution)/shard_map/ppermute | solution.py:43
  34.0 25.7 %collective-permute-start.6 = (bf16[256,1024]{1,0:T(8,128)(2,1)S(1)}, bf16[256,1024]{1,0:T(8,128)(2,1)S(1)}, u32[]{:S(2)}, u32[]{:S(2)}) collective-permute-start(bf16[256,1024]{1,0:T(8,128)(2,1)S(1)} %collective-permute-done.5.refs_0_), channel_id=1, source_target_pairs={{0,2},{1,3},{2,0},{3,1},{4,6},{5,7},{6,4},{7,5},{8,10},{9,11},{10,... | collective-permute-start | bytes 1572872 | tf_op jit(solution)/shard_map/ppermute | solution.py:43
  37.4 28.7 %copy-start = (bf16[2048,512]{1,0:T(8,128)(2,1)S(1)}, bf16[2048,512]{1,0:T(8,128)(2,1)}, u32[]{:S(2)}) copy-start(bf16[2048,512]{1,0:T(8,128)(2,1)} %refs_2_.7) | copy-start | bytes 6291460
  37.7 45.7 %collective-permute-start.10 = (bf16[512,512]{1,0:T(8,128)(2,1)S(1)}, bf16[512,512]{1,0:T(8,128)(2,1)}, u32[]{:S(2)}, u32[]{:S(2)}) collective-permute-start(bf16[512,512]{1,0:T(8,128)(2,1)S(1)} %get-tuple-element.111.refs_0_), channel_id=1, source_target_pairs={{0,0},{1,1},{2,4},{3,5},{4,2},{5,3},{6,6},{7,7},{8,8},{9,9},{10,12... | collective-permute-start | bytes 1572872 | tf_op jit(solution)/shard_map/ppermute | solution.py:55
  39.3 38.0 %collective-permute-start.13 = (bf16[256,1024]{1,0:T(8,128)(2,1)}, bf16[256,1024]{1,0:T(8,128)(2,1)}, u32[]{:S(2)}, u32[]{:S(2)}) collective-permute-start(bf16[256,1024]{1,0:T(8,128)(2,1)} %collective-permute-done.4.refs_0_), channel_id=1, source_target_pairs={{0,2},{1,3},{2,0},{3,1},{4,6},{5,7},{6,4},{7,5},{8,10},{9,11},{10,... | collective-permute-start | bytes 1572872 | tf_op jit(solution)/shard_map/ppermute | solution.py:43
  59.3 24.2 %collective-permute-start.12 = (bf16[512,512]{1,0:T(8,128)(2,1)S(1)}, bf16[512,512]{1,0:T(8,128)(2,1)}, u32[]{:S(2)}, u32[]{:S(2)}) collective-permute-start(bf16[512,512]{1,0:T(8,128)(2,1)S(1)} %get-tuple-element.111.refs_0_), channel_id=1, source_target_pairs={{0,1},{1,0},{2,3},{3,2},{4,5},{5,4},{6,7},{7,6},{8,9},{9,8},{10,11... | collective-permute-start | bytes 1572872 | tf_op jit(solution)/shard_map/ppermute | solution.py:43
  60.6 22.9 %collective-permute-start.11 = (bf16[512,512]{1,0:T(8,128)(2,1)S(1)}, bf16[512,512]{1,0:T(8,128)(2,1)}, u32[]{:S(2)}, u32[]{:S(2)}) collective-permute-start(bf16[512,512]{1,0:T(8,128)(2,1)S(1)} %get-tuple-element.157.refs_4_), channel_id=1, source_target_pairs={{0,0},{1,1},{2,4},{3,5},{4,2},{5,3},{6,6},{7,7},{8,8},{9,9},{10,12... | collective-permute-start | bytes 1572872 | tf_op jit(solution)/shard_map/ppermute | solution.py:55
  63.3 20.1 %collective-permute-start.9 = (bf16[256,1024]{1,0:T(8,128)(2,1)}, bf16[256,1024]{1,0:T(8,128)(2,1)}, u32[]{:S(2)}, u32[]{:S(2)}) collective-permute-start(bf16[256,1024]{1,0:T(8,128)(2,1)} %collective-permute-done.7.refs_2_), channel_id=1, source_target_pairs={{0,2},{1,3},{2,0},{3,1},{4,6},{5,7},{6,4},{7,5},{8,10},{9,11},{10,... | collective-permute-start | bytes 1572872 | tf_op jit(solution)/shard_map/ppermute | solution.py:43
  77.3 14.1 %collective-permute-start.20 = (bf16[512,512]{1,0:T(8,128)(2,1)S(1)}, bf16[512,512]{1,0:T(8,128)(2,1)S(1)}, u32[]{:S(2)}, u32[]{:S(2)}) collective-permute-start(bf16[512,512]{1,0:T(8,128)(2,1)S(1)} %get-tuple-element.111.refs_0_), channel_id=1, source_target_pairs={{0,6},{1,7},{2,2},{3,3},{4,4},{5,5},{6,0},{7,1},{8,14},{9,15},{10,... | collective-permute-start | bytes 1572872 | tf_op jit(solution)/shard_map/ppermute | solution.py:55
  83.5 1.6 collective-permute-start.14
  83.6 1.9 collective-permute-start.15
  84.1 4.3 %collective-permute-start.16 = (f32[64,1024]{1,0:T(8,128)S(1)}, f32[64,1024]{1,0:T(8,128)S(1)}, u32[]{:S(2)}, u32[]{:S(2)}) collective-permute-start(f32[64,1024]{1,0:T(8,128)S(1)} %get-tuple-element.192), channel_id=1, source_target_pairs={{0,8},{8,0},{16,24},{24,16},{1,9},{9,1},{17,25},{25,17},{2,10},{10... | collective-permute-start | bytes 786440 | tf_op jit(solution)/shard_map/ppermute | solution.py:43
  84.3 4.2 %collective-permute-start.17 = (f32[64,1024]{1,0:T(8,128)S(1)}, f32[64,1024]{1,0:T(8,128)S(1)}, u32[]{:S(2)}, u32[]{:S(2)}) collective-permute-start(f32[64,1024]{1,0:T(8,128)S(1)} %get-tuple-element.191), channel_id=1, source_target_pairs={{0,8},{8,0},{16,24},{24,16},{1,9},{9,1},{17,25},{25,17},{2,10},{10... | collective-permute-start | bytes 786440 | tf_op jit(solution)/shard_map/ppermute | solution.py:43
  85.1 3.4 %collective-permute-start.18 = (f32[64,1024]{1,0:T(8,128)S(1)}, f32[64,1024]{1,0:T(8,128)S(1)}, u32[]{:S(2)}, u32[]{:S(2)}) collective-permute-start(f32[64,1024]{1,0:T(8,128)S(1)} %get-tuple-element.190), channel_id=1, source_target_pairs={{0,8},{8,0},{16,24},{24,16},{1,9},{9,1},{17,25},{25,17},{2,10},{10... | collective-permute-start | bytes 786440 | tf_op jit(solution)/shard_map/ppermute | solution.py:43
  85.5 3.0 %collective-permute-start.19 = (f32[64,1024]{1,0:T(8,128)S(1)}, f32[64,1024]{1,0:T(8,128)S(1)}, u32[]{:S(2)}, u32[]{:S(2)}) collective-permute-start(f32[64,1024]{1,0:T(8,128)S(1)} %get-tuple-element.189), channel_id=1, source_target_pairs={{0,8},{8,0},{16,24},{24,16},{1,9},{9,1},{17,25},{25,17},{2,10},{10... | collective-permute-start | bytes 786440 | tf_op jit(solution)/shard_map/ppermute | solution.py:43
  91.5 8.3 %collective-permute-start.21 = (f32[64,1024]{1,0:T(8,128)S(1)}, f32[64,1024]{1,0:T(8,128)S(1)}, u32[]{:S(2)}, u32[]{:S(2)}) collective-permute-start(f32[64,1024]{1,0:T(8,128)S(1)} %get-tuple-element.188), channel_id=1, source_target_pairs={{0,8},{8,0},{16,24},{24,16},{1,9},{9,1},{17,25},{25,17},{2,10},{10... | collective-permute-start | bytes 786440 | tf_op jit(solution)/shard_map/ppermute | solution.py:43
  91.5 8.2 %collective-permute-start.22 = (f32[64,1024]{1,0:T(8,128)S(1)}, f32[64,1024]{1,0:T(8,128)S(1)}, u32[]{:S(2)}, u32[]{:S(2)}) collective-permute-start(f32[64,1024]{1,0:T(8,128)S(1)} %get-tuple-element.187), channel_id=1, source_target_pairs={{0,8},{8,0},{16,24},{24,16},{1,9},{9,1},{17,25},{25,17},{2,10},{10... | collective-permute-start | bytes 786440 | tf_op jit(solution)/shard_map/ppermute | solution.py:43
  92.0 13.9 %collective-permute-start.24 = (bf16[512,512]{1,0:T(8,128)(2,1)S(1)}, bf16[512,512]{1,0:T(8,128)(2,1)S(1)}, u32[]{:S(2)}, u32[]{:S(2)}) collective-permute-start(bf16[512,512]{1,0:T(8,128)(2,1)S(1)} %get-tuple-element.157.refs_4_), channel_id=1, source_target_pairs={{0,1},{1,0},{2,3},{3,2},{4,5},{5,4},{6,7},{7,6},{8,9},{9,8},{10,11... | collective-permute-start | bytes 1572872 | tf_op jit(solution)/shard_map/ppermute | solution.py:43
  93.3 8.1 %collective-permute-start.25 = (f32[64,1024]{1,0:T(8,128)S(1)}, f32[64,1024]{1,0:T(8,128)S(1)}, u32[]{:S(2)}, u32[]{:S(2)}) collective-permute-start(f32[64,1024]{1,0:T(8,128)S(1)} %get-tuple-element.142), channel_id=1, source_target_pairs={{0,16},{8,24},{16,0},{24,8},{1,17},{9,25},{17,1},{25,9},{2,18},{10... | collective-permute-start | bytes 786440 | tf_op jit(solution)/shard_map/ppermute | solution.py:43
  94.9 18.7 %collective-permute-start.27 = (bf16[512,512]{1,0:T(8,128)(2,1)S(1)}, bf16[512,512]{1,0:T(8,128)(2,1)}, u32[]{:S(2)}, u32[]{:S(2)}) collective-permute-start(bf16[512,512]{1,0:T(8,128)(2,1)S(1)} %get-tuple-element.157.refs_4_), channel_id=1, source_target_pairs={{0,6},{1,7},{2,2},{3,3},{4,4},{5,5},{6,0},{7,1},{8,14},{9,15},{10,... | collective-permute-start | bytes 1572872 | tf_op jit(solution)/shard_map/ppermute | solution.py:55
  100.4 9.4 %collective-permute-start.23 = (f32[64,1024]{1,0:T(8,128)S(1)}, f32[64,1024]{1,0:T(8,128)}, u32[]{:S(2)}, u32[]{:S(2)}) collective-permute-start(f32[64,1024]{1,0:T(8,128)S(1)} %get-tuple-element.136), channel_id=1, source_target_pairs={{0,16},{8,24},{16,0},{24,8},{1,17},{9,25},{17,1},{25,9},{2,18},{10... | collective-permute-start | bytes 786440 | tf_op jit(solution)/shard_map/ppermute | solution.py:43
  101.4 12.3 %collective-permute-start.26 = (f32[64,1024]{1,0:T(8,128)S(1)}, f32[64,1024]{1,0:T(8,128)}, u32[]{:S(2)}, u32[]{:S(2)}) collective-permute-start(f32[64,1024]{1,0:T(8,128)S(1)} %get-tuple-element.149), channel_id=1, source_target_pairs={{0,16},{8,24},{16,0},{24,8},{1,17},{9,25},{17,1},{25,9},{2,18},{10... | collective-permute-start | bytes 786440 | tf_op jit(solution)/shard_map/ppermute | solution.py:43
  103.0 25.9 %collective-permute-start.29 = (f32[64,1024]{1,0:T(8,128)S(1)}, f32[64,1024]{1,0:T(8,128)S(1)}, u32[]{:S(2)}, u32[]{:S(2)}) collective-permute-start(f32[64,1024]{1,0:T(8,128)S(1)} %add.94), channel_id=1, source_target_pairs={{0,4},{1,5},{2,6},{3,7},{4,0},{5,1},{6,2},{7,3},{8,12},{9,13},{10,... | collective-permute-start | bytes 786440 | tf_op jit(solution)/shard_map/ppermute | solution.py:43
  110.8 19.5 %collective-permute-start.30 = (f32[64,1024]{1,0:T(8,128)S(1)}, f32[64,1024]{1,0:T(8,128)S(1)}, u32[]{:S(2)}, u32[]{:S(2)}) collective-permute-start(f32[64,1024]{1,0:T(8,128)S(1)} %add.95), channel_id=1, source_target_pairs={{0,6},{1,7},{2,4},{3,5},{4,2},{5,3},{6,0},{7,1},{8,14},{9,15},{10,... | collective-permute-start | bytes 786440 | tf_op jit(solution)/shard_map/ppermute | solution.py:43
  114.6 17.7 %collective-permute-start.28 = (f32[64,1024]{1,0:T(8,128)S(1)}, f32[64,1024]{1,0:T(8,128)S(1)}, u32[]{:S(2)}, u32[]{:S(2)}) collective-permute-start(f32[64,1024]{1,0:T(8,128)S(1)} %add.93), channel_id=1, source_target_pairs={{0,2},{1,3},{2,0},{3,1},{4,6},{5,7},{6,4},{7,5},{8,10},{9,11},{10,... | collective-permute-start | bytes 786440 | tf_op jit(solution)/shard_map/ppermute | solution.py:43
  114.8 17.6 %collective-permute-start.32 = (bf16[512,512]{1,0:T(8,128)(2,1)S(1)}, bf16[512,512]{1,0:T(8,128)(2,1)S(1)}, u32[]{:S(2)}, u32[]{:S(2)}) collective-permute-start(bf16[512,512]{1,0:T(8,128)(2,1)S(1)} %broadcast_select_fusion.1.refs_2_), channel_id=1, source_target_pairs={{0,1},{1,0},{2,3},{3,2},{4,5},{5,4},{6,7},{7,6},{8,9},{9,8},{10,11... | collective-permute-start | bytes 1572872 | tf_op jit(solution)/shard_map/ppermute | solution.py:43
  116.2 16.1 %collective-permute-start.31 = (f32[64,1024]{1,0:T(8,128)S(1)}, f32[64,1024]{1,0:T(8,128)S(1)}, u32[]{:S(2)}, u32[]{:S(2)}) collective-permute-start(f32[64,1024]{1,0:T(8,128)S(1)} %get-tuple-element.155), channel_id=1, source_target_pairs={{0,16},{8,24},{16,0},{24,8},{1,17},{9,25},{17,1},{25,9},{2,18},{10... | collective-permute-start | bytes 786440 | tf_op jit(solution)/shard_map/ppermute | solution.py:43
  128.9 13.8 %collective-permute-start.35 = (bf16[512,512]{1,0:T(8,128)(2,1)S(1)}, bf16[512,512]{1,0:T(8,128)(2,1)S(1)}, u32[]{:S(2)}, u32[]{:S(2)}) collective-permute-start(bf16[512,512]{1,0:T(8,128)(2,1)S(1)} %broadcast_select_fusion.refs_6_), channel_id=1, source_target_pairs={{0,1},{1,0},{2,3},{3,2},{4,5},{5,4},{6,7},{7,6},{8,9},{9,8},{10,11... | collective-permute-start | bytes 1572872 | tf_op jit(solution)/shard_map/ppermute | solution.py:43
  133.2 9.4 %collective-permute-start.33 = (bf16[64,2048]{1,0:T(8,128)(2,1)S(1)}, bf16[64,2048]{1,0:T(8,128)(2,1)S(1)}, u32[]{:S(2)}, u32[]{:S(2)}) collective-permute-start(bf16[64,2048]{1,0:T(8,128)(2,1)S(1)} %get-tuple-element.166), channel_id=1, source_target_pairs={{0,2},{1,3},{2,0},{3,1},{4,6},{5,7},{6,4},{7,5},{8,10},{9,11},{10,... | collective-permute-start | bytes 786440 | tf_op jit(solution)/shard_map/ppermute | solution.py:43
  136.0 7.9 %collective-permute-start.34 = (bf16[64,2048]{1,0:T(8,128)(2,1)S(1)}, bf16[64,2048]{1,0:T(8,128)(2,1)S(1)}, u32[]{:S(2)}, u32[]{:S(2)}) collective-permute-start(bf16[64,2048]{1,0:T(8,128)(2,1)S(1)} %get-tuple-element.171.refs_8_), channel_id=1, source_target_pairs={{0,16},{8,24},{16,0},{24,8},{1,17},{9,25},{17,1},{25,9},{2,18},{10... | collective-permute-start | bytes 786440 | tf_op jit(solution)/shard_map/ppermute | solution.py:43
  143.9 1.5 collective-permute-start.36
  143.9 8.7 %collective-permute-start.38 = (bf16[64,2048]{1,0:T(8,128)(2,1)S(1)}, bf16[64,2048]{1,0:T(8,128)(2,1)S(1)}, u32[]{:S(2)}, u32[]{:S(2)}) collective-permute-start(bf16[64,2048]{1,0:T(8,128)(2,1)S(1)} %collective-permute-done.33.refs_8_), channel_id=1, source_target_pairs={{0,16},{8,24},{16,0},{24,8},{1,17},{9,25},{17,1},{25,9},{2,18},{10... | collective-permute-start | bytes 786440 | tf_op jit(solution)/shard_map/ppermute | solution.py:43
  148.3 14.0 %collective-permute-start.37 = (f32[256,512]{1,0:T(8,128)S(1)}, f32[256,512]{1,0:T(8,128)S(1)}, u32[]{:S(2)}, u32[]{:S(2)}) collective-permute-start(f32[256,512]{1,0:T(8,128)S(1)} %shard_map.101), channel_id=1, source_target_pairs={{0,2},{1,3},{2,0},{3,1},{4,6},{5,7},{6,4},{7,5},{8,10},{9,11},{10,... | collective-permute-start | bytes 1572872 | tf_op jit(solution)/shard_map/ppermute | solution.py:43
  152.6 1.5 collective-permute-start.39
  152.6 5.1 %collective-permute-start.40 = (bf16[64,2048]{1,0:T(8,128)(2,1)S(1)}, bf16[64,2048]{1,0:T(8,128)(2,1)S(1)}, u32[]{:S(2)}, u32[]{:S(2)}) collective-permute-start(bf16[64,2048]{1,0:T(8,128)(2,1)S(1)} %get-tuple-element.171.refs_8_), channel_id=1, source_target_pairs={{0,8},{8,0},{16,24},{24,16},{1,9},{9,1},{17,25},{25,17},{2,10},{10... | collective-permute-start | bytes 786440 | tf_op jit(solution)/shard_map/ppermute | solution.py:43
  153.1 5.3 %collective-permute-start.41 = (bf16[64,2048]{1,0:T(8,128)(2,1)S(1)}, bf16[64,2048]{1,0:T(8,128)(2,1)S(1)}, u32[]{:S(2)}, u32[]{:S(2)}) collective-permute-start(bf16[64,2048]{1,0:T(8,128)(2,1)S(1)} %collective-permute-done.34.refs_10_), channel_id=1, source_target_pairs={{0,8},{8,0},{16,24},{24,16},{1,9},{9,1},{17,25},{25,17},{2,10},{10... | collective-permute-start | bytes 786440 | tf_op jit(solution)/shard_map/ppermute | solution.py:43
  163.1 13.5 %collective-permute-start.42 = (f32[256,512]{1,0:T(8,128)}, f32[256,512]{1,0:T(8,128)}, u32[]{:S(2)}, u32[]{:S(2)}) collective-permute-start(f32[256,512]{1,0:T(8,128)} %shard_map.102), channel_id=1, source_target_pairs={{0,2},{1,3},{2,0},{3,1},{4,6},{5,7},{6,4},{7,5},{8,10},{9,11},{10,... | collective-permute-start | bytes 1572872 | tf_op jit(solution)/shard_map/ppermute | solution.py:43
  180.0 2.0 %collective-permute-start.43 = (f32[32,4096]{1,0:T(8,128)S(1)}, f32[32,4096]{1,0:T(8,128)S(1)}, u32[]{:S(2)}, u32[]{:S(2)}) collective-permute-start(f32[32,4096]{1,0:T(8,128)S(1)} %get-tuple-element.182), channel_id=1, source_target_pairs={{0,8},{8,0},{16,24},{24,16},{1,9},{9,1},{17,25},{25,17},{2,10},{10... | collective-permute-start | bytes 1572872 | tf_op jit(solution)/shard_map/ppermute | solution.py:43
  180.1 2.6 %collective-permute-start.44 = (f32[32,4096]{1,0:T(8,128)S(1)}, f32[32,4096]{1,0:T(8,128)S(1)}, u32[]{:S(2)}, u32[]{:S(2)}) collective-permute-start(f32[32,4096]{1,0:T(8,128)S(1)} %get-tuple-element.181), channel_id=1, source_target_pairs={{0,8},{8,0},{16,24},{24,16},{1,9},{9,1},{17,25},{25,17},{2,10},{10... | collective-permute-start | bytes 1572872 | tf_op jit(solution)/shard_map/ppermute | solution.py:43
  183.4 8.4 %collective-permute-start.45 = (bf16[32,4096]{1,0:T(8,128)(2,1)S(1)}, bf16[32,4096]{1,0:T(8,128)(2,1)S(1)}, u32[]{:S(2)}, u32[]{:S(2)}) collective-permute-start(bf16[32,4096]{1,0:T(8,128)(2,1)S(1)} %get-tuple-element.180), channel_id=1, source_target_pairs={{0,16},{8,24},{16,0},{24,8},{1,17},{9,25},{17,1},{25,9},{2,18},{10... | collective-permute-start | bytes 786440 | tf_op jit(solution)/shard_map/ppermute | solution.py:43
  (36 other events, 200.8 us)
